TPU v7x, 1024 devices: a whole 8x8x8 slice. The times are simulated.
1024 devices in a mesh: occ: 32 (over z_lo, x, core), vir: 32 (over z_hi, y).
Axes of the slice: x: 8, y: 8, z: 8 (z_hi: 4, z_lo: 2; z = z_hi * 2 + z_lo), core: 2. Of those that a mesh axis runs over, the one named last changes fastest.
Arguments:
- amplitudes: bfloat16 [131072, 256], P(('vir', 'occ')), may hold values from -6 to 6
- pair_irrep: int32 [1024], P('vir'), may hold values from 0 to 7
- integrals: bfloat16 [32, 8, 128, 4096], P('vir', None, None, 'occ'), may hold values from -0.375 to 0.375
- panel_blocks: int32 [32, 8], P('vir'), may hold values from 0 to 7, each once within a row
- panel_owner: int32 [2], replicated, may hold values from 0 to 31
Outputs:
- ladder: bfloat16 [131072, 4096], P('vir', 'occ')
Inputs may be any that keep to these rules, and one draw needn't show every extreme that they name: Each row of panel_blocks names every irrep once.
All inputs are finite; a program needn't handle non-finite values.
Results may differ from a plain program's by a relative error of at most 0.001.
Values may be sent and summed in bfloat16 or wider, within the bound.
No kernel may reach another device: no remote copies, remote signals or barrier semaphores. Data moves between devices by JAX's collectives and lax.ppermute only.
A program may use at most 32 MiB of HBM per device.

v0:
```python
import jax
import jax.numpy as jnp
from jax import lax
from jax.experimental import pallas as pl
from jax.experimental.pallas import tpu as pltpu
from jax.sharding import Mesh, PartitionSpec as P

OCC = ("zl", "x", "core")
VIR = ("zh", "y")
N_VIR = 32


def order_kernel(blocks_ref, panel_ref, out_ref):
    for slot in range(panel_ref.shape[0]):
        out_ref[blocks_ref[slot]] = panel_ref[slot]


def irrep_order(panel, blocks):
    return pl.pallas_call(
        order_kernel,
        out_shape=jax.ShapeDtypeStruct(panel.shape, panel.dtype),
        in_specs=[
            pl.BlockSpec(memory_space=pltpu.SMEM),
            pl.BlockSpec(memory_space=pltpu.VMEM),
        ],
        out_specs=pl.BlockSpec(memory_space=pltpu.VMEM),
        name="irrep_order",
    )(blocks, panel)


def pick_and_copy(pieces, owners):
    chosen = jnp.concatenate(
        [lax.dynamic_slice_in_dim(pieces, owners[step], 1, 0) for step in range(owners.shape[0])], axis=1
    )
    return jnp.broadcast_to(chosen, pieces.shape[:1] + chosen.shape[1:])


def ladder_kernel(label_ref, half_ref, own_ref, other_ref, weight_ref, out_ref):
    per_block = own_ref.shape[0]
    first = pl.program_id(0) * per_block
    total = pl.num_programs(0) * per_block
    quarters = weight_ref.shape[0] // 8
    for member in range(per_block):
        for half, tiles_ref in ((half_ref[0], own_ref), (1 - half_ref[0], other_ref)):
            irrep = label_ref[half * total + first + member]
            weights = weight_ref[pl.ds(irrep * quarters, quarters)]
            rows = weights.shape[1] // 2
            weights = jnp.concatenate(
                [weights[:, :rows].reshape(-1, weights.shape[2]),
                 weights[:, rows:].reshape(-1, weights.shape[2])], axis=0)
            out_ref[half, member] = jnp.dot(
                tiles_ref[member], weights, preferred_element_type=jnp.float32
            ).astype(out_ref.dtype)


def contract(own, other, labels, half, weights, per_block):
    members, rows, depth = own.shape
    cols = weights.shape[2]
    tiles = pl.BlockSpec((per_block, rows, depth), lambda i, *scalars: (i, 0, 0))
    out = pl.pallas_call(
        ladder_kernel,
        out_shape=jax.ShapeDtypeStruct((2, members, rows, cols), jnp.bfloat16),
        grid_spec=pltpu.PrefetchScalarGridSpec(
            num_scalar_prefetch=2,
            grid=(members // per_block,),
            in_specs=[tiles, tiles, pl.BlockSpec(weights.shape, lambda i, *scalars: (0, 0, 0))],
            out_specs=pl.BlockSpec((2, per_block, rows, cols), lambda i, *scalars: (0, i, 0, 0)),
        ),
        name="ladder",
    )(labels, half, own, other, weights)
    return out.reshape(2 * members * rows, cols)


def per_device(amplitudes, pair_irrep, integrals, panel_blocks, panel_owner):
    rows, depth = amplitudes.shape
    cols = integrals.shape[-1]
    partner = lax.ppermute(amplitudes, "zl", [(0, 1), (1, 0)])
    own = lax.all_gather(amplitudes, ("x", "core"), axis=0, tiled=True)
    other = lax.all_gather(partner, ("x", "core"), axis=0, tiled=True)
    ordered = irrep_order(integrals[0], panel_blocks[0])
    pieces = lax.all_to_all(ordered.reshape(N_VIR, -1, cols), VIR, 0, 0, tiled=True)
    copies = pick_and_copy(pieces, panel_owner)
    weights = lax.all_to_all(copies, VIR, 0, 0, tiled=True)
    half = lax.axis_index("zl").reshape(1)
    tiles = lambda amps: amps.reshape(-1, rows, depth)
    return contract(tiles(own), tiles(other), pair_irrep, half, weights, 8)


def solution(mesh):
    fine = Mesh(mesh.devices.reshape(2, 8, 2, 4, 8), OCC + VIR)
    return jax.shard_map(
        per_device,
        mesh=fine,
        in_specs=(
            P(VIR + OCC, None),
            P(VIR),
            P(VIR, None, None, OCC),
            P(VIR, None),
            P(),
        ),
        out_specs=P(VIR, OCC),
        check_vma=False,
    )
```

profile of v0, /device:TPU:1, one launch (start us, length us, event | category | flops | bytes accessed | tf_op | source)
XLA Modules:
  0.0 122.3 jit_solution(2428449187038757242)
XLA Ops:
  6.5 0.0 copy-start.1
  6.5 0.0 all-gather.3.cloned.1.call-start
  6.5 0.7 all-gather.3.cloned.1.call-update
  7.3 0.0 all-gather.5.cloned.1.call-start
  7.3 0.1 copy-done.1
  7.4 5.7 %collective-permute-start = (bf16[128,256]{1,0:T(8,128)(2,1)S(1)}, bf16[128,256]{1,0:T(8,128)(2,1)S(1)}, u32[]{:S(2)}, u32[]{:S(2)}) collective-permute-start(bf16[128,256]{1,0:T(8,128)(2,1)S(1)} %copy-done.1), channel_id=1, source_target_pairs={{0,512},{512,0},{1,513},{513,1},{2,514},{514,2},{3,515},{515,3},{4... | collective-permute-start | bytes 196616 | tf_op jit(solution)/shard_map/ppermute | solution.py:77
  13.1 1.6 %collective-permute-done = bf16[128,256]{1,0:T(8,128)(2,1)S(1)} collective-permute-done((bf16[128,256]{1,0:T(8,128)(2,1)S(1)}, bf16[128,256]{1,0:T(8,128)(2,1)S(1)}, u32[]{:S(2)}, u32[]{:S(2)}) %collective-permute-start) | collective-permute-done | bytes 65568 | tf_op jit(solution)/shard_map/ppermute | solution.py:77
  14.7 0.0 copy-start.2
  14.7 0.6 copy-done.2
  15.4 0.0 all-gather.5.cloned.1.call-update
  15.4 1.7 %irrep_order.1 = bf16[8,128,128]{2,1,0:T(8,128)(2,1)} custom-call(s32[8]{0:T(128)} %bitcast.15, bf16[8,128,128]{2,1,0:T(8,128)(2,1)} %bitcast.14), custom_call_target="tpu_custom_call" | custom-call | tf_op jit(solution)/shard_map/irrep_order/pallas_call | solution.py:19
  17.1 0.0 copy-start.3
  17.1 20.8 %all-to-all-start = ((bf16[32,32,128]{2,1,0:T(8,128)(2,1)}), bf16[32,32,128]{2,1,0:T(8,128)(2,1)S(1)}, u32[]{:S(2)}, u32[]{:S(2)}) async-start(bf16[32,32,128]{2,1,0:T(8,128)(2,1)} %bitcast.11), calls=%async_computation | async-start | bytes 524288 | tf_op jit(solution)/shard_map/all_to_all | solution.py:81
  37.9 0.0 copy-done.3
  37.9 0.7 fusion
  42.5 7.8 %all-to-all-done = bf16[32,32,128]{2,1,0:T(8,128)(2,1)S(1)} async-done(((bf16[32,32,128]{2,1,0:T(8,128)(2,1)}), bf16[32,32,128]{2,1,0:T(8,128)(2,1)S(1)}, u32[]{:S(2)}, u32[]{:S(2)}) %all-to-all-start) | async-done | bytes 262176 | tf_op jit(solution)/shard_map/all_to_all | solution.py:81
  50.3 0.9 broadcast_in_dim.8
  51.2 5.4 %all-to-all-start.1 = ((bf16[32,64,128]{2,1,0:T(8,128)(2,1)}), bf16[32,64,128]{2,1,0:T(8,128)(2,1)S(1)}, u32[]{:S(2)}, u32[]{:S(2)}) async-start(bf16[32,64,128]{2,1,0:T(8,128)(2,1)} %broadcast_in_dim.8), calls=%async_computation.1 | async-start | bytes 1048576 | tf_op jit(solution)/shard_map/all_to_all | solution.py:83
  56.6 15.4 %all-to-all-done.1.weight_ref = bf16[32,64,128]{2,1,0:T(8,128)(2,1)S(1)} async-done(((bf16[32,64,128]{2,1,0:T(8,128)(2,1)}), bf16[32,64,128]{2,1,0:T(8,128)(2,1)S(1)}, u32[]{:S(2)}, u32[]{:S(2)}) %all-to-all-start.1) | async-done | bytes 524320 | tf_op jit(solution)/shard_map/all_to_all | solution.py:83
  72.1 0.0 copy-start
  72.1 0.0 all-gather.3.cloned.1.call-done
  72.1 39.7 %all-gather.5.cloned.1.call-done = bf16[2048,256]{1,0:T(8,128)(2,1)} async-done(((bf16[128,256]{1,0:T(8,128)(2,1)}), bf16[2048,256]{1,0:T(8,128)(2,1)}) %all-gather.5.cloned.1.call-update) | async-done | bytes 1048592 | tf_op jit(solution)/shard_map/all_gather | solution.py:79
  111.7 0.0 copy-done
  111.7 3.7 %ladder.1 = bf16[2,16,128,128]{3,2,1,0:T(8,128)(2,1)} custom-call(s32[32]{0:T(128)} %label_ref.1, s32[1]{0:T(128)} %bitcast.half_ref, bf16[16,128,256]{2,1,0:T(8,128)(2,1)} %bitcast.12, bf16[16,128,256]{2,1,0:T(8,128)(2,1)} %bitcast.13, bf16[32,64,128]{2,1,0:T(8,128)(2,1)} %copy-done), custom_call_target="tpu_custom_call" | custom-call | tf_op jit(solution)/shard_map/ladder/pallas_call | solution.py:60
  (2 shorter events, 0.0 us)
Async XLA Ops:
  6.5 0.8 copy-start.1
  6.5 65.5 %all-gather.3.cloned.1.call-start = ((), (), s32[]{:S(2)}) async-start(), calls=%async_computation.2 | async-start | bytes 1114112 | tf_op jit(solution)/shard_map/all_gather | solution.py:78
  7.3 104.4 %all-gather.5.cloned.1.call-start = ((), (), s32[]{:S(2)}) async-start(), calls=%async_computation.3 | async-start | bytes 1114112 | tf_op jit(solution)/shard_map/all_gather | solution.py:79
  7.4 7.4 %collective-permute-start = (bf16[128,256]{1,0:T(8,128)(2,1)S(1)}, bf16[128,256]{1,0:T(8,128)(2,1)S(1)}, u32[]{:S(2)}, u32[]{:S(2)}) collective-permute-start(bf16[128,256]{1,0:T(8,128)(2,1)S(1)} %copy-done.1), channel_id=1, source_target_pairs={{0,512},{512,0},{1,513},{513,1},{2,514},{514,2},{3,515},{515,3},{4... | collective-permute-start | bytes 196616 | tf_op jit(solution)/shard_map/ppermute | solution.py:77
  14.7 0.6 copy-start.2
  17.1 20.8 %copy-start.3 = (s32[2]{0:T(128)S(1)}, s32[2]{0:T(128)}, u32[]{:S(2)}) copy-start(s32[2]{0:T(128)} %param.9) | copy-start | bytes 28
  17.1 33.2 %all-to-all-start = ((bf16[32,32,128]{2,1,0:T(8,128)(2,1)}), bf16[32,32,128]{2,1,0:T(8,128)(2,1)S(1)}, u32[]{:S(2)}, u32[]{:S(2)}) async-start(bf16[32,32,128]{2,1,0:T(8,128)(2,1)} %bitcast.11), calls=%async_computation | async-start | bytes 524288 | tf_op jit(solution)/shard_map/all_to_all | solution.py:81
  51.2 20.8 %all-to-all-start.1 = ((bf16[32,64,128]{2,1,0:T(8,128)(2,1)}), bf16[32,64,128]{2,1,0:T(8,128)(2,1)S(1)}, u32[]{:S(2)}, u32[]{:S(2)}) async-start(bf16[32,64,128]{2,1,0:T(8,128)(2,1)} %broadcast_in_dim.8), calls=%async_computation.1 | async-start | bytes 1048576 | tf_op jit(solution)/shard_map/all_to_all | solution.py:83
  72.1 39.7 %copy-start = (bf16[32,64,128]{2,1,0:T(8,128)(2,1)}, bf16[32,64,128]{2,1,0:T(8,128)(2,1)S(1)}, u32[]{:S(2)}) copy-start(bf16[32,64,128]{2,1,0:T(8,128)(2,1)S(1)} %all-to-all-done.1.weight_ref) | copy-start | bytes 1572868
Sparse Core Ops, SparseCore 0:
  10.0 55.8 all-gather.2
  68.6 43.0 all-gather.4
where the time goes:
time: 123 us; the launch traced here: 122 us
  waiting for transfers between devices  65.2 us (53%)
  starting transfers between devices  32 us (26%)
  between operations  17.4 us (14%)
  Pallas kernels  5.4 us (4%)
  local copies, waits for them, and re-layouts  2.27 us (2%)
    all_gather x1, waiting for transfers between devices, per_device(): other = lax.all_gather(partner, ('x', 'core'), axis=0, tiled=True)  39.7 us
    all_to_all x1, starting transfers between devices, per_device(): lax.all_to_all(ordered.reshape(N_VIR, -1, cols), VIR, 0, 0, tiled=True)  20.8 us
    all_to_all x1, waiting for transfers between devices, per_device(): weights = lax.all_to_all(copies, VIR, 0, 0, tiled=True)  15.4 us
    all_to_all x1, waiting for transfers between devices, per_device(): lax.all_to_all(ordered.reshape(N_VIR, -1, cols), VIR, 0, 0, tiled=True)  7.8 us
    ppermute x1, starting transfers between devices, per_device(): partner = lax.ppermute(amplitudes, 'zl', [(0, 1), (1, 0)])  5.72 us
    all_to_all x1, starting transfers between devices, per_device(): weights = lax.all_to_all(copies, VIR, 0, 0, tiled=True)  5.4 us
    pallas_call x1, Pallas kernels, contract(): pl.pallas_call(ladder_kernel, out_shape=jax.ShapeDtypeStruct((2, members,...  3.72 us
  transfers between devices with their start and end apart: 5, of which 4 were waited for; matrix products, arithmetic and copies ran while one was open for 1% of the time, Pallas kernels for 1%

commit v1 on v0

v1 whole, which is shorter than its diff:
```python
import jax
import jax.numpy as jnp
from jax import lax
from jax.experimental import pallas as pl
from jax.experimental.pallas import tpu as pltpu
from jax.sharding import Mesh, PartitionSpec as P


OCC = ("zl", "x", "core")
VIR = ("zh", "y")
N_VIR = 32
N_X = 8
IRREPS = 8


def order_kernel(blocks_ref, panel_ref, out_ref):
    for slot in range(panel_ref.shape[0]):
        out_ref[blocks_ref[slot]] = panel_ref[slot]


def irrep_order(panel, blocks):
    return pl.pallas_call(
        order_kernel,
        out_shape=pltpu.VMEM(panel.shape, panel.dtype),
        in_specs=[
            pl.BlockSpec(memory_space=pltpu.SMEM),
            pl.BlockSpec(memory_space=pltpu.VMEM),
        ],
        out_specs=pl.BlockSpec(memory_space=pltpu.VMEM),
        name="irrep_order",
    )(blocks, panel)


def pick_kernel(owner_ref, pieces_ref, out_ref):
    count, rows, cols = pieces_ref.shape
    for step in range(out_ref.shape[1] // rows):
        out_ref[:, step * rows:(step + 1) * rows, :] = jnp.broadcast_to(
            pieces_ref[pl.ds(owner_ref[step], 1)], (count, rows, cols)
        )


def pick_and_copy(pieces, owners):
    count, rows, cols = pieces.shape
    return pl.pallas_call(
        pick_kernel,
        out_shape=pltpu.VMEM((count, owners.shape[0] * rows, cols), pieces.dtype),
        in_specs=[
            pl.BlockSpec(memory_space=pltpu.SMEM),
            pl.BlockSpec(memory_space=pltpu.VMEM),
        ],
        out_specs=pl.BlockSpec(memory_space=pltpu.VMEM),
    )(owners, pltpu.with_memory_space_constraint(pieces, pltpu.VMEM))


BLOCK = ((-1, 0), (0, 0), (1, 0))
FAR = ((-4, 0), (-3, 0), (-2, 0), (2, 0), (3, 0))
OTHER_BLOCK = tuple((x, 1) for x, _ in BLOCK)
OTHER_FAR = tuple((x, 1) for x, _ in FAR)
NEAR = BLOCK + FAR + OTHER_BLOCK


def ladder_kernel(groups, piece_ref, here_ref, side_ref, *refs):
    held_refs, refs = refs[:len(groups)], refs[len(groups):]
    weight_ref, out_ref, done_ref, sems, in_sems = refs[:5]
    tiles_refs = refs[5:]
    quarters = weight_ref.shape[0] // IRREPS
    copies = []
    arrivals = [
        pltpu.make_async_copy(held_ref, tiles_ref, in_sems.at[group])
        for group, (held_ref, tiles_ref) in enumerate(zip(held_refs, tiles_refs))
    ]
    for arrival in arrivals:
        arrival.start()
    for (core_step, places), tiles_ref, arrival in zip(groups, tiles_refs, arrivals):
        arrival.wait()
        for index, (x_step, zl_step) in enumerate(places):
            zl = lax.rem(here_ref[0] + zl_step, 2)
            x = lax.rem(here_ref[1] + x_step + N_X, N_X)
            core = lax.rem(side_ref[0] + core_step, 2)
            tile = (zl * N_X + x) * 2 + core
            weights = weight_ref[pl.ds(piece_ref[tile], quarters)]
            rows = weights.shape[1] // 2
            weights = jnp.concatenate(
                [weights[:, :rows].reshape(-1, weights.shape[2]),
                 weights[:, rows:].reshape(-1, weights.shape[2])], axis=0)
            slot = len(copies)
            done_ref[slot] = jnp.dot(
                tiles_ref[index], weights, preferred_element_type=jnp.float32
            ).astype(done_ref.dtype)
            copy = pltpu.make_async_copy(done_ref.at[slot], out_ref.at[tile], sems.at[slot])
            copy.start()
            copies.append(copy)
    for copy in copies:
        copy.wait()


def contract(groups, arrays, first_piece, here, side, weights):
    rows = arrays[0].shape[1]
    cols = weights.shape[2]
    count = sum(array.shape[0] for array in arrays)
    vmem, smem = pl.BlockSpec(memory_space=pltpu.VMEM), pl.BlockSpec(memory_space=pltpu.SMEM)
    operands = [pltpu.with_memory_space_constraint(array, pltpu.HBM) for array in arrays]
    operands.append(pltpu.with_memory_space_constraint(weights, pltpu.VMEM))
    out = pl.pallas_call(
        lambda *refs: ladder_kernel(groups, *refs),
        out_shape=jax.ShapeDtypeStruct((count, rows, cols), jnp.bfloat16),
        in_specs=[smem, smem, smem] + [pl.BlockSpec(memory_space=pltpu.HBM)] * len(arrays) + [vmem],
        out_specs=pl.BlockSpec(memory_space=pl.ANY),
        scratch_shapes=[
            pltpu.VMEM((count, rows, cols), jnp.bfloat16),
            pltpu.SemaphoreType.DMA((count,)),
            pltpu.SemaphoreType.DMA((len(arrays),)),
            *(pltpu.VMEM(array.shape, array.dtype) for array in arrays),
        ],
        name="ladder",
    )(first_piece, here, side, *operands)
    return out.reshape(count * rows, cols)


def shift(array, axis, size, step):
    return lax.ppermute(array, axis, [(index, (index + step) % size) for index in range(size)])


def per_device(amplitudes, pair_irrep, integrals, panel_blocks, panel_owner):
    cols = integrals.shape[-1]
    left = shift(amplitudes, "x", N_X, 1)
    right = shift(amplitudes, "x", N_X, -1)
    ordered = irrep_order(integrals[0], panel_blocks[0])
    pieces = lax.all_to_all(ordered.reshape(N_VIR, -1, cols), VIR, 0, 0, tiled=True)
    block = jnp.stack([left, amplitudes, right])
    up = shift(block, "x", N_X, 3)
    down = shift(block, "x", N_X, -3)
    other_block = shift(block, "zl", 2, 1)
    here = jnp.stack([lax.axis_index("zl"), lax.axis_index("x")])
    copies = pick_and_copy(pieces, panel_owner)
    weights = lax.all_to_all(copies, VIR, 0, 0, tiled=True)
    side = jnp.arange(16, dtype=jnp.int32) + lax.axis_index("core")
    far = jnp.concatenate([up, down[:2]])
    other_far = shift(far, "zl", 2, 1)
    near = jnp.concatenate([block, up, down[:2], other_block])
    share_near = shift(near, "core", 2, 1)
    first_piece = pair_irrep * (N_VIR // IRREPS)
    share_far = shift(other_far, "core", 2, 1)
    groups = ((0, NEAR), (1, NEAR), (0, OTHER_FAR), (1, OTHER_FAR))
    return contract(
        groups, (near, share_near, other_far, share_far), first_piece, here, side, weights)


def solution(mesh):
    fine = Mesh(mesh.devices.reshape(2, 8, 2, 4, 8), OCC + VIR)
    return jax.shard_map(
        per_device,
        mesh=fine,
        in_specs=(
            P(VIR + OCC, None),
            P(VIR),
            P(VIR, None, None, OCC),
            P(VIR, None),
            P(),
        ),
        out_specs=P(VIR, OCC),
        check_vma=False,
    )
```

time: 123 us -> 102 us (0.83)
  waiting for transfers between devices: 65.2 us -> 30.6 us
  starting transfers between devices: 32 us -> 60.5 us
  between operations: 17.4 us -> 0.24 us
  Pallas kernels: 5.4 us -> 7.23 us
  other arithmetic: 0.01 us -> 1.73 us
    all_gather x2 -> x0, waiting for transfers between devices: 39.7 us -> none  [the longest x1 39.7 us: per_device(): other = lax.all_gather(partner, ('x', 'core'), axis=0, tiled=True)]
    ppermute x1 -> x8, waiting for transfers between devices: 1.64 us -> 30.6 us  [shift(): lax.ppermute(array, axis, [(index, (index + step) % size) for index in ra...]
    ppermute x1 -> x8, starting transfers between devices: 5.72 us -> 27.1 us  [shift(): lax.ppermute(array, axis, [(index, (index + step) % size) for index in ra...]
    all_to_all x1, waiting for transfers between devices: 15.4 us -> 0.01 us  [per_device(): weights = lax.all_to_all(copies, VIR, 0, 0, tiled=True)]
    all_to_all x1, waiting for transfers between devices: 7.8 us -> 0.01 us  [per_device(): lax.all_to_all(ordered.reshape(N_VIR, -1, cols), VIR, 0, 0, tiled=True)]
    all_to_all x1, starting transfers between devices: 5.4 us -> 11.6 us  [per_device(): weights = lax.all_to_all(copies, VIR, 0, 0, tiled=True)]
    pallas_call x2 -> x3, Pallas kernels: 5.4 us -> 7.23 us  [the longest x1 3.97 us: contract(): pl.pallas_call(lambda *refs: ladder_kernel(groups, *refs), out_shape=jax....]
  transfers between devices with their start and end apart: 5 -> 10, of which waited for: 4 -> 3; matrix products, arithmetic and copies ran while one was open for 1% -> 2% of each run, Pallas kernels for 1% -> 3%
where the time goes in v1:
time: 102 us; the launch traced here: 101 us
  starting transfers between devices  60.5 us (59%)
  waiting for transfers between devices  30.6 us (30%)
  Pallas kernels  7.23 us (7%)
  other arithmetic  1.73 us (2%)
  local copies, waits for them, and re-layouts  1.11 us (1%)
    ppermute x8, waiting for transfers between devices, shift(): lax.ppermute(array, axis, [(index, (index + step) % size) for index in ra...  30.6 us
    ppermute x8, starting transfers between devices, shift(): lax.ppermute(array, axis, [(index, (index + step) % size) for index in ra...  27.1 us
    all_to_all x1, starting transfers between devices, per_device(): lax.all_to_all(ordered.reshape(N_VIR, -1, cols), VIR, 0, 0, tiled=True)  21.8 us
    all_to_all x1, starting transfers between devices, per_device(): weights = lax.all_to_all(copies, VIR, 0, 0, tiled=True)  11.6 us
    pallas_call x1, Pallas kernels, contract(): pl.pallas_call(lambda *refs: ladder_kernel(groups, *refs), out_shape=jax....  3.97 us
  transfers between devices with their start and end apart: 10, of which 3 were waited for; matrix products, arithmetic and copies ran while one was open for 2% of the time, Pallas kernels for 3%

profile of v1, /device:TPU:1, one launch (start us, length us, event | category | flops | bytes accessed | tf_op | source)
XLA Modules:
  0.0 101.4 jit_solution(4811230111265483876)
XLA Ops:
  0.0 3.9 %collective-permute-start = (bf16[128,256]{1,0:T(8,128)(2,1)}, bf16[128,256]{1,0:T(8,128)(2,1)S(1)}, u32[]{:S(2)}, u32[]{:S(2)}) collective-permute-start(bf16[128,256]{1,0:T(8,128)(2,1)} %param.5), channel_id=1, source_target_pairs={{0,64},{64,128},{128,192},{192,256},{256,320},{320,384},{384,448},... | collective-permute-start | bytes 196616 | tf_op jit(solution)/shard_map/ppermute | solution.py:121
  3.9 3.3 %collective-permute-start.1 = (bf16[128,256]{1,0:T(8,128)(2,1)}, bf16[128,256]{1,0:T(8,128)(2,1)S(1)}, u32[]{:S(2)}, u32[]{:S(2)}) collective-permute-start(bf16[128,256]{1,0:T(8,128)(2,1)} %param.5), channel_id=1, source_target_pairs={{0,448},{64,0},{128,64},{192,128},{256,192},{320,256},{384,320},{4... | collective-permute-start | bytes 196616 | tf_op jit(solution)/shard_map/ppermute | solution.py:121
  7.2 1.7 %irrep_order.1 = bf16[8,128,128]{2,1,0:T(8,128)(2,1)} custom-call(s32[8]{0:T(128)} %bitcast.16, bf16[8,128,128]{2,1,0:T(8,128)(2,1)} %bitcast.12), custom_call_target="tpu_custom_call" | custom-call | tf_op jit(solution)/shard_map/irrep_order/pallas_call | solution.py:22
  8.9 21.8 %all-to-all-start = ((bf16[32,32,128]{2,1,0:T(8,128)(2,1)}), bf16[32,32,128]{2,1,0:T(8,128)(2,1)S(1)}, u32[]{:S(2)}, u32[]{:S(2)}) async-start(bf16[32,32,128]{2,1,0:T(8,128)(2,1)} %bitcast.7), calls=%async_computation | async-start | bytes 524288 | tf_op jit(solution)/shard_map/all_to_all | solution.py:129
  30.7 0.0 collective-permute-done
  30.7 0.0 collective-permute-done.1
  30.8 4.0 %collective-permute-start.4 = (bf16[3,128,256]{2,1,0:T(8,128)(2,1)S(1)}, bf16[3,128,256]{2,1,0:T(8,128)(2,1)S(1)}, u32[]{:S(2)}, u32[]{:S(2)}) collective-permute-start(bf16[3,128,256]{2,1,0:T(8,128)(2,1)S(1)} %pad_maximum_fusion.1), channel_id=1, source_target_pairs={{0,512},{512,0},{1,513},{513,1},{2,514},{514,2},{3,515},{515,3},{4... | collective-permute-start | bytes 589832 | tf_op jit(solution)/shard_map/ppermute | solution.py:121
  34.8 5.0 %collective-permute-start.3 = (bf16[3,128,256]{2,1,0:T(8,128)(2,1)S(1)}, bf16[3,128,256]{2,1,0:T(8,128)(2,1)S(1)}, u32[]{:S(2)}, u32[]{:S(2)}) collective-permute-start(bf16[3,128,256]{2,1,0:T(8,128)(2,1)S(1)} %pad_maximum_fusion.1), channel_id=1, source_target_pairs={{0,320},{64,384},{128,448},{192,0},{256,64},{320,128},{384,192},{4... | collective-permute-start | bytes 589832 | tf_op jit(solution)/shard_map/ppermute | solution.py:121
  39.9 2.0 %collective-permute-start.2 = (bf16[3,128,256]{2,1,0:T(8,128)(2,1)S(1)}, bf16[3,128,256]{2,1,0:T(8,128)(2,1)S(1)}, u32[]{:S(2)}, u32[]{:S(2)}) collective-permute-start(bf16[3,128,256]{2,1,0:T(8,128)(2,1)S(1)} %pad_maximum_fusion.1), channel_id=1, source_target_pairs={{0,192},{64,256},{128,320},{192,384},{256,448},{320,0},{384,64},{4... | collective-permute-start | bytes 589832 | tf_op jit(solution)/shard_map/ppermute | solution.py:121
  42.0 15.4 %collective-permute-done.2 = bf16[3,128,256]{2,1,0:T(8,128)(2,1)S(1)} collective-permute-done((bf16[3,128,256]{2,1,0:T(8,128)(2,1)S(1)}, bf16[3,128,256]{2,1,0:T(8,128)(2,1)S(1)}, u32[]{:S(2)}, u32[]{:S(2)}) %collective-permute-start.2) | collective-permute-done | bytes 196640 | tf_op jit(solution)/shard_map/ppermute | solution.py:121
  57.4 0.0 all-to-all-done.pieces_ref
  57.4 1.6 %shard_map.55 = bf16[32,64,128]{2,1,0:T(8,128)(2,1)} custom-call(s32[2]{0:T(128)} %owner_ref.1, bf16[32,32,128]{2,1,0:T(8,128)(2,1)S(1)} %all-to-all-done.pieces_ref), custom_call_target="tpu_custom_call" | custom-call | tf_op jit(solution)/shard_map/pallas_call | solution.py:44
  59.0 11.6 %all-to-all-start.1 = ((bf16[32,64,128]{2,1,0:T(8,128)(2,1)}), bf16[32,64,128]{2,1,0:T(8,128)(2,1)S(1)}, u32[]{:S(2)}, u32[]{:S(2)}) async-start(bf16[32,64,128]{2,1,0:T(8,128)(2,1)} %shard_map.55), calls=%async_computation.1 | async-start | bytes 1048576 | tf_op jit(solution)/shard_map/all_to_all | solution.py:136
  70.6 0.0 collective-permute-done.3
  70.7 0.0 collective-permute-done.4
  70.7 4.6 %collective-permute-start.5 = (bf16[11,128,256]{2,1,0:T(8,128)(2,1)S(1)}, bf16[11,128,256]{2,1,0:T(8,128)(2,1)S(1)}, u32[]{:S(2)}, u32[]{:S(2)}) collective-permute-start(bf16[11,128,256]{2,1,0:T(8,128)(2,1)S(1)} %constant_dynamic-update-slice_fusion.refs_3_), channel_id=1, source_target_pairs={{0,32},{32,0},{1,33},{33,1},{2,34},{34,2},{3,35},{35,3},{4,36},{36... | collective-permute-start | bytes 2162696 | tf_op jit(solution)/shard_map/ppermute | solution.py:121
  75.3 1.9 %collective-permute-start.6 = (bf16[5,128,256]{2,1,0:T(8,128)(2,1)S(1)}, bf16[5,128,256]{2,1,0:T(8,128)(2,1)S(1)}, u32[]{:S(2)}, u32[]{:S(2)}) collective-permute-start(bf16[5,128,256]{2,1,0:T(8,128)(2,1)S(1)} %pad_maximum_fusion), channel_id=1, source_target_pairs={{0,512},{512,0},{1,513},{513,1},{2,514},{514,2},{3,515},{515,3},{4... | collective-permute-start | bytes 983048 | tf_op jit(solution)/shard_map/ppermute | solution.py:121
  77.3 0.6 iota_add_fusion.refs_2_
  77.9 15.1 %collective-permute-done.6.refs_5_ = bf16[5,128,256]{2,1,0:T(8,128)(2,1)S(1)} collective-permute-done((bf16[5,128,256]{2,1,0:T(8,128)(2,1)S(1)}, bf16[5,128,256]{2,1,0:T(8,128)(2,1)S(1)}, u32[]{:S(2)}, u32[]{:S(2)}) %collective-permute-start.6) | collective-permute-done | bytes 327712 | tf_op jit(solution)/shard_map/ppermute | solution.py:121
  92.9 2.3 %collective-permute-start.7 = (bf16[5,128,256]{2,1,0:T(8,128)(2,1)S(1)}, bf16[5,128,256]{2,1,0:T(8,128)(2,1)S(1)}, u32[]{:S(2)}, u32[]{:S(2)}) collective-permute-start(bf16[5,128,256]{2,1,0:T(8,128)(2,1)S(1)} %collective-permute-done.6.refs_5_), channel_id=1, source_target_pairs={{0,32},{32,0},{1,33},{33,1},{2,34},{34,2},{3,35},{35,3},{4,36},{36... | collective-permute-start | bytes 983048 | tf_op jit(solution)/shard_map/ppermute | solution.py:121
  95.2 0.0 copy-start.5
  95.2 0.6 pad_add_fusion.refs_1_
  95.8 0.1 copy-done.5
  95.9 0.5 broadcast_multiply_fusion.refs_0_
  96.4 0.1 collective-permute-done.7.refs_6_
  96.5 0.0 collective-permute-done.5.refs_4_
  96.5 0.0 all-to-all-done.1.refs_7_
  96.5 0.0 copy-done
  96.5 0.0 copy-done.2
  96.5 0.7 copy-done.3
  97.2 0.2 copy-done.1
  97.5 4.0 %ladder.1 = bf16[32,128,128]{2,1,0:T(8,128)(2,1)} custom-call(s32[32]{0:T(128)} %broadcast_multiply_fusion.refs_0_, s32[2]{0:T(128)} %pad_add_fusion.refs_1_, s32[16]{0:T(128)} %iota_add_fusion.refs_2_, bf16[11,128,256]{2,1,0:T(8,128)(2,1)} %copy-done, bf16[11,128,256]{2,1,0:T(8,128)(2,1)} %copy-done.1, bf16[5,128,256]{2,1,0:T(8,128)(2,1)} %copy-done.2, ...), custom_call_target="tpu_custom_call" | custom-call | tf_op jit(solution)/shard_map/ladder/pallas_call | solution.py:104
  (14 shorter events, 0.1 us)
Async XLA Ops:
  0.0 30.7 %collective-permute-start = (bf16[128,256]{1,0:T(8,128)(2,1)}, bf16[128,256]{1,0:T(8,128)(2,1)S(1)}, u32[]{:S(2)}, u32[]{:S(2)}) collective-permute-start(bf16[128,256]{1,0:T(8,128)(2,1)} %param.5), channel_id=1, source_target_pairs={{0,64},{64,128},{128,192},{192,256},{256,320},{320,384},{384,448},... | collective-permute-start | bytes 196616 | tf_op jit(solution)/shard_map/ppermute | solution.py:121
  3.9 26.8 %collective-permute-start.1 = (bf16[128,256]{1,0:T(8,128)(2,1)}, bf16[128,256]{1,0:T(8,128)(2,1)S(1)}, u32[]{:S(2)}, u32[]{:S(2)}) collective-permute-start(bf16[128,256]{1,0:T(8,128)(2,1)} %param.5), channel_id=1, source_target_pairs={{0,448},{64,0},{128,64},{192,128},{256,192},{320,256},{384,320},{4... | collective-permute-start | bytes 196616 | tf_op jit(solution)/shard_map/ppermute | solution.py:121
  8.9 21.8 %copy-start.4 = (bf16[128,256]{1,0:T(8,128)(2,1)S(1)}, bf16[128,256]{1,0:T(8,128)(2,1)}, u32[]{:S(2)}) copy-start(bf16[128,256]{1,0:T(8,128)(2,1)} %param.5) | copy-start | bytes 196612
  8.9 48.5 %all-to-all-start = ((bf16[32,32,128]{2,1,0:T(8,128)(2,1)}), bf16[32,32,128]{2,1,0:T(8,128)(2,1)S(1)}, u32[]{:S(2)}, u32[]{:S(2)}) async-start(bf16[32,32,128]{2,1,0:T(8,128)(2,1)} %bitcast.7), calls=%async_computation | async-start | bytes 524288 | tf_op jit(solution)/shard_map/all_to_all | solution.py:129
  30.8 39.9 %collective-permute-start.4 = (bf16[3,128,256]{2,1,0:T(8,128)(2,1)S(1)}, bf16[3,128,256]{2,1,0:T(8,128)(2,1)S(1)}, u32[]{:S(2)}, u32[]{:S(2)}) collective-permute-start(bf16[3,128,256]{2,1,0:T(8,128)(2,1)S(1)} %pad_maximum_fusion.1), channel_id=1, source_target_pairs={{0,512},{512,0},{1,513},{513,1},{2,514},{514,2},{3,515},{515,3},{4... | collective-permute-start | bytes 589832 | tf_op jit(solution)/shard_map/ppermute | solution.py:121
  34.8 35.8 %collective-permute-start.3 = (bf16[3,128,256]{2,1,0:T(8,128)(2,1)S(1)}, bf16[3,128,256]{2,1,0:T(8,128)(2,1)S(1)}, u32[]{:S(2)}, u32[]{:S(2)}) collective-permute-start(bf16[3,128,256]{2,1,0:T(8,128)(2,1)S(1)} %pad_maximum_fusion.1), channel_id=1, source_target_pairs={{0,320},{64,384},{128,448},{192,0},{256,64},{320,128},{384,192},{4... | collective-permute-start | bytes 589832 | tf_op jit(solution)/shard_map/ppermute | solution.py:121
  39.9 17.5 %collective-permute-start.2 = (bf16[3,128,256]{2,1,0:T(8,128)(2,1)S(1)}, bf16[3,128,256]{2,1,0:T(8,128)(2,1)S(1)}, u32[]{:S(2)}, u32[]{:S(2)}) collective-permute-start(bf16[3,128,256]{2,1,0:T(8,128)(2,1)S(1)} %pad_maximum_fusion.1), channel_id=1, source_target_pairs={{0,192},{64,256},{128,320},{192,384},{256,448},{320,0},{384,64},{4... | collective-permute-start | bytes 589832 | tf_op jit(solution)/shard_map/ppermute | solution.py:121
  59.0 37.5 %all-to-all-start.1 = ((bf16[32,64,128]{2,1,0:T(8,128)(2,1)}), bf16[32,64,128]{2,1,0:T(8,128)(2,1)S(1)}, u32[]{:S(2)}, u32[]{:S(2)}) async-start(bf16[32,64,128]{2,1,0:T(8,128)(2,1)} %shard_map.55), calls=%async_computation.1 | async-start | bytes 1048576 | tf_op jit(solution)/shard_map/all_to_all | solution.py:136
  70.7 25.8 %copy-start = (bf16[11,128,256]{2,1,0:T(8,128)(2,1)}, bf16[11,128,256]{2,1,0:T(8,128)(2,1)S(1)}, u32[]{:S(2)}) copy-start(bf16[11,128,256]{2,1,0:T(8,128)(2,1)S(1)} %constant_dynamic-update-slice_fusion.refs_3_) | copy-start | bytes 2162692
  70.7 25.7 %collective-permute-start.5 = (bf16[11,128,256]{2,1,0:T(8,128)(2,1)S(1)}, bf16[11,128,256]{2,1,0:T(8,128)(2,1)S(1)}, u32[]{:S(2)}, u32[]{:S(2)}) collective-permute-start(bf16[11,128,256]{2,1,0:T(8,128)(2,1)S(1)} %constant_dynamic-update-slice_fusion.refs_3_), channel_id=1, source_target_pairs={{0,32},{32,0},{1,33},{33,1},{2,34},{34,2},{3,35},{35,3},{4,36},{36... | collective-permute-start | bytes 2162696 | tf_op jit(solution)/shard_map/ppermute | solution.py:121
  75.3 17.6 %collective-permute-start.6 = (bf16[5,128,256]{2,1,0:T(8,128)(2,1)S(1)}, bf16[5,128,256]{2,1,0:T(8,128)(2,1)S(1)}, u32[]{:S(2)}, u32[]{:S(2)}) collective-permute-start(bf16[5,128,256]{2,1,0:T(8,128)(2,1)S(1)} %pad_maximum_fusion), channel_id=1, source_target_pairs={{0,512},{512,0},{1,513},{513,1},{2,514},{514,2},{3,515},{515,3},{4... | collective-permute-start | bytes 983048 | tf_op jit(solution)/shard_map/ppermute | solution.py:121
  92.9 3.6 %copy-start.2 = (bf16[5,128,256]{2,1,0:T(8,128)(2,1)}, bf16[5,128,256]{2,1,0:T(8,128)(2,1)S(1)}, u32[]{:S(2)}) copy-start(bf16[5,128,256]{2,1,0:T(8,128)(2,1)S(1)} %collective-permute-done.6.refs_5_) | copy-start | bytes 983044
  92.9 3.5 %collective-permute-start.7 = (bf16[5,128,256]{2,1,0:T(8,128)(2,1)S(1)}, bf16[5,128,256]{2,1,0:T(8,128)(2,1)S(1)}, u32[]{:S(2)}, u32[]{:S(2)}) collective-permute-start(bf16[5,128,256]{2,1,0:T(8,128)(2,1)S(1)} %collective-permute-done.6.refs_5_), channel_id=1, source_target_pairs={{0,32},{32,0},{1,33},{33,1},{2,34},{34,2},{3,35},{35,3},{4,36},{36... | collective-permute-start | bytes 983048 | tf_op jit(solution)/shard_map/ppermute | solution.py:121
  95.2 0.7 copy-start.5
  96.5 0.8 copy-start.3
  96.5 1.0 copy-start.1

commit v2 on v1

--- a/solution.py
+++ b/solution.py
@@ -52,11 +52,9 @@
     )(owners, pltpu.with_memory_space_constraint(pieces, pltpu.VMEM))
 
 
-BLOCK = ((-1, 0), (0, 0), (1, 0))
-FAR = ((-4, 0), (-3, 0), (-2, 0), (2, 0), (3, 0))
-OTHER_BLOCK = tuple((x, 1) for x, _ in BLOCK)
-OTHER_FAR = tuple((x, 1) for x, _ in FAR)
-NEAR = BLOCK + FAR + OTHER_BLOCK
+NEAR = ((-1, 0), (-1, 1), (0, 0), (0, 1), (1, 0), (1, 1))
+UP = ((-4, 0), (-3, 0), (-3, 1), (-2, 0), (-2, 1))
+DOWN = ((2, 0), (2, 1), (3, 0), (3, 1), (4, 1))
 
 
 def ladder_kernel(groups, piece_ref, here_ref, side_ref, *refs):
@@ -123,27 +121,28 @@
 
 def per_device(amplitudes, pair_irrep, integrals, panel_blocks, panel_owner):
     cols = integrals.shape[-1]
-    left = shift(amplitudes, "x", N_X, 1)
-    right = shift(amplitudes, "x", N_X, -1)
+    partner = shift(amplitudes, "zl", 2, 1)
     ordered = irrep_order(integrals[0], panel_blocks[0])
     pieces = lax.all_to_all(ordered.reshape(N_VIR, -1, cols), VIR, 0, 0, tiled=True)
-    block = jnp.stack([left, amplitudes, right])
-    up = shift(block, "x", N_X, 3)
-    down = shift(block, "x", N_X, -3)
-    other_block = shift(block, "zl", 2, 1)
+    pair = jnp.stack([amplitudes, partner])
+    left = shift(pair, "x", N_X, 1)
+    right = shift(pair, "x", N_X, -1)
     here = jnp.stack([lax.axis_index("zl"), lax.axis_index("x")])
     copies = pick_and_copy(pieces, panel_owner)
+    for_up = jnp.concatenate([left[:1], pair, right])
+    for_down = jnp.concatenate([left, pair, right[1:]])
+    up = shift(for_up, "x", N_X, 3)
+    down = shift(for_down, "x", N_X, -3)
     weights = lax.all_to_all(copies, VIR, 0, 0, tiled=True)
+    near = jnp.concatenate([left, pair, right])
+    share_near = shift(near, "core", 2, 1)
     side = jnp.arange(16, dtype=jnp.int32) + lax.axis_index("core")
-    far = jnp.concatenate([up, down[:2]])
-    other_far = shift(far, "zl", 2, 1)
-    near = jnp.concatenate([block, up, down[:2], other_block])
-    share_near = shift(near, "core", 2, 1)
+    share_up = shift(up, "core", 2, 1)
+    share_down = shift(down, "core", 2, 1)
     first_piece = pair_irrep * (N_VIR // IRREPS)
-    share_far = shift(other_far, "core", 2, 1)
-    groups = ((0, NEAR), (1, NEAR), (0, OTHER_FAR), (1, OTHER_FAR))
-    return contract(
-        groups, (near, share_near, other_far, share_far), first_piece, here, side, weights)
+    groups = ((0, NEAR), (1, NEAR), (0, UP), (0, DOWN), (1, UP), (1, DOWN))
+    arrays = (near, share_near, up, down, share_up, share_down)
+    return contract(groups, arrays, first_piece, here, side, weights)
 
 
 def solution(mesh):

time: 102 us -> 99.4 us (0.975)
  waiting for transfers between devices: 30.6 us -> 22.1 us
  starting transfers between devices: 60.5 us -> 63.7 us
  local copies, waits for them, and re-layouts: 1.11 us -> 2.38 us
  other arithmetic: 1.73 us -> 2.86 us
    ppermute x8, waiting for transfers between devices: 30.6 us -> 13.8 us  [shift(): lax.ppermute(array, axis, [(index, (index + step) % size) for index in ra...]
    all_to_all x1, waiting for transfers between devices: 0.01 us -> 8.33 us  [per_device(): lax.all_to_all(ordered.reshape(N_VIR, -1, cols), VIR, 0, 0, tiled=True)]
    ppermute x8, starting transfers between devices: 27.1 us -> 35.4 us  [shift(): lax.ppermute(array, axis, [(index, (index + step) % size) for index in ra...]
    all_to_all x1, starting transfers between devices: 11.6 us -> 5.7 us  [per_device(): weights = lax.all_to_all(copies, VIR, 0, 0, tiled=True)]
    concatenate x1 -> x2, other arithmetic: 0.03 us -> 1.1 us  [the longest x1 1.05 us: per_device(): for_down = jnp.concatenate([left, pair, right[1:]])]
  transfers between devices with their start and end apart: 10 -> 10, of which waited for: 3 -> 3; matrix products, arithmetic and copies ran while one was open for 2% -> 3% of each run, Pallas kernels for 3% -> 2%
where the time goes in v2:
time: 99.4 us; the launch traced here: 98.7 us
  starting transfers between devices  63.7 us (64%)
  waiting for transfers between devices  22.1 us (22%)
  Pallas kernels  7.46 us (8%)
  other arithmetic  2.86 us (3%)
  local copies, waits for them, and re-layouts  2.38 us (2%)
    ppermute x8, starting transfers between devices, shift(): lax.ppermute(array, axis, [(index, (index + step) % size) for index in ra...  35.4 us
    all_to_all x1, starting transfers between devices, per_device(): lax.all_to_all(ordered.reshape(N_VIR, -1, cols), VIR, 0, 0, tiled=True)  22.5 us
    ppermute x8, waiting for transfers between devices, shift(): lax.ppermute(array, axis, [(index, (index + step) % size) for index in ra...  13.8 us
    all_to_all x1, waiting for transfers between devices, per_device(): lax.all_to_all(ordered.reshape(N_VIR, -1, cols), VIR, 0, 0, tiled=True)  8.33 us
    all_to_all x1, starting transfers between devices, per_device(): weights = lax.all_to_all(copies, VIR, 0, 0, tiled=True)  5.7 us
    pallas_call x1, Pallas kernels, contract(): pl.pallas_call(lambda *refs: ladder_kernel(groups, *refs), out_shape=jax....  4.2 us
  transfers between devices with their start and end apart: 10, of which 3 were waited for; matrix products, arithmetic and copies ran while one was open for 3% of the time, Pallas kernels for 2%

profile of v2, /device:TPU:1, one launch (start us, length us, event | category | flops | bytes accessed | tf_op | source)
XLA Modules:
  0.0 98.7 jit_solution(554915467938817154)
XLA Ops:
  0.0 1.7 %irrep_order.1 = bf16[8,128,128]{2,1,0:T(8,128)(2,1)} custom-call(s32[8]{0:T(128)} %bitcast.15, bf16[8,128,128]{2,1,0:T(8,128)(2,1)} %bitcast.14), custom_call_target="tpu_custom_call" | custom-call | tf_op jit(solution)/shard_map/irrep_order/pallas_call | solution.py:22
  1.7 22.5 %all-to-all-start = ((bf16[32,32,128]{2,1,0:T(8,128)(2,1)}), bf16[32,32,128]{2,1,0:T(8,128)(2,1)S(1)}, u32[]{:S(2)}, u32[]{:S(2)}) async-start(bf16[32,32,128]{2,1,0:T(8,128)(2,1)} %bitcast.6), calls=%async_computation | async-start | bytes 524288 | tf_op jit(solution)/shard_map/all_to_all | solution.py:126
  24.2 4.0 %collective-permute-start = (bf16[128,256]{1,0:T(8,128)(2,1)S(1)}, bf16[128,256]{1,0:T(8,128)(2,1)S(1)}, u32[]{:S(2)}, u32[]{:S(2)}) collective-permute-start(bf16[128,256]{1,0:T(8,128)(2,1)S(1)} %copy-done.3), channel_id=1, source_target_pairs={{0,512},{512,0},{1,513},{513,1},{2,514},{514,2},{3,515},{515,3},{4... | collective-permute-start | bytes 196616 | tf_op jit(solution)/shard_map/ppermute | solution.py:119
  28.3 8.3 %all-to-all-done.pieces_ref = bf16[32,32,128]{2,1,0:T(8,128)(2,1)S(1)} async-done(((bf16[32,32,128]{2,1,0:T(8,128)(2,1)}), bf16[32,32,128]{2,1,0:T(8,128)(2,1)S(1)}, u32[]{:S(2)}, u32[]{:S(2)}) %all-to-all-start) | async-done | bytes 262176 | tf_op jit(solution)/shard_map/all_to_all | solution.py:126
  36.6 1.6 %shard_map.55 = bf16[32,64,128]{2,1,0:T(8,128)(2,1)} custom-call(s32[2]{0:T(128)} %owner_ref.1, bf16[32,32,128]{2,1,0:T(8,128)(2,1)S(1)} %all-to-all-done.pieces_ref), custom_call_target="tpu_custom_call" | custom-call | tf_op jit(solution)/shard_map/pallas_call | solution.py:44
  38.2 5.7 %all-to-all-start.1 = ((bf16[32,64,128]{2,1,0:T(8,128)(2,1)}), bf16[32,64,128]{2,1,0:T(8,128)(2,1)S(1)}, u32[]{:S(2)}, u32[]{:S(2)}) async-start(bf16[32,64,128]{2,1,0:T(8,128)(2,1)} %shard_map.55), calls=%async_computation.1 | async-start | bytes 1048576 | tf_op jit(solution)/shard_map/all_to_all | solution.py:136
  43.9 4.5 %collective-permute-start.2 = (bf16[2,128,256]{2,1,0:T(8,128)(2,1)S(1)}, bf16[2,128,256]{2,1,0:T(8,128)(2,1)S(1)}, u32[]{:S(2)}, u32[]{:S(2)}) collective-permute-start(bf16[2,128,256]{2,1,0:T(8,128)(2,1)S(1)} %pad_maximum_fusion.3), channel_id=1, source_target_pairs={{0,448},{64,0},{128,64},{192,128},{256,192},{320,256},{384,320},{4... | collective-permute-start | bytes 393224 | tf_op jit(solution)/shard_map/ppermute | solution.py:119
  48.4 1.9 %collective-permute-start.1 = (bf16[2,128,256]{2,1,0:T(8,128)(2,1)S(1)}, bf16[2,128,256]{2,1,0:T(8,128)(2,1)S(1)}, u32[]{:S(2)}, u32[]{:S(2)}) collective-permute-start(bf16[2,128,256]{2,1,0:T(8,128)(2,1)S(1)} %pad_maximum_fusion.3), channel_id=1, source_target_pairs={{0,64},{64,128},{128,192},{192,256},{256,320},{320,384},{384,448},... | collective-permute-start | bytes 393224 | tf_op jit(solution)/shard_map/ppermute | solution.py:119
  50.3 0.0 collective-permute-done.2
  50.4 0.6 copy-done.1
  51.0 4.6 %collective-permute-done.1 = bf16[2,128,256]{2,1,0:T(8,128)(2,1)S(1)} collective-permute-done((bf16[2,128,256]{2,1,0:T(8,128)(2,1)S(1)}, bf16[2,128,256]{2,1,0:T(8,128)(2,1)S(1)}, u32[]{:S(2)}, u32[]{:S(2)}) %collective-permute-start.1) | collective-permute-done | bytes 131104 | tf_op jit(solution)/shard_map/ppermute | solution.py:119
  55.6 0.8 slice-done
  56.5 1.0 %pad_maximum_fusion.2 = (bf16[5,128,256]{2,1,0:T(8,128)(2,1)S(1)}, bf16[5,128,256]{2,1,0:T(8,128)(2,1)S(1)}) fusion(bf16[1,128,256]{2,1,0:T(8,128)(2,1)S(1)} %slice-done, bf16[1,128,256]{2,1,0:T(8,128)(2,1)S(1)} %bitcast.12, bf16[1,128,256]{2,1,0:T(8,128)(2,1)S(1)} %bitcast.9, bf16[2,128,256]{2,1,0:T(8,128)(2,1)S(1)} %collective-permute-done.1, ...), kind=kLoop, calls=%fused_computation.2 | loop fusion | flops 983040 | bytes 1179648 | tf_op jit(solution)/shard_map/concatenate | solution.py:133
  57.5 3.6 %collective-permute-start.5 = (bf16[5,128,256]{2,1,0:T(8,128)(2,1)S(1)}, bf16[5,128,256]{2,1,0:T(8,128)(2,1)S(1)}, u32[]{:S(2)}, u32[]{:S(2)}) collective-permute-start(bf16[5,128,256]{2,1,0:T(8,128)(2,1)S(1)} %get-tuple-element.5), channel_id=1, source_target_pairs={{0,320},{64,384},{128,448},{192,0},{256,64},{320,128},{384,192},{4... | collective-permute-start | bytes 983048 | tf_op jit(solution)/shard_map/ppermute | solution.py:119
  61.1 3.5 %collective-permute-start.4 = (bf16[5,128,256]{2,1,0:T(8,128)(2,1)S(1)}, bf16[5,128,256]{2,1,0:T(8,128)(2,1)S(1)}, u32[]{:S(2)}, u32[]{:S(2)}) collective-permute-start(bf16[5,128,256]{2,1,0:T(8,128)(2,1)S(1)} %get-tuple-element.6), channel_id=1, source_target_pairs={{0,192},{64,256},{128,320},{192,384},{256,448},{320,0},{384,64},{4... | collective-permute-start | bytes 983048 | tf_op jit(solution)/shard_map/ppermute | solution.py:119
  64.6 0.1 pad_maximum_fusion.refs_3_
  64.7 5.3 %collective-permute-start.3 = (bf16[6,128,256]{2,1,0:T(8,128)(2,1)S(1)}, bf16[6,128,256]{2,1,0:T(8,128)(2,1)S(1)}, u32[]{:S(2)}, u32[]{:S(2)}) collective-permute-start(bf16[6,128,256]{2,1,0:T(8,128)(2,1)S(1)} %pad_maximum_fusion.refs_3_), channel_id=1, source_target_pairs={{0,32},{32,0},{1,33},{33,1},{2,34},{34,2},{3,35},{35,3},{4,36},{36... | collective-permute-start | bytes 1179656 | tf_op jit(solution)/shard_map/ppermute | solution.py:119
  70.0 0.5 iota_add_fusion.refs_2_
  70.5 9.2 %collective-permute-done.5.refs_6_ = bf16[5,128,256]{2,1,0:T(8,128)(2,1)S(1)} collective-permute-done((bf16[5,128,256]{2,1,0:T(8,128)(2,1)S(1)}, bf16[5,128,256]{2,1,0:T(8,128)(2,1)S(1)}, u32[]{:S(2)}, u32[]{:S(2)}) %collective-permute-start.5) | collective-permute-done | bytes 327712 | tf_op jit(solution)/shard_map/ppermute | solution.py:119
  79.7 7.2 %collective-permute-start.7 = (bf16[5,128,256]{2,1,0:T(8,128)(2,1)S(1)}, bf16[5,128,256]{2,1,0:T(8,128)(2,1)S(1)}, u32[]{:S(2)}, u32[]{:S(2)}) collective-permute-start(bf16[5,128,256]{2,1,0:T(8,128)(2,1)S(1)} %collective-permute-done.5.refs_6_), channel_id=1, source_target_pairs={{0,32},{32,0},{1,33},{33,1},{2,34},{34,2},{3,35},{35,3},{4,36},{36... | collective-permute-start | bytes 983048 | tf_op jit(solution)/shard_map/ppermute | solution.py:119
  86.9 0.0 collective-permute-done.4.refs_5_
  86.9 5.5 %collective-permute-start.6 = (bf16[5,128,256]{2,1,0:T(8,128)(2,1)S(1)}, bf16[5,128,256]{2,1,0:T(8,128)(2,1)S(1)}, u32[]{:S(2)}, u32[]{:S(2)}) collective-permute-start(bf16[5,128,256]{2,1,0:T(8,128)(2,1)S(1)} %collective-permute-done.4.refs_5_), channel_id=1, source_target_pairs={{0,32},{32,0},{1,33},{33,1},{2,34},{34,2},{3,35},{35,3},{4,36},{36... | collective-permute-start | bytes 983048 | tf_op jit(solution)/shard_map/ppermute | solution.py:119
  92.4 0.0 copy-start.9
  92.4 0.7 pad_add_fusion.refs_1_
  93.0 0.5 broadcast_multiply_fusion.refs_0_
  93.6 0.0 collective-permute-done.3.refs_4_
  93.6 0.0 collective-permute-done.7.refs_8_
  93.6 0.0 all-to-all-done.1.refs_9_
  93.7 0.7 copy-done.4
  94.3 0.1 copy-done.7
  94.4 0.1 copy-done.8
  94.5 4.2 %ladder.1 = bf16[32,128,128]{2,1,0:T(8,128)(2,1)} custom-call(s32[32]{0:T(128)} %broadcast_multiply_fusion.refs_0_, s32[2]{0:T(128)} %pad_add_fusion.refs_1_, s32[16]{0:T(128)} %iota_add_fusion.refs_2_, bf16[6,128,256]{2,1,0:T(8,128)(2,1)} %copy-done, bf16[6,128,256]{2,1,0:T(8,128)(2,1)} %copy-done.4, bf16[5,128,256]{2,1,0:T(8,128)(2,1)} %copy-done.6, ...), custom_call_target="tpu_custom_call" | custom-call | tf_op jit(solution)/shard_map/ladder/pallas_call | solution.py:102
  (20 shorter events, 0.1 us)
Async XLA Ops:
  1.7 22.5 %copy-start.3 = (bf16[128,256]{1,0:T(8,128)(2,1)S(1)}, bf16[128,256]{1,0:T(8,128)(2,1)}, u32[]{:S(2)}) copy-start(bf16[128,256]{1,0:T(8,128)(2,1)} %param.5) | copy-start | bytes 196612
  1.7 34.9 %all-to-all-start = ((bf16[32,32,128]{2,1,0:T(8,128)(2,1)}), bf16[32,32,128]{2,1,0:T(8,128)(2,1)S(1)}, u32[]{:S(2)}, u32[]{:S(2)}) async-start(bf16[32,32,128]{2,1,0:T(8,128)(2,1)} %bitcast.6), calls=%async_computation | async-start | bytes 524288 | tf_op jit(solution)/shard_map/all_to_all | solution.py:126
  24.2 19.6 %collective-permute-start = (bf16[128,256]{1,0:T(8,128)(2,1)S(1)}, bf16[128,256]{1,0:T(8,128)(2,1)S(1)}, u32[]{:S(2)}, u32[]{:S(2)}) collective-permute-start(bf16[128,256]{1,0:T(8,128)(2,1)S(1)} %copy-done.3), channel_id=1, source_target_pairs={{0,512},{512,0},{1,513},{513,1},{2,514},{514,2},{3,515},{515,3},{4... | collective-permute-start | bytes 196616 | tf_op jit(solution)/shard_map/ppermute | solution.py:119
  38.2 55.5 %all-to-all-start.1 = ((bf16[32,64,128]{2,1,0:T(8,128)(2,1)}), bf16[32,64,128]{2,1,0:T(8,128)(2,1)S(1)}, u32[]{:S(2)}, u32[]{:S(2)}) async-start(bf16[32,64,128]{2,1,0:T(8,128)(2,1)} %shard_map.55), calls=%async_computation.1 | async-start | bytes 1048576 | tf_op jit(solution)/shard_map/all_to_all | solution.py:136
  43.9 6.4 %collective-permute-start.2 = (bf16[2,128,256]{2,1,0:T(8,128)(2,1)S(1)}, bf16[2,128,256]{2,1,0:T(8,128)(2,1)S(1)}, u32[]{:S(2)}, u32[]{:S(2)}) collective-permute-start(bf16[2,128,256]{2,1,0:T(8,128)(2,1)S(1)} %pad_maximum_fusion.3), channel_id=1, source_target_pairs={{0,448},{64,0},{128,64},{192,128},{256,192},{320,256},{384,320},{4... | collective-permute-start | bytes 393224 | tf_op jit(solution)/shard_map/ppermute | solution.py:119
  48.4 7.2 %collective-permute-start.1 = (bf16[2,128,256]{2,1,0:T(8,128)(2,1)S(1)}, bf16[2,128,256]{2,1,0:T(8,128)(2,1)S(1)}, u32[]{:S(2)}, u32[]{:S(2)}) collective-permute-start(bf16[2,128,256]{2,1,0:T(8,128)(2,1)S(1)} %pad_maximum_fusion.3), channel_id=1, source_target_pairs={{0,64},{64,128},{128,192},{192,256},{256,320},{320,384},{384,448},... | collective-permute-start | bytes 393224 | tf_op jit(solution)/shard_map/ppermute | solution.py:119
  50.4 0.6 copy-start.1
  55.6 0.8 slice-start
  56.5 8.2 %copy-start.2 = (bf16[2,128,256]{2,1,0:T(8,128)(2,1)S(1)}, bf16[2,128,256]{2,1,0:T(8,128)(2,1)}, u32[]{:S(2)}) copy-start(bf16[2,128,256]{2,1,0:T(8,128)(2,1)} %copy-done.1) | copy-start | bytes 393220
  57.5 22.2 %collective-permute-start.5 = (bf16[5,128,256]{2,1,0:T(8,128)(2,1)S(1)}, bf16[5,128,256]{2,1,0:T(8,128)(2,1)S(1)}, u32[]{:S(2)}, u32[]{:S(2)}) collective-permute-start(bf16[5,128,256]{2,1,0:T(8,128)(2,1)S(1)} %get-tuple-element.5), channel_id=1, source_target_pairs={{0,320},{64,384},{128,448},{192,0},{256,64},{320,128},{384,192},{4... | collective-permute-start | bytes 983048 | tf_op jit(solution)/shard_map/ppermute | solution.py:119
  61.1 25.7 %collective-permute-start.4 = (bf16[5,128,256]{2,1,0:T(8,128)(2,1)S(1)}, bf16[5,128,256]{2,1,0:T(8,128)(2,1)S(1)}, u32[]{:S(2)}, u32[]{:S(2)}) collective-permute-start(bf16[5,128,256]{2,1,0:T(8,128)(2,1)S(1)} %get-tuple-element.6), channel_id=1, source_target_pairs={{0,192},{64,256},{128,320},{192,384},{256,448},{320,0},{384,64},{4... | collective-permute-start | bytes 983048 | tf_op jit(solution)/shard_map/ppermute | solution.py:119
  64.7 28.9 %copy-start = (bf16[6,128,256]{2,1,0:T(8,128)(2,1)}, bf16[6,128,256]{2,1,0:T(8,128)(2,1)S(1)}, u32[]{:S(2)}) copy-start(bf16[6,128,256]{2,1,0:T(8,128)(2,1)S(1)} %pad_maximum_fusion.refs_3_) | copy-start | bytes 1179652
  64.7 28.9 %collective-permute-start.3 = (bf16[6,128,256]{2,1,0:T(8,128)(2,1)S(1)}, bf16[6,128,256]{2,1,0:T(8,128)(2,1)S(1)}, u32[]{:S(2)}, u32[]{:S(2)}) collective-permute-start(bf16[6,128,256]{2,1,0:T(8,128)(2,1)S(1)} %pad_maximum_fusion.refs_3_), channel_id=1, source_target_pairs={{0,32},{32,0},{1,33},{33,1},{2,34},{34,2},{3,35},{35,3},{4,36},{36... | collective-permute-start | bytes 1179656 | tf_op jit(solution)/shard_map/ppermute | solution.py:119
  79.7 14.0 %copy-start.5 = (bf16[5,128,256]{2,1,0:T(8,128)(2,1)}, bf16[5,128,256]{2,1,0:T(8,128)(2,1)S(1)}, u32[]{:S(2)}) copy-start(bf16[5,128,256]{2,1,0:T(8,128)(2,1)S(1)} %collective-permute-done.5.refs_6_) | copy-start | bytes 983044
  79.7 13.9 %collective-permute-start.7 = (bf16[5,128,256]{2,1,0:T(8,128)(2,1)S(1)}, bf16[5,128,256]{2,1,0:T(8,128)(2,1)S(1)}, u32[]{:S(2)}, u32[]{:S(2)}) collective-permute-start(bf16[5,128,256]{2,1,0:T(8,128)(2,1)S(1)} %collective-permute-done.5.refs_6_), channel_id=1, source_target_pairs={{0,32},{32,0},{1,33},{33,1},{2,34},{34,2},{3,35},{35,3},{4,36},{36... | collective-permute-start | bytes 983048 | tf_op jit(solution)/shard_map/ppermute | solution.py:119
  86.9 6.8 %copy-start.6 = (bf16[5,128,256]{2,1,0:T(8,128)(2,1)}, bf16[5,128,256]{2,1,0:T(8,128)(2,1)S(1)}, u32[]{:S(2)}) copy-start(bf16[5,128,256]{2,1,0:T(8,128)(2,1)S(1)} %collective-permute-done.4.refs_5_) | copy-start | bytes 983044
  86.9 6.7 %collective-permute-start.6 = (bf16[5,128,256]{2,1,0:T(8,128)(2,1)S(1)}, bf16[5,128,256]{2,1,0:T(8,128)(2,1)S(1)}, u32[]{:S(2)}, u32[]{:S(2)}) collective-permute-start(bf16[5,128,256]{2,1,0:T(8,128)(2,1)S(1)} %collective-permute-done.4.refs_5_), channel_id=1, source_target_pairs={{0,32},{32,0},{1,33},{33,1},{2,34},{34,2},{3,35},{35,3},{4,36},{36... | collective-permute-start | bytes 983048 | tf_op jit(solution)/shard_map/ppermute | solution.py:119
  92.4 0.7 copy-start.9
  93.6 0.7 copy-start.4
  93.6 0.8 copy-start.7
  93.6 0.9 copy-start.8

commit v3 on v2

--- a/solution.py
+++ b/solution.py
@@ -52,9 +52,7 @@
     )(owners, pltpu.with_memory_space_constraint(pieces, pltpu.VMEM))
 
 
-NEAR = ((-1, 0), (-1, 1), (0, 0), (0, 1), (1, 0), (1, 1))
-UP = ((-4, 0), (-3, 0), (-3, 1), (-2, 0), (-2, 1))
-DOWN = ((2, 0), (2, 1), (3, 0), (3, 1), (4, 1))
+TILES = tuple((x, zl) for x in (-1, 0, 1, 4, -3, -2, 2, 3) for zl in (0, 1))
 
 
 def ladder_kernel(groups, piece_ref, here_ref, side_ref, *refs):
@@ -127,22 +125,18 @@
     pair = jnp.stack([amplitudes, partner])
     left = shift(pair, "x", N_X, 1)
     right = shift(pair, "x", N_X, -1)
+    opposite = shift(pair, "x", N_X, 4)
     here = jnp.stack([lax.axis_index("zl"), lax.axis_index("x")])
     copies = pick_and_copy(pieces, panel_owner)
-    for_up = jnp.concatenate([left[:1], pair, right])
-    for_down = jnp.concatenate([left, pair, right[1:]])
-    up = shift(for_up, "x", N_X, 3)
-    down = shift(for_down, "x", N_X, -3)
+    up = shift(jnp.concatenate([left, pair]), "x", N_X, 2)
+    down = shift(jnp.concatenate([pair, right]), "x", N_X, -2)
     weights = lax.all_to_all(copies, VIR, 0, 0, tiled=True)
-    near = jnp.concatenate([left, pair, right])
-    share_near = shift(near, "core", 2, 1)
     side = jnp.arange(16, dtype=jnp.int32) + lax.axis_index("core")
-    share_up = shift(up, "core", 2, 1)
-    share_down = shift(down, "core", 2, 1)
+    mine = jnp.concatenate([left, pair, right, opposite, up, down])
+    theirs = shift(mine, "core", 2, 1)
     first_piece = pair_irrep * (N_VIR // IRREPS)
-    groups = ((0, NEAR), (1, NEAR), (0, UP), (0, DOWN), (1, UP), (1, DOWN))
-    arrays = (near, share_near, up, down, share_up, share_down)
-    return contract(groups, arrays, first_piece, here, side, weights)
+    groups = ((0, TILES), (1, TILES))
+    return contract(groups, (mine, theirs), first_piece, here, side, weights)
 
 
 def solution(mesh):

time: 99.4 us -> 103 us (1.036)
  the two profiles are of different devices: /device:TPU:1 before, /device:TPU:18 now
where the time goes in v3:
time: 103 us
  starting transfers between devices  59.6 us (58%)
  waiting for transfers between devices  33.2 us (32%)
  Pallas kernels  6.97 us (7%)
  other arithmetic  2.59 us (3%)
    ppermute x7, starting transfers between devices, shift(): lax.ppermute(array, axis, [(index, (index + step) % size) for index in ra...  26.2 us
    all_to_all x1, starting transfers between devices, per_device(): lax.all_to_all(ordered.reshape(N_VIR, -1, cols), VIR, 0, 0, tiled=True)  21.2 us
    all_to_all x1, waiting for transfers between devices, per_device(): weights = lax.all_to_all(copies, VIR, 0, 0, tiled=True)  19.1 us
    ppermute x7, waiting for transfers between devices, shift(): lax.ppermute(array, axis, [(index, (index + step) % size) for index in ra...  14.1 us
    all_to_all x1, starting transfers between devices, per_device(): weights = lax.all_to_all(copies, VIR, 0, 0, tiled=True)  12.2 us
    pallas_call x1, Pallas kernels, contract(): pl.pallas_call(lambda *refs: ladder_kernel(groups, *refs), out_shape=jax....  3.7 us
  transfers between devices with their start and end apart: 9, of which 3 were waited for; matrix products, arithmetic and copies ran while one was open for 2% of the time, Pallas kernels for 3%

profile of v3, /device:TPU:18, one launch (start us, length us, event | category | flops | bytes accessed | tf_op | source)
XLA Modules:
  0.0 102.7 jit_solution(14973690882140461147)
XLA Ops:
  0.0 5.2 %collective-permute-start = (bf16[128,256]{1,0:T(8,128)(2,1)}, bf16[128,256]{1,0:T(8,128)(2,1)S(1)}, u32[]{:S(2)}, u32[]{:S(2)}) collective-permute-start(bf16[128,256]{1,0:T(8,128)(2,1)} %param.5), channel_id=1, source_target_pairs={{0,512},{512,0},{1,513},{513,1},{2,514},{514,2},{3,515},{515,3},{4... | collective-permute-start | bytes 196616 | tf_op jit(solution)/shard_map/ppermute | solution.py:117
  5.2 2.4 %collective-permute-done = bf16[128,256]{1,0:T(8,128)(2,1)S(1)} collective-permute-done((bf16[128,256]{1,0:T(8,128)(2,1)}, bf16[128,256]{1,0:T(8,128)(2,1)S(1)}, u32[]{:S(2)}, u32[]{:S(2)}) %collective-permute-start) | collective-permute-done | bytes 65568 | tf_op jit(solution)/shard_map/ppermute | solution.py:117
  7.6 0.9 pad_maximum_fusion.2
  8.5 2.4 %collective-permute-start.2 = (bf16[2,128,256]{2,1,0:T(8,128)(2,1)S(1)}, bf16[2,128,256]{2,1,0:T(8,128)(2,1)S(1)}, u32[]{:S(2)}, u32[]{:S(2)}) collective-permute-start(bf16[2,128,256]{2,1,0:T(8,128)(2,1)S(1)} %pad_maximum_fusion.2), channel_id=1, source_target_pairs={{0,448},{64,0},{128,64},{192,128},{256,192},{320,256},{384,320},{4... | collective-permute-start | bytes 393224 | tf_op jit(solution)/shard_map/ppermute | solution.py:117
  10.9 3.4 %collective-permute-start.1 = (bf16[2,128,256]{2,1,0:T(8,128)(2,1)S(1)}, bf16[2,128,256]{2,1,0:T(8,128)(2,1)S(1)}, u32[]{:S(2)}, u32[]{:S(2)}) collective-permute-start(bf16[2,128,256]{2,1,0:T(8,128)(2,1)S(1)} %pad_maximum_fusion.2), channel_id=1, source_target_pairs={{0,64},{64,128},{128,192},{192,256},{256,320},{320,384},{384,448},... | collective-permute-start | bytes 393224 | tf_op jit(solution)/shard_map/ppermute | solution.py:117
  14.3 1.7 %irrep_order.1 = bf16[8,128,128]{2,1,0:T(8,128)(2,1)} custom-call(s32[8]{0:T(128)} %bitcast.15, bf16[8,128,128]{2,1,0:T(8,128)(2,1)} %bitcast.14), custom_call_target="tpu_custom_call" | custom-call | tf_op jit(solution)/shard_map/irrep_order/pallas_call | solution.py:22
  16.0 0.0 copy-start.2
  16.0 21.2 %all-to-all-start = ((bf16[32,32,128]{2,1,0:T(8,128)(2,1)}), bf16[32,32,128]{2,1,0:T(8,128)(2,1)S(1)}, u32[]{:S(2)}, u32[]{:S(2)}) async-start(bf16[32,32,128]{2,1,0:T(8,128)(2,1)} %bitcast.6), calls=%async_computation | async-start | bytes 524288 | tf_op jit(solution)/shard_map/all_to_all | solution.py:124
  37.2 6.5 %collective-permute-start.3 = (bf16[2,128,256]{2,1,0:T(8,128)(2,1)S(1)}, bf16[2,128,256]{2,1,0:T(8,128)(2,1)S(1)}, u32[]{:S(2)}, u32[]{:S(2)}) collective-permute-start(bf16[2,128,256]{2,1,0:T(8,128)(2,1)S(1)} %pad_maximum_fusion.2), channel_id=1, source_target_pairs={{0,256},{64,320},{128,384},{192,448},{256,0},{320,64},{384,128},{4... | collective-permute-start | bytes 393224 | tf_op jit(solution)/shard_map/ppermute | solution.py:117
  43.7 0.0 collective-permute-done.2
  43.8 0.0 collective-permute-done.1
  43.8 0.0 copy-done.2
  43.8 4.5 %collective-permute-start.5 = (bf16[4,128,256]{2,1,0:T(8,128)(2,1)S(1)}, bf16[4,128,256]{2,1,0:T(8,128)(2,1)S(1)}, u32[]{:S(2)}, u32[]{:S(2)}) collective-permute-start(bf16[4,128,256]{2,1,0:T(8,128)(2,1)S(1)} %get-tuple-element.5), channel_id=1, source_target_pairs={{0,384},{64,448},{128,0},{192,64},{256,128},{320,192},{384,256},{4... | collective-permute-start | bytes 786440 | tf_op jit(solution)/shard_map/ppermute | solution.py:117
  48.4 2.2 %collective-permute-start.4 = (bf16[4,128,256]{2,1,0:T(8,128)(2,1)S(1)}, bf16[4,128,256]{2,1,0:T(8,128)(2,1)S(1)}, u32[]{:S(2)}, u32[]{:S(2)}) collective-permute-start(bf16[4,128,256]{2,1,0:T(8,128)(2,1)S(1)} %get-tuple-element.6), channel_id=1, source_target_pairs={{0,128},{64,192},{128,256},{192,320},{256,384},{320,448},{384,0},{... | collective-permute-start | bytes 786440 | tf_op jit(solution)/shard_map/ppermute | solution.py:117
  50.7 0.0 collective-permute-done.3
  50.7 11.7 %collective-permute-done.4 = bf16[4,128,256]{2,1,0:T(8,128)(2,1)S(1)} collective-permute-done((bf16[4,128,256]{2,1,0:T(8,128)(2,1)S(1)}, bf16[4,128,256]{2,1,0:T(8,128)(2,1)S(1)}, u32[]{:S(2)}, u32[]{:S(2)}) %collective-permute-start.4) | collective-permute-done | bytes 262176 | tf_op jit(solution)/shard_map/ppermute | solution.py:117
  62.4 0.0 collective-permute-done.5
  62.4 0.0 copy-start
  62.4 1.9 %collective-permute-start.6 = (bf16[16,128,256]{2,1,0:T(8,128)(2,1)S(1)}, bf16[16,128,256]{2,1,0:T(8,128)(2,1)S(1)}, u32[]{:S(2)}, u32[]{:S(2)}) collective-permute-start(bf16[16,128,256]{2,1,0:T(8,128)(2,1)S(1)} %constant_dynamic-update-slice_fusion.refs_3_), channel_id=1, source_target_pairs={{0,32},{32,0},{1,33},{33,1},{2,34},{34,2},{3,35},{35,3},{4,36},{36... | collective-permute-start | bytes 3145736 | tf_op jit(solution)/shard_map/ppermute | solution.py:117
  64.3 0.0 all-to-all-done.pieces_ref
  64.3 1.6 %shard_map.55 = bf16[32,64,128]{2,1,0:T(8,128)(2,1)} custom-call(s32[2]{0:T(128)} %owner_ref.1, bf16[32,32,128]{2,1,0:T(8,128)(2,1)S(1)} %all-to-all-done.pieces_ref), custom_call_target="tpu_custom_call" | custom-call | tf_op jit(solution)/shard_map/pallas_call | solution.py:44
  65.9 12.2 %all-to-all-start.1 = ((bf16[32,64,128]{2,1,0:T(8,128)(2,1)}), bf16[32,64,128]{2,1,0:T(8,128)(2,1)S(1)}, u32[]{:S(2)}, u32[]{:S(2)}) async-start(bf16[32,64,128]{2,1,0:T(8,128)(2,1)} %shard_map.55), calls=%async_computation.1 | async-start | bytes 1048576 | tf_op jit(solution)/shard_map/all_to_all | solution.py:133
  78.1 0.5 iota_add_fusion.refs_2_
  78.7 0.0 copy-start.3
  78.7 0.6 pad_add_fusion.refs_1_
  79.2 0.1 copy-done.3
  79.3 0.6 broadcast_multiply_fusion.refs_0_
  79.9 0.0 collective-permute-done.6.refs_4_
  79.9 19.1 %all-to-all-done.1.refs_5_ = bf16[32,64,128]{2,1,0:T(8,128)(2,1)S(1)} async-done(((bf16[32,64,128]{2,1,0:T(8,128)(2,1)}), bf16[32,64,128]{2,1,0:T(8,128)(2,1)S(1)}, u32[]{:S(2)}, u32[]{:S(2)}) %all-to-all-start.1) | async-done | bytes 524320 | tf_op jit(solution)/shard_map/all_to_all | solution.py:133
  99.0 0.0 copy-done
  99.0 0.0 copy-done.1
  99.0 3.7 %ladder.1 = bf16[32,128,128]{2,1,0:T(8,128)(2,1)} custom-call(s32[32]{0:T(128)} %broadcast_multiply_fusion.refs_0_, s32[2]{0:T(128)} %pad_add_fusion.refs_1_, s32[16]{0:T(128)} %iota_add_fusion.refs_2_, bf16[16,128,256]{2,1,0:T(8,128)(2,1)} %copy-done, bf16[16,128,256]{2,1,0:T(8,128)(2,1)} %copy-done.1, bf16[32,64,128]{2,1,0:T(8,128)(2,1)S(1)} %all-to-all-done.1.refs_5_), custom_call_target="tpu_custom_call" | custom-call | tf_op jit(solution)/shard_map/ladder/pallas_call | solution.py:100
  (9 shorter events, 0.1 us)
Async XLA Ops:
  0.0 7.6 %collective-permute-start = (bf16[128,256]{1,0:T(8,128)(2,1)}, bf16[128,256]{1,0:T(8,128)(2,1)S(1)}, u32[]{:S(2)}, u32[]{:S(2)}) collective-permute-start(bf16[128,256]{1,0:T(8,128)(2,1)} %param.5), channel_id=1, source_target_pairs={{0,512},{512,0},{1,513},{513,1},{2,514},{514,2},{3,515},{515,3},{4... | collective-permute-start | bytes 196616 | tf_op jit(solution)/shard_map/ppermute | solution.py:117
  8.5 35.3 %collective-permute-start.2 = (bf16[2,128,256]{2,1,0:T(8,128)(2,1)S(1)}, bf16[2,128,256]{2,1,0:T(8,128)(2,1)S(1)}, u32[]{:S(2)}, u32[]{:S(2)}) collective-permute-start(bf16[2,128,256]{2,1,0:T(8,128)(2,1)S(1)} %pad_maximum_fusion.2), channel_id=1, source_target_pairs={{0,448},{64,0},{128,64},{192,128},{256,192},{320,256},{384,320},{4... | collective-permute-start | bytes 393224 | tf_op jit(solution)/shard_map/ppermute | solution.py:117
  10.9 32.8 %collective-permute-start.1 = (bf16[2,128,256]{2,1,0:T(8,128)(2,1)S(1)}, bf16[2,128,256]{2,1,0:T(8,128)(2,1)S(1)}, u32[]{:S(2)}, u32[]{:S(2)}) collective-permute-start(bf16[2,128,256]{2,1,0:T(8,128)(2,1)S(1)} %pad_maximum_fusion.2), channel_id=1, source_target_pairs={{0,64},{64,128},{128,192},{192,256},{256,320},{320,384},{384,448},... | collective-permute-start | bytes 393224 | tf_op jit(solution)/shard_map/ppermute | solution.py:117
  16.0 27.7 %copy-start.2 = (bf16[128,256]{1,0:T(8,128)(2,1)S(1)}, bf16[128,256]{1,0:T(8,128)(2,1)}, u32[]{:S(2)}) copy-start(bf16[128,256]{1,0:T(8,128)(2,1)} %param.5) | copy-start | bytes 196612
  16.0 48.3 %all-to-all-start = ((bf16[32,32,128]{2,1,0:T(8,128)(2,1)}), bf16[32,32,128]{2,1,0:T(8,128)(2,1)S(1)}, u32[]{:S(2)}, u32[]{:S(2)}) async-start(bf16[32,32,128]{2,1,0:T(8,128)(2,1)} %bitcast.6), calls=%async_computation | async-start | bytes 524288 | tf_op jit(solution)/shard_map/all_to_all | solution.py:124
  37.2 13.4 %collective-permute-start.3 = (bf16[2,128,256]{2,1,0:T(8,128)(2,1)S(1)}, bf16[2,128,256]{2,1,0:T(8,128)(2,1)S(1)}, u32[]{:S(2)}, u32[]{:S(2)}) collective-permute-start(bf16[2,128,256]{2,1,0:T(8,128)(2,1)S(1)} %pad_maximum_fusion.2), channel_id=1, source_target_pairs={{0,256},{64,320},{128,384},{192,448},{256,0},{320,64},{384,128},{4... | collective-permute-start | bytes 393224 | tf_op jit(solution)/shard_map/ppermute | solution.py:117
  43.8 18.5 %collective-permute-start.5 = (bf16[4,128,256]{2,1,0:T(8,128)(2,1)S(1)}, bf16[4,128,256]{2,1,0:T(8,128)(2,1)S(1)}, u32[]{:S(2)}, u32[]{:S(2)}) collective-permute-start(bf16[4,128,256]{2,1,0:T(8,128)(2,1)S(1)} %get-tuple-element.5), channel_id=1, source_target_pairs={{0,384},{64,448},{128,0},{192,64},{256,128},{320,192},{384,256},{4... | collective-permute-start | bytes 786440 | tf_op jit(solution)/shard_map/ppermute | solution.py:117
  48.4 14.0 %collective-permute-start.4 = (bf16[4,128,256]{2,1,0:T(8,128)(2,1)S(1)}, bf16[4,128,256]{2,1,0:T(8,128)(2,1)S(1)}, u32[]{:S(2)}, u32[]{:S(2)}) collective-permute-start(bf16[4,128,256]{2,1,0:T(8,128)(2,1)S(1)} %get-tuple-element.6), channel_id=1, source_target_pairs={{0,128},{64,192},{128,256},{192,320},{256,384},{320,448},{384,0},{... | collective-permute-start | bytes 786440 | tf_op jit(solution)/shard_map/ppermute | solution.py:117
  62.4 36.6 %copy-start = (bf16[16,128,256]{2,1,0:T(8,128)(2,1)}, bf16[16,128,256]{2,1,0:T(8,128)(2,1)S(1)}, u32[]{:S(2)}) copy-start(bf16[16,128,256]{2,1,0:T(8,128)(2,1)S(1)} %constant_dynamic-update-slice_fusion.refs_3_) | copy-start | bytes 3145732
  62.4 17.5 %collective-permute-start.6 = (bf16[16,128,256]{2,1,0:T(8,128)(2,1)S(1)}, bf16[16,128,256]{2,1,0:T(8,128)(2,1)S(1)}, u32[]{:S(2)}, u32[]{:S(2)}) collective-permute-start(bf16[16,128,256]{2,1,0:T(8,128)(2,1)S(1)} %constant_dynamic-update-slice_fusion.refs_3_), channel_id=1, source_target_pairs={{0,32},{32,0},{1,33},{33,1},{2,34},{34,2},{3,35},{35,3},{4,36},{36... | collective-permute-start | bytes 3145736 | tf_op jit(solution)/shard_map/ppermute | solution.py:117
  65.9 33.0 %all-to-all-start.1 = ((bf16[32,64,128]{2,1,0:T(8,128)(2,1)}), bf16[32,64,128]{2,1,0:T(8,128)(2,1)S(1)}, u32[]{:S(2)}, u32[]{:S(2)}) async-start(bf16[32,64,128]{2,1,0:T(8,128)(2,1)} %shard_map.55), calls=%async_computation.1 | async-start | bytes 1048576 | tf_op jit(solution)/shard_map/all_to_all | solution.py:133
  78.7 0.7 copy-start.3
  79.9 19.1 %copy-start.1 = (bf16[16,128,256]{2,1,0:T(8,128)(2,1)}, bf16[16,128,256]{2,1,0:T(8,128)(2,1)S(1)}, u32[]{:S(2)}) copy-start(bf16[16,128,256]{2,1,0:T(8,128)(2,1)S(1)} %collective-permute-done.6.refs_4_) | copy-start | bytes 3145732

commit v4 on v3

--- a/solution.py
+++ b/solution.py
@@ -13,9 +13,15 @@
 IRREPS = 8
 
 
-def order_kernel(blocks_ref, panel_ref, out_ref):
-    for slot in range(panel_ref.shape[0]):
-        out_ref[blocks_ref[slot]] = panel_ref[slot]
+def order_kernel(blocks_ref, panel_ref, out_ref, sems):
+    copies = [
+        pltpu.make_async_copy(panel_ref.at[slot], out_ref.at[blocks_ref[slot]], sems.at[slot])
+        for slot in range(panel_ref.shape[0])
+    ]
+    for copy in copies:
+        copy.start()
+    for copy in copies:
+        copy.wait()
 
 
 def irrep_order(panel, blocks):
@@ -24,9 +30,10 @@
         out_shape=pltpu.VMEM(panel.shape, panel.dtype),
         in_specs=[
             pl.BlockSpec(memory_space=pltpu.SMEM),
-            pl.BlockSpec(memory_space=pltpu.VMEM),
+            pl.BlockSpec(memory_space=pltpu.HBM),
         ],
         out_specs=pl.BlockSpec(memory_space=pltpu.VMEM),
+        scratch_shapes=[pltpu.SemaphoreType.DMA((panel.shape[0],))],
         name="irrep_order",
     )(blocks, panel)
 
@@ -52,13 +59,13 @@
     )(owners, pltpu.with_memory_space_constraint(pieces, pltpu.VMEM))
 
 
-TILES = tuple((x, zl) for x in (-1, 0, 1, 4, -3, -2, 2, 3) for zl in (0, 1))
+HERE, OPPOSITE, MINE, THEIRS = (0,), (4,), (1, 3, 2), (-1, -3, -2)
 
 
 def ladder_kernel(groups, piece_ref, here_ref, side_ref, *refs):
-    held_refs, refs = refs[:len(groups)], refs[len(groups):]
-    weight_ref, out_ref, done_ref, sems, in_sems = refs[:5]
-    tiles_refs = refs[5:]
+    held_refs, refs = refs[:len(groups) - 1], refs[len(groups) - 1:]
+    last_ref, weight_ref, out_ref, done_ref, sems, in_sems = refs[:6]
+    tiles_refs = refs[6:]
     quarters = weight_ref.shape[0] // IRREPS
     copies = []
     arrivals = [
@@ -67,12 +74,13 @@
     ]
     for arrival in arrivals:
         arrival.start()
-    for (core_step, places), tiles_ref, arrival in zip(groups, tiles_refs, arrivals):
-        arrival.wait()
-        for index, (x_step, zl_step) in enumerate(places):
-            zl = lax.rem(here_ref[0] + zl_step, 2)
-            x = lax.rem(here_ref[1] + x_step + N_X, N_X)
-            core = lax.rem(side_ref[0] + core_step, 2)
+    side = 2 * side_ref[0] - 1
+    for group, (steps, tiles_ref) in enumerate(zip(groups, (*tiles_refs, last_ref))):
+        if group < len(arrivals):
+            arrivals[group].wait()
+        for index in range(tiles_ref.shape[0]):
+            core, zl = index % 4 // 2, index % 2
+            x = lax.rem(here_ref[0] + steps[index // 4] * side + N_X, N_X)
             tile = (zl * N_X + x) * 2 + core
             weights = weight_ref[pl.ds(piece_ref[tile], quarters)]
             rows = weights.shape[1] // 2
@@ -95,12 +103,13 @@
     cols = weights.shape[2]
     count = sum(array.shape[0] for array in arrays)
     vmem, smem = pl.BlockSpec(memory_space=pltpu.VMEM), pl.BlockSpec(memory_space=pltpu.SMEM)
+    *arrays, last = arrays
     operands = [pltpu.with_memory_space_constraint(array, pltpu.HBM) for array in arrays]
-    operands.append(pltpu.with_memory_space_constraint(weights, pltpu.VMEM))
+    operands += [pltpu.with_memory_space_constraint(array, pltpu.VMEM) for array in (last, weights)]
     out = pl.pallas_call(
         lambda *refs: ladder_kernel(groups, *refs),
         out_shape=jax.ShapeDtypeStruct((count, rows, cols), jnp.bfloat16),
-        in_specs=[smem, smem, smem] + [pl.BlockSpec(memory_space=pltpu.HBM)] * len(arrays) + [vmem],
+        in_specs=[smem, smem, smem] + [pl.BlockSpec(memory_space=pltpu.HBM)] * len(arrays) + [vmem] * 2,
         out_specs=pl.BlockSpec(memory_space=pl.ANY),
         scratch_shapes=[
             pltpu.VMEM((count, rows, cols), jnp.bfloat16),
@@ -113,30 +122,33 @@
     return out.reshape(count * rows, cols)
 
 
-def shift(array, axis, size, step):
-    return lax.ppermute(array, axis, [(index, (index + step) % size) for index in range(size)])
+def away(array, step):
+    pairs = []
+    for x in range(N_X):
+        pairs.append((2 * x, 2 * ((x + step) % N_X)))
+        pairs.append((2 * x + 1, 2 * ((x - step) % N_X) + 1))
+    return lax.ppermute(array, ("x", "core"), pairs)
 
 
 def per_device(amplitudes, pair_irrep, integrals, panel_blocks, panel_owner):
     cols = integrals.shape[-1]
-    partner = shift(amplitudes, "zl", 2, 1)
     ordered = irrep_order(integrals[0], panel_blocks[0])
     pieces = lax.all_to_all(ordered.reshape(N_VIR, -1, cols), VIR, 0, 0, tiled=True)
-    pair = jnp.stack([amplitudes, partner])
-    left = shift(pair, "x", N_X, 1)
-    right = shift(pair, "x", N_X, -1)
-    opposite = shift(pair, "x", N_X, 4)
-    here = jnp.stack([lax.axis_index("zl"), lax.axis_index("x")])
+    pair = lax.all_gather(amplitudes[None], "zl", axis=0, tiled=True)
+    chip = lax.all_gather(pair, "core", axis=0, tiled=True)
+    beside = away(chip, 1)
+    here = jnp.stack([lax.axis_index("x"), lax.axis_index("zl")])
     copies = pick_and_copy(pieces, panel_owner)
-    up = shift(jnp.concatenate([left, pair]), "x", N_X, 2)
-    down = shift(jnp.concatenate([pair, right]), "x", N_X, -2)
+    wide = away(jnp.concatenate([beside, chip]), 2)
     weights = lax.all_to_all(copies, VIR, 0, 0, tiled=True)
     side = jnp.arange(16, dtype=jnp.int32) + lax.axis_index("core")
-    mine = jnp.concatenate([left, pair, right, opposite, up, down])
-    theirs = shift(mine, "core", 2, 1)
+    opposite = away(wide[:4], 1)
+    mine = jnp.concatenate([beside, wide])
+    theirs = lax.ppermute(mine, "core", [(0, 1), (1, 0)])
     first_piece = pair_irrep * (N_VIR // IRREPS)
-    groups = ((0, TILES), (1, TILES))
-    return contract(groups, (mine, theirs), first_piece, here, side, weights)
+    groups = (HERE, MINE, OPPOSITE, THEIRS)
+    arrays = (chip, mine, opposite, theirs)
+    return contract(groups, arrays, first_piece, here, side, weights)
 
 
 def solution(mesh):

time: 103 us -> 81.5 us (0.79)
  the two profiles are of different devices: /device:TPU:18 before, /device:TPU:16 now
where the time goes in v4:
time: 81.5 us; the launch traced here: 81 us
  starting transfers between devices  37 us (45%)
  waiting for transfers between devices  26.1 us (32%)
  blocking collectives  8.43 us (10%)
  Pallas kernels  7.52 us (9%)
  other arithmetic  1.75 us (2%)
    all_to_all x1, starting transfers between devices, per_device(): lax.all_to_all(ordered.reshape(N_VIR, -1, cols), VIR, 0, 0, tiled=True)  21.1 us
    all_to_all x1, waiting for transfers between devices, per_device(): lax.all_to_all(ordered.reshape(N_VIR, -1, cols), VIR, 0, 0, tiled=True)  11.6 us
    ppermute x3, starting transfers between devices, away(): return lax.ppermute(array, ('x', 'core'), pairs)  9.64 us
    all_to_all x1, waiting for transfers between devices, per_device(): weights = lax.all_to_all(copies, VIR, 0, 0, tiled=True)  8.11 us
    all_gather x1, blocking collectives, per_device(): pair = lax.all_gather(amplitudes[None], 'zl', axis=0, tiled=True)  6.44 us
    ppermute x3, waiting for transfers between devices, away(): return lax.ppermute(array, ('x', 'core'), pairs)  6.37 us
    all_to_all x1, starting transfers between devices, per_device(): weights = lax.all_to_all(copies, VIR, 0, 0, tiled=True)  4.33 us
    pallas_call x1, Pallas kernels, contract(): pl.pallas_call(lambda *refs: ladder_kernel(groups, *refs), out_shape=jax....  3.63 us
  transfers between devices with their start and end apart: 6, of which 3 were waited for; matrix products, arithmetic and copies ran while one was open for 2% of the time, Pallas kernels for 5%

profile of v4, /device:TPU:16, one launch (start us, length us, event | category | flops | bytes accessed | tf_op | source)
XLA Modules:
  0.0 81.0 jit_solution(4446196715262862019)
XLA Ops:
  0.0 6.4 %all-gather = bf16[256,256]{1,0:T(8,128)(2,1)S(1)} all-gather(bf16[128,256]{1,0:T(8,128)(2,1)} %param.5), channel_id=2, replica_groups=mesh['zl'=2,'x'=8,'core'=2,'zh'=4,'y'=8] {'zl'}, dimensions={0}, use_global_device_ids=true | all-gather | bytes 196608 | tf_op jit(solution)/shard_map/all_gather | solution.py:137
  6.4 2.0 %all_gather.7.refs_3_ = bf16[4,128,256]{2,1,0:T(8,128)(2,1)S(1)} all-gather(bf16[2,128,256]{2,1,0:T(8,128)(2,1)S(1)} %bitcast.7), channel_id=1, replica_groups=mesh['zl'=2,'x'=8,'core'=2,'zh'=4,'y'=8] {'core'}, dimensions={0}, use_global_device_ids=true | all-gather | bytes 393216 | tf_op jit(solution)/shard_map/all_gather | solution.py:138
  8.4 0.0 copy-start
  8.4 3.4 %collective-permute-start = (bf16[4,128,256]{2,1,0:T(8,128)(2,1)S(1)}, bf16[4,128,256]{2,1,0:T(8,128)(2,1)S(1)}, u32[]{:S(2)}, u32[]{:S(2)}) collective-permute-start(bf16[4,128,256]{2,1,0:T(8,128)(2,1)S(1)} %all_gather.7.refs_3_), channel_id=1, source_target_pairs={{0,64},{32,480},{64,128},{96,32},{128,192},{160,96},{192,256},{224... | collective-permute-start | bytes 786440 | tf_op jit(solution)/shard_map/ppermute | solution.py:130
  11.8 2.3 %irrep_order.1 = bf16[8,128,128]{2,1,0:T(8,128)(2,1)} custom-call(s32[8]{0:T(128)} %bitcast.9, bf16[8,128,128]{2,1,0:T(8,128)(2,1)} %bitcast.8), custom_call_target="tpu_custom_call" | custom-call | tf_op jit(solution)/shard_map/irrep_order/pallas_call | solution.py:28
  14.1 21.1 %all-to-all-start = ((bf16[32,32,128]{2,1,0:T(8,128)(2,1)}), bf16[32,32,128]{2,1,0:T(8,128)(2,1)S(1)}, u32[]{:S(2)}, u32[]{:S(2)}) async-start(bf16[32,32,128]{2,1,0:T(8,128)(2,1)} %bitcast.5), calls=%async_computation | async-start | bytes 524288 | tf_op jit(solution)/shard_map/all_to_all | solution.py:136
  35.2 0.0 collective-permute-done
  35.2 0.0 copy-done
  35.3 4.3 %collective-permute-start.1 = (bf16[8,128,256]{2,1,0:T(8,128)(2,1)S(1)}, bf16[8,128,256]{2,1,0:T(8,128)(2,1)S(1)}, u32[]{:S(2)}, u32[]{:S(2)}) collective-permute-start(bf16[8,128,256]{2,1,0:T(8,128)(2,1)S(1)} %pad_maximum_fusion), channel_id=1, source_target_pairs={{0,128},{32,416},{64,192},{96,480},{128,256},{160,32},{192,320},{2... | collective-permute-start | bytes 1572872 | tf_op jit(solution)/shard_map/ppermute | solution.py:130
  39.6 11.6 %all-to-all-done.pieces_ref = bf16[32,32,128]{2,1,0:T(8,128)(2,1)S(1)} async-done(((bf16[32,32,128]{2,1,0:T(8,128)(2,1)}), bf16[32,32,128]{2,1,0:T(8,128)(2,1)S(1)}, u32[]{:S(2)}, u32[]{:S(2)}) %all-to-all-start) | async-done | bytes 262176 | tf_op jit(solution)/shard_map/all_to_all | solution.py:136
  51.3 1.6 %shard_map.55 = bf16[32,64,128]{2,1,0:T(8,128)(2,1)} custom-call(s32[2]{0:T(128)} %owner_ref.1, bf16[32,32,128]{2,1,0:T(8,128)(2,1)S(1)} %all-to-all-done.pieces_ref), custom_call_target="tpu_custom_call" | custom-call | tf_op jit(solution)/shard_map/pallas_call | solution.py:51
  52.9 4.3 %all-to-all-start.1 = ((bf16[32,64,128]{2,1,0:T(8,128)(2,1)}), bf16[32,64,128]{2,1,0:T(8,128)(2,1)S(1)}, u32[]{:S(2)}, u32[]{:S(2)}) async-start(bf16[32,64,128]{2,1,0:T(8,128)(2,1)} %shard_map.55), calls=%async_computation.1 | async-start | bytes 1048576 | tf_op jit(solution)/shard_map/all_to_all | solution.py:143
  57.2 0.0 collective-permute-done.1
  57.3 0.0 copy-start.1
  57.3 1.9 %collective-permute-start.3 = (bf16[12,128,256]{2,1,0:T(8,128)(2,1)S(1)}, bf16[12,128,256]{2,1,0:T(8,128)(2,1)S(1)}, u32[]{:S(2)}, u32[]{:S(2)}) collective-permute-start(bf16[12,128,256]{2,1,0:T(8,128)(2,1)S(1)} %constant_dynamic-update-slice_fusion.refs_4_), channel_id=1, source_target_pairs={{0,32},{32,0},{1,33},{33,1},{2,34},{34,2},{3,35},{35,3},{4,36},{36... | collective-permute-start | bytes 2359304 | tf_op jit(solution)/shard_map/ppermute | solution.py:147
  59.2 0.5 iota_add_fusion.refs_2_
  59.8 1.9 %collective-permute-start.2 = (bf16[4,128,256]{2,1,0:T(8,128)(2,1)S(1)}, bf16[4,128,256]{2,1,0:T(8,128)(2,1)S(1)}, u32[]{:S(2)}, u32[]{:S(2)}) collective-permute-start(bf16[4,128,256]{2,1,0:T(8,128)(2,1)S(1)} %slice.4), channel_id=1, source_target_pairs={{0,64},{32,480},{64,128},{96,32},{128,192},{160,96},{192,256},{224... | collective-permute-start | bytes 786440 | tf_op jit(solution)/shard_map/ppermute | solution.py:130
  61.7 0.0 copy-start.3
  61.7 0.7 pad_add_fusion.refs_1_
  62.4 0.0 copy-done.3
  62.4 0.5 broadcast_multiply_fusion.refs_0_
  62.9 6.4 %collective-permute-done.2.refs_5_ = bf16[4,128,256]{2,1,0:T(8,128)(2,1)S(1)} collective-permute-done((bf16[4,128,256]{2,1,0:T(8,128)(2,1)S(1)}, bf16[4,128,256]{2,1,0:T(8,128)(2,1)S(1)}, u32[]{:S(2)}, u32[]{:S(2)}) %collective-permute-start.2) | collective-permute-done | bytes 262176 | tf_op jit(solution)/shard_map/ppermute | solution.py:130
  69.3 0.0 copy-start.2
  69.3 8.1 %all-to-all-done.1.refs_7_ = bf16[32,64,128]{2,1,0:T(8,128)(2,1)S(1)} async-done(((bf16[32,64,128]{2,1,0:T(8,128)(2,1)}), bf16[32,64,128]{2,1,0:T(8,128)(2,1)S(1)}, u32[]{:S(2)}, u32[]{:S(2)}) %all-to-all-start.1) | async-done | bytes 524320 | tf_op jit(solution)/shard_map/all_to_all | solution.py:143
  77.4 0.0 collective-permute-done.3.refs_6_
  77.4 0.0 copy-done.1
  77.4 0.0 copy-done.2
  77.4 3.6 %ladder.1 = bf16[32,128,128]{2,1,0:T(8,128)(2,1)} custom-call(s32[32]{0:T(128)} %broadcast_multiply_fusion.refs_0_, s32[2]{0:T(128)} %pad_add_fusion.refs_1_, s32[16]{0:T(128)} %iota_add_fusion.refs_2_, bf16[4,128,256]{2,1,0:T(8,128)(2,1)} %copy-done, bf16[12,128,256]{2,1,0:T(8,128)(2,1)} %copy-done.1, bf16[4,128,256]{2,1,0:T(8,128)(2,1)} %copy-done.2, ...), custom_call_target="tpu_custom_call" | custom-call | tf_op jit(solution)/shard_map/ladder/pallas_call | solution.py:109
  (4 shorter events, 0.1 us)
Async XLA Ops:
  8.4 26.8 %copy-start = (bf16[4,128,256]{2,1,0:T(8,128)(2,1)}, bf16[4,128,256]{2,1,0:T(8,128)(2,1)S(1)}, u32[]{:S(2)}) copy-start(bf16[4,128,256]{2,1,0:T(8,128)(2,1)S(1)} %all_gather.7.refs_3_) | copy-start | bytes 786436
  8.4 26.8 %collective-permute-start = (bf16[4,128,256]{2,1,0:T(8,128)(2,1)S(1)}, bf16[4,128,256]{2,1,0:T(8,128)(2,1)S(1)}, u32[]{:S(2)}, u32[]{:S(2)}) collective-permute-start(bf16[4,128,256]{2,1,0:T(8,128)(2,1)S(1)} %all_gather.7.refs_3_), channel_id=1, source_target_pairs={{0,64},{32,480},{64,128},{96,32},{128,192},{160,96},{192,256},{224... | collective-permute-start | bytes 786440 | tf_op jit(solution)/shard_map/ppermute | solution.py:130
  14.1 37.1 %all-to-all-start = ((bf16[32,32,128]{2,1,0:T(8,128)(2,1)}), bf16[32,32,128]{2,1,0:T(8,128)(2,1)S(1)}, u32[]{:S(2)}, u32[]{:S(2)}) async-start(bf16[32,32,128]{2,1,0:T(8,128)(2,1)} %bitcast.5), calls=%async_computation | async-start | bytes 524288 | tf_op jit(solution)/shard_map/all_to_all | solution.py:136
  35.3 21.9 %collective-permute-start.1 = (bf16[8,128,256]{2,1,0:T(8,128)(2,1)S(1)}, bf16[8,128,256]{2,1,0:T(8,128)(2,1)S(1)}, u32[]{:S(2)}, u32[]{:S(2)}) collective-permute-start(bf16[8,128,256]{2,1,0:T(8,128)(2,1)S(1)} %pad_maximum_fusion), channel_id=1, source_target_pairs={{0,128},{32,416},{64,192},{96,480},{128,256},{160,32},{192,320},{2... | collective-permute-start | bytes 1572872 | tf_op jit(solution)/shard_map/ppermute | solution.py:130
  52.9 24.5 %all-to-all-start.1 = ((bf16[32,64,128]{2,1,0:T(8,128)(2,1)}), bf16[32,64,128]{2,1,0:T(8,128)(2,1)S(1)}, u32[]{:S(2)}, u32[]{:S(2)}) async-start(bf16[32,64,128]{2,1,0:T(8,128)(2,1)} %shard_map.55), calls=%async_computation.1 | async-start | bytes 1048576 | tf_op jit(solution)/shard_map/all_to_all | solution.py:143
  57.3 20.1 %copy-start.1 = (bf16[12,128,256]{2,1,0:T(8,128)(2,1)}, bf16[12,128,256]{2,1,0:T(8,128)(2,1)S(1)}, u32[]{:S(2)}) copy-start(bf16[12,128,256]{2,1,0:T(8,128)(2,1)S(1)} %constant_dynamic-update-slice_fusion.refs_4_) | copy-start | bytes 2359300
  57.3 20.1 %collective-permute-start.3 = (bf16[12,128,256]{2,1,0:T(8,128)(2,1)S(1)}, bf16[12,128,256]{2,1,0:T(8,128)(2,1)S(1)}, u32[]{:S(2)}, u32[]{:S(2)}) collective-permute-start(bf16[12,128,256]{2,1,0:T(8,128)(2,1)S(1)} %constant_dynamic-update-slice_fusion.refs_4_), channel_id=1, source_target_pairs={{0,32},{32,0},{1,33},{33,1},{2,34},{34,2},{3,35},{35,3},{4,36},{36... | collective-permute-start | bytes 2359304 | tf_op jit(solution)/shard_map/ppermute | solution.py:147
  59.8 9.5 %collective-permute-start.2 = (bf16[4,128,256]{2,1,0:T(8,128)(2,1)S(1)}, bf16[4,128,256]{2,1,0:T(8,128)(2,1)S(1)}, u32[]{:S(2)}, u32[]{:S(2)}) collective-permute-start(bf16[4,128,256]{2,1,0:T(8,128)(2,1)S(1)} %slice.4), channel_id=1, source_target_pairs={{0,64},{32,480},{64,128},{96,32},{128,192},{160,96},{192,256},{224... | collective-permute-start | bytes 786440 | tf_op jit(solution)/shard_map/ppermute | solution.py:130
  61.7 0.7 copy-start.3
  69.3 8.1 %copy-start.2 = (bf16[4,128,256]{2,1,0:T(8,128)(2,1)}, bf16[4,128,256]{2,1,0:T(8,128)(2,1)S(1)}, u32[]{:S(2)}) copy-start(bf16[4,128,256]{2,1,0:T(8,128)(2,1)S(1)} %collective-permute-done.2.refs_5_) | copy-start | bytes 786436

commit v5 on v4

--- a/solution.py
+++ b/solution.py
@@ -13,15 +13,9 @@
 IRREPS = 8
 
 
-def order_kernel(blocks_ref, panel_ref, out_ref, sems):
-    copies = [
-        pltpu.make_async_copy(panel_ref.at[slot], out_ref.at[blocks_ref[slot]], sems.at[slot])
-        for slot in range(panel_ref.shape[0])
-    ]
-    for copy in copies:
-        copy.start()
-    for copy in copies:
-        copy.wait()
+def order_kernel(blocks_ref, panel_ref, out_ref):
+    for slot in range(panel_ref.shape[0]):
+        out_ref[blocks_ref[slot]] = panel_ref[slot]
 
 
 def irrep_order(panel, blocks):
@@ -30,10 +24,9 @@
         out_shape=pltpu.VMEM(panel.shape, panel.dtype),
         in_specs=[
             pl.BlockSpec(memory_space=pltpu.SMEM),
-            pl.BlockSpec(memory_space=pltpu.HBM),
+            pl.BlockSpec(memory_space=pltpu.VMEM),
         ],
         out_specs=pl.BlockSpec(memory_space=pltpu.VMEM),
-        scratch_shapes=[pltpu.SemaphoreType.DMA((panel.shape[0],))],
         name="irrep_order",
     )(blocks, panel)
 
@@ -59,10 +52,11 @@
     )(owners, pltpu.with_memory_space_constraint(pieces, pltpu.VMEM))
 
 
-HERE, OPPOSITE, MINE, THEIRS = (0,), (4,), (1, 3, 2), (-1, -3, -2)
+HERE, NEXT, WIDE, OPPOSITE = (0,), (1,), (3, 2), (4,)
+OTHER_NEXT, OTHER_WIDE = (-1,), (-3, -2)
 
 
-def ladder_kernel(groups, piece_ref, here_ref, side_ref, *refs):
+def ladder_kernel(groups, first_ref, second_ref, here_ref, side_ref, *refs):
     held_refs, refs = refs[:len(groups) - 1], refs[len(groups) - 1:]
     last_ref, weight_ref, out_ref, done_ref, sems, in_sems = refs[:6]
     tiles_refs = refs[6:]
@@ -80,9 +74,9 @@
             arrivals[group].wait()
         for index in range(tiles_ref.shape[0]):
             core, zl = index % 4 // 2, index % 2
-            x = lax.rem(here_ref[0] + steps[index // 4] * side + N_X, N_X)
+            x = lax.rem((second_ref if zl else here_ref)[0] + steps[index // 4] * side + N_X, N_X)
             tile = (zl * N_X + x) * 2 + core
-            weights = weight_ref[pl.ds(piece_ref[tile], quarters)]
+            weights = weight_ref[pl.ds(first_ref[tile], quarters)]
             rows = weights.shape[1] // 2
             weights = jnp.concatenate(
                 [weights[:, :rows].reshape(-1, weights.shape[2]),
@@ -98,7 +92,7 @@
         copy.wait()
 
 
-def contract(groups, arrays, first_piece, here, side, weights):
+def contract(groups, arrays, first_piece, second, here, side, weights):
     rows = arrays[0].shape[1]
     cols = weights.shape[2]
     count = sum(array.shape[0] for array in arrays)
@@ -109,7 +103,7 @@
     out = pl.pallas_call(
         lambda *refs: ladder_kernel(groups, *refs),
         out_shape=jax.ShapeDtypeStruct((count, rows, cols), jnp.bfloat16),
-        in_specs=[smem, smem, smem] + [pl.BlockSpec(memory_space=pltpu.HBM)] * len(arrays) + [vmem] * 2,
+        in_specs=[smem] * 4 + [pl.BlockSpec(memory_space=pltpu.HBM)] * len(arrays) + [vmem] * 2,
         out_specs=pl.BlockSpec(memory_space=pl.ANY),
         scratch_shapes=[
             pltpu.VMEM((count, rows, cols), jnp.bfloat16),
@@ -118,7 +112,7 @@
             *(pltpu.VMEM(array.shape, array.dtype) for array in arrays),
         ],
         name="ladder",
-    )(first_piece, here, side, *operands)
+    )(first_piece, second, here, side, *operands)
     return out.reshape(count * rows, cols)
 
 
@@ -139,16 +133,17 @@
     beside = away(chip, 1)
     here = jnp.stack([lax.axis_index("x"), lax.axis_index("zl")])
     copies = pick_and_copy(pieces, panel_owner)
-    wide = away(jnp.concatenate([beside, chip]), 2)
     weights = lax.all_to_all(copies, VIR, 0, 0, tiled=True)
     side = jnp.arange(16, dtype=jnp.int32) + lax.axis_index("core")
+    wide = away(jnp.concatenate([beside, chip]), 2)
+    other_beside = lax.ppermute(beside, "core", [(0, 1), (1, 0)])
+    second = jnp.arange(24, dtype=jnp.int32) + lax.axis_index("x")
     opposite = away(wide[:4], 1)
-    mine = jnp.concatenate([beside, wide])
-    theirs = lax.ppermute(mine, "core", [(0, 1), (1, 0)])
+    other_wide = lax.ppermute(wide, "core", [(0, 1), (1, 0)])
     first_piece = pair_irrep * (N_VIR // IRREPS)
-    groups = (HERE, MINE, OPPOSITE, THEIRS)
-    arrays = (chip, mine, opposite, theirs)
-    return contract(groups, arrays, first_piece, here, side, weights)
+    groups = (HERE, NEXT, OTHER_NEXT, WIDE, OPPOSITE, OTHER_WIDE)
+    arrays = (chip, beside, other_beside, wide, opposite, other_wide)
+    return contract(groups, arrays, first_piece, second, here, side, weights)
 
 
 def solution(mesh):

time: 81.5 us -> 86.7 us (1.064)
  the two profiles are of different devices: /device:TPU:16 before, /device:TPU:18 now
where the time goes in v5:
time: 86.7 us; the launch traced here: 86.1 us
  starting transfers between devices  53.9 us (62%)
  waiting for transfers between devices  13 us (15%)
  blocking collectives  9.48 us (11%)
  Pallas kernels  7.2 us (8%)
  other arithmetic  2.39 us (3%)
    all_to_all x1, starting transfers between devices, per_device(): lax.all_to_all(ordered.reshape(N_VIR, -1, cols), VIR, 0, 0, tiled=True)  22.1 us
    all_to_all x1, starting transfers between devices, per_device(): weights = lax.all_to_all(copies, VIR, 0, 0, tiled=True)  14 us
    ppermute x3, starting transfers between devices, away(): return lax.ppermute(array, ('x', 'core'), pairs)  13.5 us
    all_gather x1, blocking collectives, per_device(): pair = lax.all_gather(amplitudes[None], 'zl', axis=0, tiled=True)  7.5 us
    ppermute x3, waiting for transfers between devices, away(): return lax.ppermute(array, ('x', 'core'), pairs)  7.48 us
    all_to_all x1, waiting for transfers between devices, per_device(): weights = lax.all_to_all(copies, VIR, 0, 0, tiled=True)  5.51 us
    pallas_call x1, Pallas kernels, contract(): pl.pallas_call(lambda *refs: ladder_kernel(groups, *refs), out_shape=jax....  3.94 us
    ppermute x1, starting transfers between devices, per_device(): other_beside = lax.ppermute(beside, 'core', [(0, 1), (1, 0)])  2.39 us
  transfers between devices with their start and end apart: 7, of which 3 were waited for; matrix products, arithmetic and copies ran while one was open for 3% of the time, Pallas kernels for 2%

profile of v5, /device:TPU:18, one launch (start us, length us, event | category | flops | bytes accessed | tf_op | source)
XLA Modules:
  0.0 86.1 jit_solution(14696014826379096747)
XLA Ops:
  0.0 1.7 %irrep_order.1 = bf16[8,128,128]{2,1,0:T(8,128)(2,1)} custom-call(s32[8]{0:T(128)} %bitcast.9, bf16[8,128,128]{2,1,0:T(8,128)(2,1)} %bitcast.8), custom_call_target="tpu_custom_call" | custom-call | tf_op jit(solution)/shard_map/irrep_order/pallas_call | solution.py:22
  1.7 22.1 %all-to-all-start = ((bf16[32,32,128]{2,1,0:T(8,128)(2,1)}), bf16[32,32,128]{2,1,0:T(8,128)(2,1)S(1)}, u32[]{:S(2)}, u32[]{:S(2)}) async-start(bf16[32,32,128]{2,1,0:T(8,128)(2,1)} %bitcast.5), calls=%async_computation | async-start | bytes 524288 | tf_op jit(solution)/shard_map/all_to_all | solution.py:130
  23.8 0.0 copy-done.5
  23.8 7.5 %all-gather = bf16[256,256]{1,0:T(8,128)(2,1)S(1)} all-gather(bf16[128,256]{1,0:T(8,128)(2,1)S(1)} %copy-done.5), channel_id=2, replica_groups=mesh['zl'=2,'x'=8,'core'=2,'zh'=4,'y'=8] {'zl'}, dimensions={0}, use_global_device_ids=true | all-gather | bytes 196608 | tf_op jit(solution)/shard_map/all_gather | solution.py:131
  31.3 2.0 %all_gather.7.refs_4_ = bf16[4,128,256]{2,1,0:T(8,128)(2,1)S(1)} all-gather(bf16[2,128,256]{2,1,0:T(8,128)(2,1)S(1)} %bitcast.7), channel_id=1, replica_groups=mesh['zl'=2,'x'=8,'core'=2,'zh'=4,'y'=8] {'core'}, dimensions={0}, use_global_device_ids=true | all-gather | bytes 393216 | tf_op jit(solution)/shard_map/all_gather | solution.py:132
  33.3 3.4 %collective-permute-start = (bf16[4,128,256]{2,1,0:T(8,128)(2,1)S(1)}, bf16[4,128,256]{2,1,0:T(8,128)(2,1)S(1)}, u32[]{:S(2)}, u32[]{:S(2)}) collective-permute-start(bf16[4,128,256]{2,1,0:T(8,128)(2,1)S(1)} %all_gather.7.refs_4_), channel_id=1, source_target_pairs={{0,64},{32,480},{64,128},{96,32},{128,192},{160,96},{192,256},{224... | collective-permute-start | bytes 786440 | tf_op jit(solution)/shard_map/ppermute | solution.py:124
  36.7 4.9 %collective-permute-done.refs_5_ = bf16[4,128,256]{2,1,0:T(8,128)(2,1)S(1)} collective-permute-done((bf16[4,128,256]{2,1,0:T(8,128)(2,1)S(1)}, bf16[4,128,256]{2,1,0:T(8,128)(2,1)S(1)}, u32[]{:S(2)}, u32[]{:S(2)}) %collective-permute-start) | collective-permute-done | bytes 262176 | tf_op jit(solution)/shard_map/ppermute | solution.py:124
  41.6 0.0 copy-done
  41.6 4.5 %collective-permute-start.2 = (bf16[8,128,256]{2,1,0:T(8,128)(2,1)S(1)}, bf16[8,128,256]{2,1,0:T(8,128)(2,1)S(1)}, u32[]{:S(2)}, u32[]{:S(2)}) collective-permute-start(bf16[8,128,256]{2,1,0:T(8,128)(2,1)S(1)} %pad_maximum_fusion), channel_id=1, source_target_pairs={{0,128},{32,416},{64,192},{96,480},{128,256},{160,32},{192,320},{2... | collective-permute-start | bytes 1572872 | tf_op jit(solution)/shard_map/ppermute | solution.py:124
  46.2 0.0 all-to-all-done.pieces_ref
  46.2 1.6 %shard_map.55 = bf16[32,64,128]{2,1,0:T(8,128)(2,1)} custom-call(s32[2]{0:T(128)} %owner_ref.1, bf16[32,32,128]{2,1,0:T(8,128)(2,1)S(1)} %all-to-all-done.pieces_ref), custom_call_target="tpu_custom_call" | custom-call | tf_op jit(solution)/shard_map/pallas_call | solution.py:44
  47.7 14.0 %all-to-all-start.1 = ((bf16[32,64,128]{2,1,0:T(8,128)(2,1)}), bf16[32,64,128]{2,1,0:T(8,128)(2,1)S(1)}, u32[]{:S(2)}, u32[]{:S(2)}) async-start(bf16[32,64,128]{2,1,0:T(8,128)(2,1)} %shard_map.55), calls=%async_computation.1 | async-start | bytes 1048576 | tf_op jit(solution)/shard_map/all_to_all | solution.py:136
  61.7 0.0 collective-permute-done.2.refs_7_
  61.7 0.0 copy-start.1
  61.7 1.9 %collective-permute-start.4 = (bf16[8,128,256]{2,1,0:T(8,128)(2,1)S(1)}, bf16[8,128,256]{2,1,0:T(8,128)(2,1)S(1)}, u32[]{:S(2)}, u32[]{:S(2)}) collective-permute-start(bf16[8,128,256]{2,1,0:T(8,128)(2,1)S(1)} %collective-permute-done.2.refs_7_), channel_id=1, source_target_pairs={{0,32},{32,0},{1,33},{33,1},{2,34},{34,2},{3,35},{35,3},{4,36},{36... | collective-permute-start | bytes 1572872 | tf_op jit(solution)/shard_map/ppermute | solution.py:142
  63.7 0.6 iota_add_fusion.refs_3_
  64.3 0.5 iota_add_fusion.1.refs_1_
  64.8 0.0 copy-done.2
  64.8 2.4 %collective-permute-start.1 = (bf16[4,128,256]{2,1,0:T(8,128)(2,1)S(1)}, bf16[4,128,256]{2,1,0:T(8,128)(2,1)S(1)}, u32[]{:S(2)}, u32[]{:S(2)}) collective-permute-start(bf16[4,128,256]{2,1,0:T(8,128)(2,1)S(1)} %collective-permute-done.refs_5_), channel_id=1, source_target_pairs={{0,32},{32,0},{1,33},{33,1},{2,34},{34,2},{3,35},{35,3},{4,36},{36... | collective-permute-start | bytes 786440 | tf_op jit(solution)/shard_map/ppermute | solution.py:139
  67.2 5.6 %collective-permute-start.3 = (bf16[4,128,256]{2,1,0:T(8,128)(2,1)S(1)}, bf16[4,128,256]{2,1,0:T(8,128)(2,1)S(1)}, u32[]{:S(2)}, u32[]{:S(2)}) collective-permute-start(bf16[4,128,256]{2,1,0:T(8,128)(2,1)S(1)} %slice.4), channel_id=1, source_target_pairs={{0,64},{32,480},{64,128},{96,32},{128,192},{160,96},{192,256},{224... | collective-permute-start | bytes 786440 | tf_op jit(solution)/shard_map/ppermute | solution.py:124
  72.8 0.0 copy-start.6
  72.8 0.7 pad_add_fusion.refs_2_
  73.5 0.0 copy-done.6
  73.5 0.6 broadcast_multiply_fusion.refs_0_
  74.1 0.0 collective-permute-done.1.refs_6_
  74.1 2.6 %collective-permute-done.3.refs_8_ = bf16[4,128,256]{2,1,0:T(8,128)(2,1)S(1)} collective-permute-done((bf16[4,128,256]{2,1,0:T(8,128)(2,1)S(1)}, bf16[4,128,256]{2,1,0:T(8,128)(2,1)S(1)}, u32[]{:S(2)}, u32[]{:S(2)}) %collective-permute-start.3) | collective-permute-done | bytes 262176 | tf_op jit(solution)/shard_map/ppermute | solution.py:124
  76.7 0.0 collective-permute-done.4.refs_9_
  76.7 5.5 %all-to-all-done.1.refs_10_ = bf16[32,64,128]{2,1,0:T(8,128)(2,1)S(1)} async-done(((bf16[32,64,128]{2,1,0:T(8,128)(2,1)}), bf16[32,64,128]{2,1,0:T(8,128)(2,1)S(1)}, u32[]{:S(2)}, u32[]{:S(2)}) %all-to-all-start.1) | async-done | bytes 524320 | tf_op jit(solution)/shard_map/all_to_all | solution.py:136
  82.2 0.0 copy-done.1
  82.2 0.0 copy-done.3
  82.2 0.0 copy-done.4
  82.2 3.9 %ladder.1 = bf16[32,128,128]{2,1,0:T(8,128)(2,1)} custom-call(s32[32]{0:T(128)} %broadcast_multiply_fusion.refs_0_, s32[24]{0:T(128)} %iota_add_fusion.1.refs_1_, s32[2]{0:T(128)} %pad_add_fusion.refs_2_, s32[16]{0:T(128)} %iota_add_fusion.refs_3_, bf16[4,128,256]{2,1,0:T(8,128)(2,1)} %copy-done, bf16[4,128,256]{2,1,0:T(8,128)(2,1)} %copy-done.2, ...), custom_call_target="tpu_custom_call" | custom-call | tf_op jit(solution)/shard_map/ladder/pallas_call | solution.py:103
  (7 shorter events, 0.1 us)
Async XLA Ops:
  1.7 22.1 %copy-start.5 = (bf16[128,256]{1,0:T(8,128)(2,1)S(1)}, bf16[128,256]{1,0:T(8,128)(2,1)}, u32[]{:S(2)}) copy-start(bf16[128,256]{1,0:T(8,128)(2,1)} %param.5) | copy-start | bytes 196612
  1.7 44.5 %all-to-all-start = ((bf16[32,32,128]{2,1,0:T(8,128)(2,1)}), bf16[32,32,128]{2,1,0:T(8,128)(2,1)S(1)}, u32[]{:S(2)}, u32[]{:S(2)}) async-start(bf16[32,32,128]{2,1,0:T(8,128)(2,1)} %bitcast.5), calls=%async_computation | async-start | bytes 524288 | tf_op jit(solution)/shard_map/all_to_all | solution.py:130
  33.3 8.3 %copy-start = (bf16[4,128,256]{2,1,0:T(8,128)(2,1)}, bf16[4,128,256]{2,1,0:T(8,128)(2,1)S(1)}, u32[]{:S(2)}) copy-start(bf16[4,128,256]{2,1,0:T(8,128)(2,1)S(1)} %all_gather.7.refs_4_) | copy-start | bytes 786436
  33.3 8.3 %collective-permute-start = (bf16[4,128,256]{2,1,0:T(8,128)(2,1)S(1)}, bf16[4,128,256]{2,1,0:T(8,128)(2,1)S(1)}, u32[]{:S(2)}, u32[]{:S(2)}) collective-permute-start(bf16[4,128,256]{2,1,0:T(8,128)(2,1)S(1)} %all_gather.7.refs_4_), channel_id=1, source_target_pairs={{0,64},{32,480},{64,128},{96,32},{128,192},{160,96},{192,256},{224... | collective-permute-start | bytes 786440 | tf_op jit(solution)/shard_map/ppermute | solution.py:124
  41.5 23.2 %copy-start.2 = (bf16[4,128,256]{2,1,0:T(8,128)(2,1)}, bf16[4,128,256]{2,1,0:T(8,128)(2,1)S(1)}, u32[]{:S(2)}) copy-start(bf16[4,128,256]{2,1,0:T(8,128)(2,1)S(1)} %collective-permute-done.refs_5_) | copy-start | bytes 786436
  41.6 20.1 %collective-permute-start.2 = (bf16[8,128,256]{2,1,0:T(8,128)(2,1)S(1)}, bf16[8,128,256]{2,1,0:T(8,128)(2,1)S(1)}, u32[]{:S(2)}, u32[]{:S(2)}) collective-permute-start(bf16[8,128,256]{2,1,0:T(8,128)(2,1)S(1)} %pad_maximum_fusion), channel_id=1, source_target_pairs={{0,128},{32,416},{64,192},{96,480},{128,256},{160,32},{192,320},{2... | collective-permute-start | bytes 1572872 | tf_op jit(solution)/shard_map/ppermute | solution.py:124
  47.7 34.5 %all-to-all-start.1 = ((bf16[32,64,128]{2,1,0:T(8,128)(2,1)}), bf16[32,64,128]{2,1,0:T(8,128)(2,1)S(1)}, u32[]{:S(2)}, u32[]{:S(2)}) async-start(bf16[32,64,128]{2,1,0:T(8,128)(2,1)} %shard_map.55), calls=%async_computation.1 | async-start | bytes 1048576 | tf_op jit(solution)/shard_map/all_to_all | solution.py:136
  61.7 20.5 %copy-start.1 = (bf16[8,128,256]{2,1,0:T(8,128)(2,1)}, bf16[8,128,256]{2,1,0:T(8,128)(2,1)S(1)}, u32[]{:S(2)}) copy-start(bf16[8,128,256]{2,1,0:T(8,128)(2,1)S(1)} %collective-permute-done.2.refs_7_) | copy-start | bytes 1572868
  61.7 15.0 %collective-permute-start.4 = (bf16[8,128,256]{2,1,0:T(8,128)(2,1)S(1)}, bf16[8,128,256]{2,1,0:T(8,128)(2,1)S(1)}, u32[]{:S(2)}, u32[]{:S(2)}) collective-permute-start(bf16[8,128,256]{2,1,0:T(8,128)(2,1)S(1)} %collective-permute-done.2.refs_7_), channel_id=1, source_target_pairs={{0,32},{32,0},{1,33},{33,1},{2,34},{34,2},{3,35},{35,3},{4,36},{36... | collective-permute-start | bytes 1572872 | tf_op jit(solution)/shard_map/ppermute | solution.py:142
  64.8 9.3 %collective-permute-start.1 = (bf16[4,128,256]{2,1,0:T(8,128)(2,1)S(1)}, bf16[4,128,256]{2,1,0:T(8,128)(2,1)S(1)}, u32[]{:S(2)}, u32[]{:S(2)}) collective-permute-start(bf16[4,128,256]{2,1,0:T(8,128)(2,1)S(1)} %collective-permute-done.refs_5_), channel_id=1, source_target_pairs={{0,32},{32,0},{1,33},{33,1},{2,34},{34,2},{3,35},{35,3},{4,36},{36... | collective-permute-start | bytes 786440 | tf_op jit(solution)/shard_map/ppermute | solution.py:139
  67.2 9.5 %collective-permute-start.3 = (bf16[4,128,256]{2,1,0:T(8,128)(2,1)S(1)}, bf16[4,128,256]{2,1,0:T(8,128)(2,1)S(1)}, u32[]{:S(2)}, u32[]{:S(2)}) collective-permute-start(bf16[4,128,256]{2,1,0:T(8,128)(2,1)S(1)} %slice.4), channel_id=1, source_target_pairs={{0,64},{32,480},{64,128},{96,32},{128,192},{160,96},{192,256},{224... | collective-permute-start | bytes 786440 | tf_op jit(solution)/shard_map/ppermute | solution.py:124
  72.8 0.7 copy-start.6
  74.1 8.1 %copy-start.3 = (bf16[4,128,256]{2,1,0:T(8,128)(2,1)}, bf16[4,128,256]{2,1,0:T(8,128)(2,1)S(1)}, u32[]{:S(2)}) copy-start(bf16[4,128,256]{2,1,0:T(8,128)(2,1)S(1)} %collective-permute-done.1.refs_6_) | copy-start | bytes 786436
  76.7 5.5 %copy-start.4 = (bf16[4,128,256]{2,1,0:T(8,128)(2,1)}, bf16[4,128,256]{2,1,0:T(8,128)(2,1)S(1)}, u32[]{:S(2)}) copy-start(bf16[4,128,256]{2,1,0:T(8,128)(2,1)S(1)} %collective-permute-done.3.refs_8_) | copy-start | bytes 786436

commit v6 on v4

--- a/solution.py
+++ b/solution.py
@@ -13,15 +13,9 @@
 IRREPS = 8
 
 
-def order_kernel(blocks_ref, panel_ref, out_ref, sems):
-    copies = [
-        pltpu.make_async_copy(panel_ref.at[slot], out_ref.at[blocks_ref[slot]], sems.at[slot])
-        for slot in range(panel_ref.shape[0])
-    ]
-    for copy in copies:
-        copy.start()
-    for copy in copies:
-        copy.wait()
+def order_kernel(blocks_ref, panel_ref, out_ref):
+    for slot in range(panel_ref.shape[0]):
+        out_ref[blocks_ref[slot]] = panel_ref[slot]
 
 
 def irrep_order(panel, blocks):
@@ -30,10 +24,9 @@
         out_shape=pltpu.VMEM(panel.shape, panel.dtype),
         in_specs=[
             pl.BlockSpec(memory_space=pltpu.SMEM),
-            pl.BlockSpec(memory_space=pltpu.HBM),
+            pl.BlockSpec(memory_space=pltpu.VMEM),
         ],
         out_specs=pl.BlockSpec(memory_space=pltpu.VMEM),
-        scratch_shapes=[pltpu.SemaphoreType.DMA((panel.shape[0],))],
         name="irrep_order",
     )(blocks, panel)
 
@@ -79,7 +72,7 @@
         if group < len(arrivals):
             arrivals[group].wait()
         for index in range(tiles_ref.shape[0]):
-            core, zl = index % 4 // 2, index % 2
+            core, zl = index % 4 // 2, lax.rem(here_ref[1] + index % 2, 2)
             x = lax.rem(here_ref[0] + steps[index // 4] * side + N_X, N_X)
             tile = (zl * N_X + x) * 2 + core
             weights = weight_ref[pl.ds(piece_ref[tile], quarters)]
@@ -132,9 +125,10 @@
 
 def per_device(amplitudes, pair_irrep, integrals, panel_blocks, panel_owner):
     cols = integrals.shape[-1]
+    partner = lax.ppermute(amplitudes, "zl", [(0, 1), (1, 0)])
     ordered = irrep_order(integrals[0], panel_blocks[0])
     pieces = lax.all_to_all(ordered.reshape(N_VIR, -1, cols), VIR, 0, 0, tiled=True)
-    pair = lax.all_gather(amplitudes[None], "zl", axis=0, tiled=True)
+    pair = jnp.stack([amplitudes, partner])
     chip = lax.all_gather(pair, "core", axis=0, tiled=True)
     beside = away(chip, 1)
     here = jnp.stack([lax.axis_index("x"), lax.axis_index("zl")])

time: 81.5 us -> 83 us (1.018)
  blocking collectives: 8.43 us -> 1.99 us
  starting transfers between devices: 37 us -> 42 us
  waiting for transfers between devices: 26.1 us -> 28.7 us
    all_gather x1 -> x0, blocking collectives: 6.44 us -> none  [per_device(): pair = lax.all_gather(amplitudes[None], 'zl', axis=0, tiled=True)]
    ppermute x0 -> x1, starting transfers between devices: none -> 5.18 us  [per_device(): partner = lax.ppermute(amplitudes, 'zl', [(0, 1), (1, 0)])]
    ppermute x0 -> x1, waiting for transfers between devices: none -> 2.44 us  [per_device(): partner = lax.ppermute(amplitudes, 'zl', [(0, 1), (1, 0)])]
    another operation x0 -> x1, other arithmetic: none -> 0.85 us  [per_device(): pair = jnp.stack([amplitudes, partner])]
  transfers between devices with their start and end apart: 6 -> 7, of which waited for: 3 -> 4; matrix products, arithmetic and copies ran while one was open for 2% -> 2% of each run, Pallas kernels for 5% -> 4%
where the time goes in v6:
time: 83 us; the launch traced here: 82.4 us
  starting transfers between devices  42 us (51%)
  waiting for transfers between devices  28.7 us (35%)
  Pallas kernels  6.89 us (8%)
  other arithmetic  2.54 us (3%)
  blocking collectives  1.99 us (2%)
    all_to_all x1, starting transfers between devices, per_device(): lax.all_to_all(ordered.reshape(N_VIR, -1, cols), VIR, 0, 0, tiled=True)  21.1 us
    all_to_all x1, waiting for transfers between devices, per_device(): lax.all_to_all(ordered.reshape(N_VIR, -1, cols), VIR, 0, 0, tiled=True)  11.7 us
    ppermute x3, starting transfers between devices, away(): return lax.ppermute(array, ('x', 'core'), pairs)  9.64 us
    all_to_all x1, waiting for transfers between devices, per_device(): weights = lax.all_to_all(copies, VIR, 0, 0, tiled=True)  8.18 us
    ppermute x3, waiting for transfers between devices, away(): return lax.ppermute(array, ('x', 'core'), pairs)  6.39 us
    ppermute x1, starting transfers between devices, per_device(): partner = lax.ppermute(amplitudes, 'zl', [(0, 1), (1, 0)])  5.18 us
    all_to_all x1, starting transfers between devices, per_device(): weights = lax.all_to_all(copies, VIR, 0, 0, tiled=True)  4.24 us
    pallas_call x1, Pallas kernels, contract(): pl.pallas_call(lambda *refs: ladder_kernel(groups, *refs), out_shape=jax....  3.63 us
  transfers between devices with their start and end apart: 7, of which 4 were waited for; matrix products, arithmetic and copies ran while one was open for 2% of the time, Pallas kernels for 4%

profile of v6, /device:TPU:16, one launch (start us, length us, event | category | flops | bytes accessed | tf_op | source)
XLA Modules:
  0.0 82.4 jit_solution(12615957085802336948)
XLA Ops:
  0.0 5.2 %collective-permute-start = (bf16[128,256]{1,0:T(8,128)(2,1)}, bf16[128,256]{1,0:T(8,128)(2,1)S(1)}, u32[]{:S(2)}, u32[]{:S(2)}) collective-permute-start(bf16[128,256]{1,0:T(8,128)(2,1)} %param.5), channel_id=1, source_target_pairs={{0,512},{512,0},{1,513},{513,1},{2,514},{514,2},{3,515},{515,3},{4... | collective-permute-start | bytes 196616 | tf_op jit(solution)/shard_map/ppermute | solution.py:128
  5.2 2.4 %collective-permute-done = bf16[128,256]{1,0:T(8,128)(2,1)S(1)} collective-permute-done((bf16[128,256]{1,0:T(8,128)(2,1)}, bf16[128,256]{1,0:T(8,128)(2,1)S(1)}, u32[]{:S(2)}, u32[]{:S(2)}) %collective-permute-start) | collective-permute-done | bytes 65568 | tf_op jit(solution)/shard_map/ppermute | solution.py:128
  7.6 0.9 %pad_maximum_fusion.1 = bf16[2,128,256]{2,1,0:T(8,128)(2,1)S(1)} fusion(bf16[1,128,256]{2,1,0:T(8,128)(2,1)S(1)} %bitcast.10, bf16[1,128,256]{2,1,0:T(8,128)(2,1)} %bitcast.9), kind=kLoop, calls=%fused_computation.1 | loop fusion | flops 65536 | bytes 262144 | tf_op jit(solution)/shard_map/stack | solution.py:131
  8.5 2.0 %all_gather.3.refs_3_ = bf16[4,128,256]{2,1,0:T(8,128)(2,1)S(1)} all-gather(bf16[2,128,256]{2,1,0:T(8,128)(2,1)S(1)} %pad_maximum_fusion.1), channel_id=1, replica_groups=mesh['zl'=2,'x'=8,'core'=2,'zh'=4,'y'=8] {'core'}, dimensions={0}, use_global_device_ids=true | all-gather | bytes 393216 | tf_op jit(solution)/shard_map/all_gather | solution.py:132
  10.5 0.0 copy-start
  10.5 3.4 %collective-permute-start.1 = (bf16[4,128,256]{2,1,0:T(8,128)(2,1)S(1)}, bf16[4,128,256]{2,1,0:T(8,128)(2,1)S(1)}, u32[]{:S(2)}, u32[]{:S(2)}) collective-permute-start(bf16[4,128,256]{2,1,0:T(8,128)(2,1)S(1)} %all_gather.3.refs_3_), channel_id=1, source_target_pairs={{0,64},{32,480},{64,128},{96,32},{128,192},{160,96},{192,256},{224... | collective-permute-start | bytes 786440 | tf_op jit(solution)/shard_map/ppermute | solution.py:123
  13.9 1.7 %irrep_order.1 = bf16[8,128,128]{2,1,0:T(8,128)(2,1)} custom-call(s32[8]{0:T(128)} %bitcast.11, bf16[8,128,128]{2,1,0:T(8,128)(2,1)} %bitcast.8), custom_call_target="tpu_custom_call" | custom-call | tf_op jit(solution)/shard_map/irrep_order/pallas_call | solution.py:22
  15.6 21.1 %all-to-all-start = ((bf16[32,32,128]{2,1,0:T(8,128)(2,1)}), bf16[32,32,128]{2,1,0:T(8,128)(2,1)S(1)}, u32[]{:S(2)}, u32[]{:S(2)}) async-start(bf16[32,32,128]{2,1,0:T(8,128)(2,1)} %bitcast.6), calls=%async_computation | async-start | bytes 524288 | tf_op jit(solution)/shard_map/all_to_all | solution.py:130
  36.6 0.0 collective-permute-done.1
  36.6 0.0 copy-done
  36.7 4.3 %collective-permute-start.2 = (bf16[8,128,256]{2,1,0:T(8,128)(2,1)S(1)}, bf16[8,128,256]{2,1,0:T(8,128)(2,1)S(1)}, u32[]{:S(2)}, u32[]{:S(2)}) collective-permute-start(bf16[8,128,256]{2,1,0:T(8,128)(2,1)S(1)} %pad_maximum_fusion), channel_id=1, source_target_pairs={{0,128},{32,416},{64,192},{96,480},{128,256},{160,32},{192,320},{2... | collective-permute-start | bytes 1572872 | tf_op jit(solution)/shard_map/ppermute | solution.py:123
  41.1 11.7 %all-to-all-done.pieces_ref = bf16[32,32,128]{2,1,0:T(8,128)(2,1)S(1)} async-done(((bf16[32,32,128]{2,1,0:T(8,128)(2,1)}), bf16[32,32,128]{2,1,0:T(8,128)(2,1)S(1)}, u32[]{:S(2)}, u32[]{:S(2)}) %all-to-all-start) | async-done | bytes 262176 | tf_op jit(solution)/shard_map/all_to_all | solution.py:130
  52.8 1.6 %shard_map.55 = bf16[32,64,128]{2,1,0:T(8,128)(2,1)} custom-call(s32[2]{0:T(128)} %owner_ref.1, bf16[32,32,128]{2,1,0:T(8,128)(2,1)S(1)} %all-to-all-done.pieces_ref), custom_call_target="tpu_custom_call" | custom-call | tf_op jit(solution)/shard_map/pallas_call | solution.py:44
  54.3 4.2 %all-to-all-start.1 = ((bf16[32,64,128]{2,1,0:T(8,128)(2,1)}), bf16[32,64,128]{2,1,0:T(8,128)(2,1)S(1)}, u32[]{:S(2)}, u32[]{:S(2)}) async-start(bf16[32,64,128]{2,1,0:T(8,128)(2,1)} %shard_map.55), calls=%async_computation.1 | async-start | bytes 1048576 | tf_op jit(solution)/shard_map/all_to_all | solution.py:137
  58.6 0.0 collective-permute-done.2
  58.7 0.0 copy-start.1
  58.7 1.9 %collective-permute-start.4 = (bf16[12,128,256]{2,1,0:T(8,128)(2,1)S(1)}, bf16[12,128,256]{2,1,0:T(8,128)(2,1)S(1)}, u32[]{:S(2)}, u32[]{:S(2)}) collective-permute-start(bf16[12,128,256]{2,1,0:T(8,128)(2,1)S(1)} %constant_dynamic-update-slice_fusion.refs_4_), channel_id=1, source_target_pairs={{0,32},{32,0},{1,33},{33,1},{2,34},{34,2},{3,35},{35,3},{4,36},{36... | collective-permute-start | bytes 2359304 | tf_op jit(solution)/shard_map/ppermute | solution.py:141
  60.6 0.5 iota_add_fusion.refs_2_
  61.1 1.9 %collective-permute-start.3 = (bf16[4,128,256]{2,1,0:T(8,128)(2,1)S(1)}, bf16[4,128,256]{2,1,0:T(8,128)(2,1)S(1)}, u32[]{:S(2)}, u32[]{:S(2)}) collective-permute-start(bf16[4,128,256]{2,1,0:T(8,128)(2,1)S(1)} %slice.4), channel_id=1, source_target_pairs={{0,64},{32,480},{64,128},{96,32},{128,192},{160,96},{192,256},{224... | collective-permute-start | bytes 786440 | tf_op jit(solution)/shard_map/ppermute | solution.py:123
  63.1 0.0 copy-start.3
  63.1 0.6 pad_add_fusion.refs_1_
  63.7 0.0 copy-done.3
  63.7 0.5 broadcast_multiply_fusion.refs_0_
  64.2 6.4 %collective-permute-done.3.refs_5_ = bf16[4,128,256]{2,1,0:T(8,128)(2,1)S(1)} collective-permute-done((bf16[4,128,256]{2,1,0:T(8,128)(2,1)S(1)}, bf16[4,128,256]{2,1,0:T(8,128)(2,1)S(1)}, u32[]{:S(2)}, u32[]{:S(2)}) %collective-permute-start.3) | collective-permute-done | bytes 262176 | tf_op jit(solution)/shard_map/ppermute | solution.py:123
  70.6 0.0 copy-start.2
  70.6 8.2 %all-to-all-done.1.refs_7_ = bf16[32,64,128]{2,1,0:T(8,128)(2,1)S(1)} async-done(((bf16[32,64,128]{2,1,0:T(8,128)(2,1)}), bf16[32,64,128]{2,1,0:T(8,128)(2,1)S(1)}, u32[]{:S(2)}, u32[]{:S(2)}) %all-to-all-start.1) | async-done | bytes 524320 | tf_op jit(solution)/shard_map/all_to_all | solution.py:137
  78.8 0.0 collective-permute-done.4.refs_6_
  78.8 0.0 copy-done.1
  78.8 0.0 copy-done.2
  78.8 3.6 %ladder.1 = bf16[32,128,128]{2,1,0:T(8,128)(2,1)} custom-call(s32[32]{0:T(128)} %broadcast_multiply_fusion.refs_0_, s32[2]{0:T(128)} %pad_add_fusion.refs_1_, s32[16]{0:T(128)} %iota_add_fusion.refs_2_, bf16[4,128,256]{2,1,0:T(8,128)(2,1)} %copy-done, bf16[12,128,256]{2,1,0:T(8,128)(2,1)} %copy-done.1, bf16[4,128,256]{2,1,0:T(8,128)(2,1)} %copy-done.2, ...), custom_call_target="tpu_custom_call" | custom-call | tf_op jit(solution)/shard_map/ladder/pallas_call | solution.py:102
  (4 shorter events, 0.1 us)
Async XLA Ops:
  0.0 7.6 %collective-permute-start = (bf16[128,256]{1,0:T(8,128)(2,1)}, bf16[128,256]{1,0:T(8,128)(2,1)S(1)}, u32[]{:S(2)}, u32[]{:S(2)}) collective-permute-start(bf16[128,256]{1,0:T(8,128)(2,1)} %param.5), channel_id=1, source_target_pairs={{0,512},{512,0},{1,513},{513,1},{2,514},{514,2},{3,515},{515,3},{4... | collective-permute-start | bytes 196616 | tf_op jit(solution)/shard_map/ppermute | solution.py:128
  10.5 26.2 %copy-start = (bf16[4,128,256]{2,1,0:T(8,128)(2,1)}, bf16[4,128,256]{2,1,0:T(8,128)(2,1)S(1)}, u32[]{:S(2)}) copy-start(bf16[4,128,256]{2,1,0:T(8,128)(2,1)S(1)} %all_gather.3.refs_3_) | copy-start | bytes 786436
  10.5 26.2 %collective-permute-start.1 = (bf16[4,128,256]{2,1,0:T(8,128)(2,1)S(1)}, bf16[4,128,256]{2,1,0:T(8,128)(2,1)S(1)}, u32[]{:S(2)}, u32[]{:S(2)}) collective-permute-start(bf16[4,128,256]{2,1,0:T(8,128)(2,1)S(1)} %all_gather.3.refs_3_), channel_id=1, source_target_pairs={{0,64},{32,480},{64,128},{96,32},{128,192},{160,96},{192,256},{224... | collective-permute-start | bytes 786440 | tf_op jit(solution)/shard_map/ppermute | solution.py:123
  15.6 37.2 %all-to-all-start = ((bf16[32,32,128]{2,1,0:T(8,128)(2,1)}), bf16[32,32,128]{2,1,0:T(8,128)(2,1)S(1)}, u32[]{:S(2)}, u32[]{:S(2)}) async-start(bf16[32,32,128]{2,1,0:T(8,128)(2,1)} %bitcast.6), calls=%async_computation | async-start | bytes 524288 | tf_op jit(solution)/shard_map/all_to_all | solution.py:130
  36.7 21.9 %collective-permute-start.2 = (bf16[8,128,256]{2,1,0:T(8,128)(2,1)S(1)}, bf16[8,128,256]{2,1,0:T(8,128)(2,1)S(1)}, u32[]{:S(2)}, u32[]{:S(2)}) collective-permute-start(bf16[8,128,256]{2,1,0:T(8,128)(2,1)S(1)} %pad_maximum_fusion), channel_id=1, source_target_pairs={{0,128},{32,416},{64,192},{96,480},{128,256},{160,32},{192,320},{2... | collective-permute-start | bytes 1572872 | tf_op jit(solution)/shard_map/ppermute | solution.py:123
  54.3 24.5 %all-to-all-start.1 = ((bf16[32,64,128]{2,1,0:T(8,128)(2,1)}), bf16[32,64,128]{2,1,0:T(8,128)(2,1)S(1)}, u32[]{:S(2)}, u32[]{:S(2)}) async-start(bf16[32,64,128]{2,1,0:T(8,128)(2,1)} %shard_map.55), calls=%async_computation.1 | async-start | bytes 1048576 | tf_op jit(solution)/shard_map/all_to_all | solution.py:137
  58.7 20.1 %copy-start.1 = (bf16[12,128,256]{2,1,0:T(8,128)(2,1)}, bf16[12,128,256]{2,1,0:T(8,128)(2,1)S(1)}, u32[]{:S(2)}) copy-start(bf16[12,128,256]{2,1,0:T(8,128)(2,1)S(1)} %constant_dynamic-update-slice_fusion.refs_4_) | copy-start | bytes 2359300
  58.7 20.1 %collective-permute-start.4 = (bf16[12,128,256]{2,1,0:T(8,128)(2,1)S(1)}, bf16[12,128,256]{2,1,0:T(8,128)(2,1)S(1)}, u32[]{:S(2)}, u32[]{:S(2)}) collective-permute-start(bf16[12,128,256]{2,1,0:T(8,128)(2,1)S(1)} %constant_dynamic-update-slice_fusion.refs_4_), channel_id=1, source_target_pairs={{0,32},{32,0},{1,33},{33,1},{2,34},{34,2},{3,35},{35,3},{4,36},{36... | collective-permute-start | bytes 2359304 | tf_op jit(solution)/shard_map/ppermute | solution.py:141
  61.1 9.5 %collective-permute-start.3 = (bf16[4,128,256]{2,1,0:T(8,128)(2,1)S(1)}, bf16[4,128,256]{2,1,0:T(8,128)(2,1)S(1)}, u32[]{:S(2)}, u32[]{:S(2)}) collective-permute-start(bf16[4,128,256]{2,1,0:T(8,128)(2,1)S(1)} %slice.4), channel_id=1, source_target_pairs={{0,64},{32,480},{64,128},{96,32},{128,192},{160,96},{192,256},{224... | collective-permute-start | bytes 786440 | tf_op jit(solution)/shard_map/ppermute | solution.py:123
  63.1 0.7 copy-start.3
  70.6 8.2 %copy-start.2 = (bf16[4,128,256]{2,1,0:T(8,128)(2,1)}, bf16[4,128,256]{2,1,0:T(8,128)(2,1)S(1)}, u32[]{:S(2)}) copy-start(bf16[4,128,256]{2,1,0:T(8,128)(2,1)S(1)} %collective-permute-done.3.refs_5_) | copy-start | bytes 786436

commit v7 on v6

--- a/solution.py
+++ b/solution.py
@@ -52,7 +52,7 @@
     )(owners, pltpu.with_memory_space_constraint(pieces, pltpu.VMEM))
 
 
-HERE, OPPOSITE, MINE, THEIRS = (0,), (4,), (1, 3, 2), (-1, -3, -2)
+HERE, OPPOSITE, MINE, THEIRS = (0,), (4,), (1, 2, 3), (-1, -2, -3)
 
 
 def ladder_kernel(groups, piece_ref, here_ref, side_ref, *refs):
@@ -131,13 +131,14 @@
     pair = jnp.stack([amplitudes, partner])
     chip = lax.all_gather(pair, "core", axis=0, tiled=True)
     beside = away(chip, 1)
+    two = away(chip, 2)
+    three = away(chip, 3)
     here = jnp.stack([lax.axis_index("x"), lax.axis_index("zl")])
     copies = pick_and_copy(pieces, panel_owner)
-    wide = away(jnp.concatenate([beside, chip]), 2)
     weights = lax.all_to_all(copies, VIR, 0, 0, tiled=True)
     side = jnp.arange(16, dtype=jnp.int32) + lax.axis_index("core")
-    opposite = away(wide[:4], 1)
-    mine = jnp.concatenate([beside, wide])
+    opposite = away(three, 1)
+    mine = jnp.concatenate([beside, two, three])
     theirs = lax.ppermute(mine, "core", [(0, 1), (1, 0)])
     first_piece = pair_irrep * (N_VIR // IRREPS)
     groups = (HERE, MINE, OPPOSITE, THEIRS)

time: 83 us -> 80.1 us (0.965)
  the two profiles are of different devices: /device:TPU:16 before, /device:TPU:18 now
where the time goes in v7:
time: 80.1 us; the launch traced here: 79.5 us
  starting transfers between devices  53.9 us (67%)
  waiting for transfers between devices  14.7 us (18%)
  Pallas kernels  6.89 us (9%)
  blocking collectives  1.99 us (2%)
  other arithmetic  1.72 us (2%)
    all_to_all x1, starting transfers between devices, per_device(): lax.all_to_all(ordered.reshape(N_VIR, -1, cols), VIR, 0, 0, tiled=True)  21.2 us
    ppermute x4, starting transfers between devices, away(): return lax.ppermute(array, ('x', 'core'), pairs)  14.3 us
    all_to_all x1, starting transfers between devices, per_device(): weights = lax.all_to_all(copies, VIR, 0, 0, tiled=True)  11.3 us
    all_to_all x1, waiting for transfers between devices, per_device(): weights = lax.all_to_all(copies, VIR, 0, 0, tiled=True)  9.57 us
    ppermute x1, starting transfers between devices, per_device(): partner = lax.ppermute(amplitudes, 'zl', [(0, 1), (1, 0)])  5.18 us
    ppermute x4, waiting for transfers between devices, away(): return lax.ppermute(array, ('x', 'core'), pairs)  4.23 us
    pallas_call x1, Pallas kernels, contract(): pl.pallas_call(lambda *refs: ladder_kernel(groups, *refs), out_shape=jax....  3.63 us
    all_gather x1, blocking collectives, per_device(): chip = lax.all_gather(pair, 'core', axis=0, tiled=True)  1.99 us
  transfers between devices with their start and end apart: 8, of which 4 were waited for; matrix products, arithmetic and copies ran while one was open for 2% of the time, Pallas kernels for 4%

profile of v7, /device:TPU:18, one launch (start us, length us, event | category | flops | bytes accessed | tf_op | source)
XLA Modules:
  0.0 79.5 jit_solution(16512194368940333454)
XLA Ops:
  0.0 5.2 %collective-permute-start = (bf16[128,256]{1,0:T(8,128)(2,1)}, bf16[128,256]{1,0:T(8,128)(2,1)S(1)}, u32[]{:S(2)}, u32[]{:S(2)}) collective-permute-start(bf16[128,256]{1,0:T(8,128)(2,1)} %param.5), channel_id=1, source_target_pairs={{0,512},{512,0},{1,513},{513,1},{2,514},{514,2},{3,515},{515,3},{4... | collective-permute-start | bytes 196616 | tf_op jit(solution)/shard_map/ppermute | solution.py:128
  5.2 1.7 %irrep_order.1 = bf16[8,128,128]{2,1,0:T(8,128)(2,1)} custom-call(s32[8]{0:T(128)} %bitcast.11, bf16[8,128,128]{2,1,0:T(8,128)(2,1)} %bitcast.8), custom_call_target="tpu_custom_call" | custom-call | tf_op jit(solution)/shard_map/irrep_order/pallas_call | solution.py:22
  6.9 0.0 copy-start.3
  6.9 21.2 %all-to-all-start = ((bf16[32,32,128]{2,1,0:T(8,128)(2,1)}), bf16[32,32,128]{2,1,0:T(8,128)(2,1)S(1)}, u32[]{:S(2)}, u32[]{:S(2)}) async-start(bf16[32,32,128]{2,1,0:T(8,128)(2,1)} %bitcast.6), calls=%async_computation | async-start | bytes 524288 | tf_op jit(solution)/shard_map/all_to_all | solution.py:130
  28.1 0.0 collective-permute-done
  28.1 0.0 copy-done.3
  28.1 2.0 %all_gather.3.refs_3_ = bf16[4,128,256]{2,1,0:T(8,128)(2,1)S(1)} all-gather(bf16[2,128,256]{2,1,0:T(8,128)(2,1)S(1)} %pad_maximum_fusion), channel_id=1, replica_groups=mesh['zl'=2,'x'=8,'core'=2,'zh'=4,'y'=8] {'core'}, dimensions={0}, use_global_device_ids=true | all-gather | bytes 393216 | tf_op jit(solution)/shard_map/all_gather | solution.py:132
  30.1 0.0 copy-start.1
  30.1 3.4 %collective-permute-start.1 = (bf16[4,128,256]{2,1,0:T(8,128)(2,1)S(1)}, bf16[4,128,256]{2,1,0:T(8,128)(2,1)S(1)}, u32[]{:S(2)}, u32[]{:S(2)}) collective-permute-start(bf16[4,128,256]{2,1,0:T(8,128)(2,1)S(1)} %all_gather.3.refs_3_), channel_id=1, source_target_pairs={{0,64},{32,480},{64,128},{96,32},{128,192},{160,96},{192,256},{224... | collective-permute-start | bytes 786440 | tf_op jit(solution)/shard_map/ppermute | solution.py:123
  33.5 5.5 %collective-permute-start.2 = (bf16[4,128,256]{2,1,0:T(8,128)(2,1)S(1)}, bf16[4,128,256]{2,1,0:T(8,128)(2,1)S(1)}, u32[]{:S(2)}, u32[]{:S(2)}) collective-permute-start(bf16[4,128,256]{2,1,0:T(8,128)(2,1)S(1)} %all_gather.3.refs_3_), channel_id=1, source_target_pairs={{0,128},{32,416},{64,192},{96,480},{128,256},{160,32},{192,320},{2... | collective-permute-start | bytes 786440 | tf_op jit(solution)/shard_map/ppermute | solution.py:123
  39.1 2.6 %collective-permute-start.3 = (bf16[4,128,256]{2,1,0:T(8,128)(2,1)S(1)}, bf16[4,128,256]{2,1,0:T(8,128)(2,1)S(1)}, u32[]{:S(2)}, u32[]{:S(2)}) collective-permute-start(bf16[4,128,256]{2,1,0:T(8,128)(2,1)S(1)} %all_gather.3.refs_3_), channel_id=1, source_target_pairs={{0,192},{32,352},{64,256},{96,416},{128,320},{160,480},{192,384},{... | collective-permute-start | bytes 786440 | tf_op jit(solution)/shard_map/ppermute | solution.py:123
  41.6 0.0 collective-permute-done.1
  41.7 0.0 copy-done.1
  41.7 0.9 %all-to-all-done.pieces_ref = bf16[32,32,128]{2,1,0:T(8,128)(2,1)S(1)} async-done(((bf16[32,32,128]{2,1,0:T(8,128)(2,1)}), bf16[32,32,128]{2,1,0:T(8,128)(2,1)S(1)}, u32[]{:S(2)}, u32[]{:S(2)}) %all-to-all-start) | async-done | bytes 262176 | tf_op jit(solution)/shard_map/all_to_all | solution.py:130
  42.6 1.6 %shard_map.55 = bf16[32,64,128]{2,1,0:T(8,128)(2,1)} custom-call(s32[2]{0:T(128)} %owner_ref.1, bf16[32,32,128]{2,1,0:T(8,128)(2,1)S(1)} %all-to-all-done.pieces_ref), custom_call_target="tpu_custom_call" | custom-call | tf_op jit(solution)/shard_map/pallas_call | solution.py:44
  44.1 11.3 %all-to-all-start.1 = ((bf16[32,64,128]{2,1,0:T(8,128)(2,1)}), bf16[32,64,128]{2,1,0:T(8,128)(2,1)S(1)}, u32[]{:S(2)}, u32[]{:S(2)}) async-start(bf16[32,64,128]{2,1,0:T(8,128)(2,1)} %shard_map.55), calls=%async_computation.1 | async-start | bytes 1048576 | tf_op jit(solution)/shard_map/all_to_all | solution.py:138
  55.5 0.0 collective-permute-done.2
  55.5 0.1 collective-permute-done.3
  55.6 0.0 copy-start
  55.6 1.9 %collective-permute-start.5 = (bf16[12,128,256]{2,1,0:T(8,128)(2,1)S(1)}, bf16[12,128,256]{2,1,0:T(8,128)(2,1)S(1)}, u32[]{:S(2)}, u32[]{:S(2)}) collective-permute-start(bf16[12,128,256]{2,1,0:T(8,128)(2,1)S(1)} %constant_dynamic-update-slice_fusion.refs_4_), channel_id=1, source_target_pairs={{0,32},{32,0},{1,33},{33,1},{2,34},{34,2},{3,35},{35,3},{4,36},{36... | collective-permute-start | bytes 2359304 | tf_op jit(solution)/shard_map/ppermute | solution.py:142
  57.5 0.5 iota_add_fusion.refs_2_
  58.1 2.8 %collective-permute-start.4 = (bf16[4,128,256]{2,1,0:T(8,128)(2,1)S(1)}, bf16[4,128,256]{2,1,0:T(8,128)(2,1)S(1)}, u32[]{:S(2)}, u32[]{:S(2)}) collective-permute-start(bf16[4,128,256]{2,1,0:T(8,128)(2,1)S(1)} %collective-permute-done.3), channel_id=1, source_target_pairs={{0,64},{32,480},{64,128},{96,32},{128,192},{160,96},{192,256},{224... | collective-permute-start | bytes 786440 | tf_op jit(solution)/shard_map/ppermute | solution.py:123
  60.9 0.0 copy-start.4
  60.9 0.6 pad_add_fusion.refs_1_
  61.5 0.1 copy-done.4
  61.6 0.6 broadcast_multiply_fusion.refs_0_
  62.2 4.2 %collective-permute-done.4.refs_5_ = bf16[4,128,256]{2,1,0:T(8,128)(2,1)S(1)} collective-permute-done((bf16[4,128,256]{2,1,0:T(8,128)(2,1)S(1)}, bf16[4,128,256]{2,1,0:T(8,128)(2,1)S(1)}, u32[]{:S(2)}, u32[]{:S(2)}) %collective-permute-start.4) | collective-permute-done | bytes 262176 | tf_op jit(solution)/shard_map/ppermute | solution.py:123
  66.3 0.0 collective-permute-done.5.refs_6_
  66.3 9.6 %all-to-all-done.1.refs_7_ = bf16[32,64,128]{2,1,0:T(8,128)(2,1)S(1)} async-done(((bf16[32,64,128]{2,1,0:T(8,128)(2,1)}), bf16[32,64,128]{2,1,0:T(8,128)(2,1)S(1)}, u32[]{:S(2)}, u32[]{:S(2)}) %all-to-all-start.1) | async-done | bytes 524320 | tf_op jit(solution)/shard_map/all_to_all | solution.py:138
  75.9 0.0 copy-done
  75.9 0.0 copy-done.2
  75.9 3.6 %ladder.1 = bf16[32,128,128]{2,1,0:T(8,128)(2,1)} custom-call(s32[32]{0:T(128)} %broadcast_multiply_fusion.refs_0_, s32[2]{0:T(128)} %pad_add_fusion.refs_1_, s32[16]{0:T(128)} %iota_add_fusion.refs_2_, bf16[4,128,256]{2,1,0:T(8,128)(2,1)} %copy-done.1, bf16[12,128,256]{2,1,0:T(8,128)(2,1)} %copy-done, bf16[4,128,256]{2,1,0:T(8,128)(2,1)} %copy-done.2, ...), custom_call_target="tpu_custom_call" | custom-call | tf_op jit(solution)/shard_map/ladder/pallas_call | solution.py:102
  (5 shorter events, 0.1 us)
Async XLA Ops:
  0.0 28.1 %collective-permute-start = (bf16[128,256]{1,0:T(8,128)(2,1)}, bf16[128,256]{1,0:T(8,128)(2,1)S(1)}, u32[]{:S(2)}, u32[]{:S(2)}) collective-permute-start(bf16[128,256]{1,0:T(8,128)(2,1)} %param.5), channel_id=1, source_target_pairs={{0,512},{512,0},{1,513},{513,1},{2,514},{514,2},{3,515},{515,3},{4... | collective-permute-start | bytes 196616 | tf_op jit(solution)/shard_map/ppermute | solution.py:128
  6.9 21.2 %copy-start.3 = (bf16[128,256]{1,0:T(8,128)(2,1)S(1)}, bf16[128,256]{1,0:T(8,128)(2,1)}, u32[]{:S(2)}) copy-start(bf16[128,256]{1,0:T(8,128)(2,1)} %param.5) | copy-start | bytes 196612
  6.9 35.7 %all-to-all-start = ((bf16[32,32,128]{2,1,0:T(8,128)(2,1)}), bf16[32,32,128]{2,1,0:T(8,128)(2,1)S(1)}, u32[]{:S(2)}, u32[]{:S(2)}) async-start(bf16[32,32,128]{2,1,0:T(8,128)(2,1)} %bitcast.6), calls=%async_computation | async-start | bytes 524288 | tf_op jit(solution)/shard_map/all_to_all | solution.py:130
  30.1 11.5 %copy-start.1 = (bf16[4,128,256]{2,1,0:T(8,128)(2,1)}, bf16[4,128,256]{2,1,0:T(8,128)(2,1)S(1)}, u32[]{:S(2)}) copy-start(bf16[4,128,256]{2,1,0:T(8,128)(2,1)S(1)} %all_gather.3.refs_3_) | copy-start | bytes 786436
  30.1 11.5 %collective-permute-start.1 = (bf16[4,128,256]{2,1,0:T(8,128)(2,1)S(1)}, bf16[4,128,256]{2,1,0:T(8,128)(2,1)S(1)}, u32[]{:S(2)}, u32[]{:S(2)}) collective-permute-start(bf16[4,128,256]{2,1,0:T(8,128)(2,1)S(1)} %all_gather.3.refs_3_), channel_id=1, source_target_pairs={{0,64},{32,480},{64,128},{96,32},{128,192},{160,96},{192,256},{224... | collective-permute-start | bytes 786440 | tf_op jit(solution)/shard_map/ppermute | solution.py:123
  33.5 21.9 %collective-permute-start.2 = (bf16[4,128,256]{2,1,0:T(8,128)(2,1)S(1)}, bf16[4,128,256]{2,1,0:T(8,128)(2,1)S(1)}, u32[]{:S(2)}, u32[]{:S(2)}) collective-permute-start(bf16[4,128,256]{2,1,0:T(8,128)(2,1)S(1)} %all_gather.3.refs_3_), channel_id=1, source_target_pairs={{0,128},{32,416},{64,192},{96,480},{128,256},{160,32},{192,320},{2... | collective-permute-start | bytes 786440 | tf_op jit(solution)/shard_map/ppermute | solution.py:123
  39.1 16.5 %collective-permute-start.3 = (bf16[4,128,256]{2,1,0:T(8,128)(2,1)S(1)}, bf16[4,128,256]{2,1,0:T(8,128)(2,1)S(1)}, u32[]{:S(2)}, u32[]{:S(2)}) collective-permute-start(bf16[4,128,256]{2,1,0:T(8,128)(2,1)S(1)} %all_gather.3.refs_3_), channel_id=1, source_target_pairs={{0,192},{32,352},{64,256},{96,416},{128,320},{160,480},{192,384},{... | collective-permute-start | bytes 786440 | tf_op jit(solution)/shard_map/ppermute | solution.py:123
  44.1 31.8 %all-to-all-start.1 = ((bf16[32,64,128]{2,1,0:T(8,128)(2,1)}), bf16[32,64,128]{2,1,0:T(8,128)(2,1)S(1)}, u32[]{:S(2)}, u32[]{:S(2)}) async-start(bf16[32,64,128]{2,1,0:T(8,128)(2,1)} %shard_map.55), calls=%async_computation.1 | async-start | bytes 1048576 | tf_op jit(solution)/shard_map/all_to_all | solution.py:138
  55.6 20.3 %copy-start = (bf16[12,128,256]{2,1,0:T(8,128)(2,1)}, bf16[12,128,256]{2,1,0:T(8,128)(2,1)S(1)}, u32[]{:S(2)}) copy-start(bf16[12,128,256]{2,1,0:T(8,128)(2,1)S(1)} %constant_dynamic-update-slice_fusion.refs_4_) | copy-start | bytes 2359300
  55.6 10.7 %collective-permute-start.5 = (bf16[12,128,256]{2,1,0:T(8,128)(2,1)S(1)}, bf16[12,128,256]{2,1,0:T(8,128)(2,1)S(1)}, u32[]{:S(2)}, u32[]{:S(2)}) collective-permute-start(bf16[12,128,256]{2,1,0:T(8,128)(2,1)S(1)} %constant_dynamic-update-slice_fusion.refs_4_), channel_id=1, source_target_pairs={{0,32},{32,0},{1,33},{33,1},{2,34},{34,2},{3,35},{35,3},{4,36},{36... | collective-permute-start | bytes 2359304 | tf_op jit(solution)/shard_map/ppermute | solution.py:142
  58.1 8.3 %collective-permute-start.4 = (bf16[4,128,256]{2,1,0:T(8,128)(2,1)S(1)}, bf16[4,128,256]{2,1,0:T(8,128)(2,1)S(1)}, u32[]{:S(2)}, u32[]{:S(2)}) collective-permute-start(bf16[4,128,256]{2,1,0:T(8,128)(2,1)S(1)} %collective-permute-done.3), channel_id=1, source_target_pairs={{0,64},{32,480},{64,128},{96,32},{128,192},{160,96},{192,256},{224... | collective-permute-start | bytes 786440 | tf_op jit(solution)/shard_map/ppermute | solution.py:123
  60.9 0.7 copy-start.4
  66.3 9.6 %copy-start.2 = (bf16[4,128,256]{2,1,0:T(8,128)(2,1)}, bf16[4,128,256]{2,1,0:T(8,128)(2,1)S(1)}, u32[]{:S(2)}) copy-start(bf16[4,128,256]{2,1,0:T(8,128)(2,1)S(1)} %collective-permute-done.4.refs_5_) | copy-start | bytes 786436

commit v8 on v7

--- a/solution.py
+++ b/solution.py
@@ -52,10 +52,11 @@
     )(owners, pltpu.with_memory_space_constraint(pieces, pltpu.VMEM))
 
 
-HERE, OPPOSITE, MINE, THEIRS = (0,), (4,), (1, 2, 3), (-1, -2, -3)
+HERE, MINE, THEIRS = (0,), (1, 3), (-1, -3)
+MIDDLE, OPPOSITE, OTHER_MIDDLE = (2,), (4,), (-2,)
 
 
-def ladder_kernel(groups, piece_ref, here_ref, side_ref, *refs):
+def ladder_kernel(groups, piece_ref, second_ref, here_ref, side_ref, *refs):
     held_refs, refs = refs[:len(groups) - 1], refs[len(groups) - 1:]
     last_ref, weight_ref, out_ref, done_ref, sems, in_sems = refs[:6]
     tiles_refs = refs[6:]
@@ -73,7 +74,7 @@
             arrivals[group].wait()
         for index in range(tiles_ref.shape[0]):
             core, zl = index % 4 // 2, lax.rem(here_ref[1] + index % 2, 2)
-            x = lax.rem(here_ref[0] + steps[index // 4] * side + N_X, N_X)
+            x = lax.rem((here_ref if group < 3 else second_ref)[0] + steps[index // 4] * side + N_X, N_X)
             tile = (zl * N_X + x) * 2 + core
             weights = weight_ref[pl.ds(piece_ref[tile], quarters)]
             rows = weights.shape[1] // 2
@@ -91,7 +92,7 @@
         copy.wait()
 
 
-def contract(groups, arrays, first_piece, here, side, weights):
+def contract(groups, arrays, first_piece, second, here, side, weights):
     rows = arrays[0].shape[1]
     cols = weights.shape[2]
     count = sum(array.shape[0] for array in arrays)
@@ -102,7 +103,7 @@
     out = pl.pallas_call(
         lambda *refs: ladder_kernel(groups, *refs),
         out_shape=jax.ShapeDtypeStruct((count, rows, cols), jnp.bfloat16),
-        in_specs=[smem, smem, smem] + [pl.BlockSpec(memory_space=pltpu.HBM)] * len(arrays) + [vmem] * 2,
+        in_specs=[smem] * 4 + [pl.BlockSpec(memory_space=pltpu.HBM)] * len(arrays) + [vmem] * 2,
         out_specs=pl.BlockSpec(memory_space=pl.ANY),
         scratch_shapes=[
             pltpu.VMEM((count, rows, cols), jnp.bfloat16),
@@ -111,7 +112,7 @@
             *(pltpu.VMEM(array.shape, array.dtype) for array in arrays),
         ],
         name="ladder",
-    )(first_piece, here, side, *operands)
+    )(first_piece, second, here, side, *operands)
     return out.reshape(count * rows, cols)
 
 
@@ -131,19 +132,21 @@
     pair = jnp.stack([amplitudes, partner])
     chip = lax.all_gather(pair, "core", axis=0, tiled=True)
     beside = away(chip, 1)
-    two = away(chip, 2)
     three = away(chip, 3)
     here = jnp.stack([lax.axis_index("x"), lax.axis_index("zl")])
     copies = pick_and_copy(pieces, panel_owner)
     weights = lax.all_to_all(copies, VIR, 0, 0, tiled=True)
     side = jnp.arange(16, dtype=jnp.int32) + lax.axis_index("core")
+    middle = away(beside, 1)
     opposite = away(three, 1)
-    mine = jnp.concatenate([beside, two, three])
+    mine = jnp.concatenate([beside, three])
     theirs = lax.ppermute(mine, "core", [(0, 1), (1, 0)])
+    second = jnp.arange(24, dtype=jnp.int32) + lax.axis_index("x")
+    other_middle = lax.ppermute(middle, "core", [(0, 1), (1, 0)])
     first_piece = pair_irrep * (N_VIR // IRREPS)
-    groups = (HERE, MINE, OPPOSITE, THEIRS)
-    arrays = (chip, mine, opposite, theirs)
-    return contract(groups, arrays, first_piece, here, side, weights)
+    groups = (HERE, MINE, THEIRS, MIDDLE, OPPOSITE, OTHER_MIDDLE)
+    arrays = (chip, mine, theirs, middle, opposite, other_middle)
+    return contract(groups, arrays, first_piece, second, here, side, weights)
 
 
 def solution(mesh):

time: 80.1 us -> 86.3 us (1.077)
  the two profiles are of different devices: /device:TPU:18 before, /device:TPU:1 now
where the time goes in v8:
time: 86.3 us; the launch traced here: 85.7 us
  starting transfers between devices  59.8 us (69%)
  waiting for transfers between devices  10.2 us (12%)
  Pallas kernels  7.2 us (8%)
  blocking collectives  5.07 us (6%)
  other arithmetic  2.19 us (3%)
  local copies, waits for them, and re-layouts  0.98 us (1%)
    all_to_all x1, starting transfers between devices, per_device(): lax.all_to_all(ordered.reshape(N_VIR, -1, cols), VIR, 0, 0, tiled=True)  22.5 us
    ppermute x4, starting transfers between devices, away(): return lax.ppermute(array, ('x', 'core'), pairs)  15.7 us
    all_to_all x1, starting transfers between devices, per_device(): weights = lax.all_to_all(copies, VIR, 0, 0, tiled=True)  11.1 us
    ppermute x4, waiting for transfers between devices, away(): return lax.ppermute(array, ('x', 'core'), pairs)  6.58 us
    all_gather x1, blocking collectives, per_device(): chip = lax.all_gather(pair, 'core', axis=0, tiled=True)  5.07 us
    ppermute x1, starting transfers between devices, per_device(): partner = lax.ppermute(amplitudes, 'zl', [(0, 1), (1, 0)])  4.01 us
    pallas_call x1, Pallas kernels, contract(): pl.pallas_call(lambda *refs: ladder_kernel(groups, *refs), out_shape=jax....  3.94 us
    ppermute x1, starting transfers between devices, per_device(): theirs = lax.ppermute(mine, 'core', [(0, 1), (1, 0)])  3.7 us
  transfers between devices with their start and end apart: 9, of which 3 were waited for; matrix products, arithmetic and copies ran while one was open for 3% of the time, Pallas kernels for 2%

profile of v8, /device:TPU:1, one launch (start us, length us, event | category | flops | bytes accessed | tf_op | source)
XLA Modules:
  0.0 85.7 jit_solution(4397719479810306207)
XLA Ops:
  0.0 1.7 %irrep_order.1 = bf16[8,128,128]{2,1,0:T(8,128)(2,1)} custom-call(s32[8]{0:T(128)} %bitcast.11, bf16[8,128,128]{2,1,0:T(8,128)(2,1)} %bitcast.8), custom_call_target="tpu_custom_call" | custom-call | tf_op jit(solution)/shard_map/irrep_order/pallas_call | solution.py:22
  1.7 22.5 %all-to-all-start = ((bf16[32,32,128]{2,1,0:T(8,128)(2,1)}), bf16[32,32,128]{2,1,0:T(8,128)(2,1)S(1)}, u32[]{:S(2)}, u32[]{:S(2)}) async-start(bf16[32,32,128]{2,1,0:T(8,128)(2,1)} %bitcast.6), calls=%async_computation | async-start | bytes 524288 | tf_op jit(solution)/shard_map/all_to_all | solution.py:131
  24.2 4.0 %collective-permute-start = (bf16[128,256]{1,0:T(8,128)(2,1)S(1)}, bf16[128,256]{1,0:T(8,128)(2,1)S(1)}, u32[]{:S(2)}, u32[]{:S(2)}) collective-permute-start(bf16[128,256]{1,0:T(8,128)(2,1)S(1)} %copy-done.5), channel_id=1, source_target_pairs={{0,512},{512,0},{1,513},{513,1},{2,514},{514,2},{3,515},{515,3},{4... | collective-permute-start | bytes 196616 | tf_op jit(solution)/shard_map/ppermute | solution.py:129
  28.3 3.6 %collective-permute-done = bf16[128,256]{1,0:T(8,128)(2,1)S(1)} collective-permute-done((bf16[128,256]{1,0:T(8,128)(2,1)S(1)}, bf16[128,256]{1,0:T(8,128)(2,1)S(1)}, u32[]{:S(2)}, u32[]{:S(2)}) %collective-permute-start) | collective-permute-done | bytes 65568 | tf_op jit(solution)/shard_map/ppermute | solution.py:129
  31.9 5.1 %all_gather.3.refs_4_ = bf16[4,128,256]{2,1,0:T(8,128)(2,1)S(1)} all-gather(bf16[2,128,256]{2,1,0:T(8,128)(2,1)S(1)} %pad_maximum_fusion), channel_id=1, replica_groups=mesh['zl'=2,'x'=8,'core'=2,'zh'=4,'y'=8] {'core'}, dimensions={0}, use_global_device_ids=true | all-gather | bytes 393216 | tf_op jit(solution)/shard_map/all_gather | solution.py:133
  36.9 4.5 %collective-permute-start.1 = (bf16[4,128,256]{2,1,0:T(8,128)(2,1)S(1)}, bf16[4,128,256]{2,1,0:T(8,128)(2,1)S(1)}, u32[]{:S(2)}, u32[]{:S(2)}) collective-permute-start(bf16[4,128,256]{2,1,0:T(8,128)(2,1)S(1)} %all_gather.3.refs_4_), channel_id=1, source_target_pairs={{0,64},{32,480},{64,128},{96,32},{128,192},{160,96},{192,256},{224... | collective-permute-start | bytes 786440 | tf_op jit(solution)/shard_map/ppermute | solution.py:124
  41.4 0.0 all-to-all-done.pieces_ref
  41.5 1.6 %shard_map.55 = bf16[32,64,128]{2,1,0:T(8,128)(2,1)} custom-call(s32[2]{0:T(128)} %owner_ref.1, bf16[32,32,128]{2,1,0:T(8,128)(2,1)S(1)} %all-to-all-done.pieces_ref), custom_call_target="tpu_custom_call" | custom-call | tf_op jit(solution)/shard_map/pallas_call | solution.py:44
  43.0 11.1 %all-to-all-start.1 = ((bf16[32,64,128]{2,1,0:T(8,128)(2,1)}), bf16[32,64,128]{2,1,0:T(8,128)(2,1)S(1)}, u32[]{:S(2)}, u32[]{:S(2)}) async-start(bf16[32,64,128]{2,1,0:T(8,128)(2,1)} %shard_map.55), calls=%async_computation.1 | async-start | bytes 1048576 | tf_op jit(solution)/shard_map/all_to_all | solution.py:138
  54.1 4.8 %collective-permute-start.2 = (bf16[4,128,256]{2,1,0:T(8,128)(2,1)S(1)}, bf16[4,128,256]{2,1,0:T(8,128)(2,1)S(1)}, u32[]{:S(2)}, u32[]{:S(2)}) collective-permute-start(bf16[4,128,256]{2,1,0:T(8,128)(2,1)S(1)} %all_gather.3.refs_4_), channel_id=1, source_target_pairs={{0,192},{32,352},{64,256},{96,416},{128,320},{160,480},{192,384},{... | collective-permute-start | bytes 786440 | tf_op jit(solution)/shard_map/ppermute | solution.py:124
  58.9 0.0 collective-permute-done.1
  58.9 2.2 %collective-permute-start.4 = (bf16[4,128,256]{2,1,0:T(8,128)(2,1)S(1)}, bf16[4,128,256]{2,1,0:T(8,128)(2,1)S(1)}, u32[]{:S(2)}, u32[]{:S(2)}) collective-permute-start(bf16[4,128,256]{2,1,0:T(8,128)(2,1)S(1)} %collective-permute-done.1), channel_id=1, source_target_pairs={{0,64},{32,480},{64,128},{96,32},{128,192},{160,96},{192,256},{224... | collective-permute-start | bytes 786440 | tf_op jit(solution)/shard_map/ppermute | solution.py:124
  61.1 5.9 %collective-permute-done.2 = bf16[4,128,256]{2,1,0:T(8,128)(2,1)S(1)} collective-permute-done((bf16[4,128,256]{2,1,0:T(8,128)(2,1)S(1)}, bf16[4,128,256]{2,1,0:T(8,128)(2,1)S(1)}, u32[]{:S(2)}, u32[]{:S(2)}) %collective-permute-start.2) | collective-permute-done | bytes 262176 | tf_op jit(solution)/shard_map/ppermute | solution.py:124
  67.1 3.7 %collective-permute-start.3 = (bf16[8,128,256]{2,1,0:T(8,128)(2,1)S(1)}, bf16[8,128,256]{2,1,0:T(8,128)(2,1)S(1)}, u32[]{:S(2)}, u32[]{:S(2)}) collective-permute-start(bf16[8,128,256]{2,1,0:T(8,128)(2,1)S(1)} %constant_dynamic-update-slice_fusion.refs_5_), channel_id=1, source_target_pairs={{0,32},{32,0},{1,33},{33,1},{2,34},{34,2},{3,35},{35,3},{4,36},{36... | collective-permute-start | bytes 1572872 | tf_op jit(solution)/shard_map/ppermute | solution.py:143
  70.8 0.6 iota_add_fusion.refs_3_
  71.4 0.5 iota_add_fusion.1.refs_1_
  71.9 4.2 %collective-permute-start.5 = (bf16[4,128,256]{2,1,0:T(8,128)(2,1)S(1)}, bf16[4,128,256]{2,1,0:T(8,128)(2,1)S(1)}, u32[]{:S(2)}, u32[]{:S(2)}) collective-permute-start(bf16[4,128,256]{2,1,0:T(8,128)(2,1)S(1)} %collective-permute-done.2), channel_id=1, source_target_pairs={{0,64},{32,480},{64,128},{96,32},{128,192},{160,96},{192,256},{224... | collective-permute-start | bytes 786440 | tf_op jit(solution)/shard_map/ppermute | solution.py:124
  76.1 0.0 collective-permute-done.4.refs_7_
  76.2 2.9 %collective-permute-start.6 = (bf16[4,128,256]{2,1,0:T(8,128)(2,1)S(1)}, bf16[4,128,256]{2,1,0:T(8,128)(2,1)S(1)}, u32[]{:S(2)}, u32[]{:S(2)}) collective-permute-start(bf16[4,128,256]{2,1,0:T(8,128)(2,1)S(1)} %collective-permute-done.4.refs_7_), channel_id=1, source_target_pairs={{0,32},{32,0},{1,33},{33,1},{2,34},{34,2},{3,35},{35,3},{4,36},{36... | collective-permute-start | bytes 786440 | tf_op jit(solution)/shard_map/ppermute | solution.py:145
  79.0 0.0 copy-start.6
  79.0 0.6 pad_add_fusion.refs_2_
  79.6 0.1 copy-done.6
  79.7 0.5 broadcast_multiply_fusion.refs_0_
  80.2 0.6 collective-permute-done.5.refs_8_
  80.8 0.0 collective-permute-done.6.refs_9_
  80.8 0.0 collective-permute-done.3.refs_6_
  80.9 0.0 all-to-all-done.1.refs_10_
  80.9 0.0 copy-done
  80.9 0.0 copy-done.3
  80.9 0.7 copy-done.4
  81.5 0.2 copy-done.2
  81.7 3.9 %ladder.1 = bf16[32,128,128]{2,1,0:T(8,128)(2,1)} custom-call(s32[32]{0:T(128)} %broadcast_multiply_fusion.refs_0_, s32[24]{0:T(128)} %iota_add_fusion.1.refs_1_, s32[2]{0:T(128)} %pad_add_fusion.refs_2_, s32[16]{0:T(128)} %iota_add_fusion.refs_3_, bf16[4,128,256]{2,1,0:T(8,128)(2,1)} %copy-done.1, bf16[8,128,256]{2,1,0:T(8,128)(2,1)} %copy-done, ...), custom_call_target="tpu_custom_call" | custom-call | tf_op jit(solution)/shard_map/ladder/pallas_call | solution.py:103
  (11 shorter events, 0.1 us)
Async XLA Ops:
  1.7 22.5 %copy-start.5 = (bf16[128,256]{1,0:T(8,128)(2,1)S(1)}, bf16[128,256]{1,0:T(8,128)(2,1)}, u32[]{:S(2)}) copy-start(bf16[128,256]{1,0:T(8,128)(2,1)} %param.5) | copy-start | bytes 196612
  1.7 39.8 %all-to-all-start = ((bf16[32,32,128]{2,1,0:T(8,128)(2,1)}), bf16[32,32,128]{2,1,0:T(8,128)(2,1)S(1)}, u32[]{:S(2)}, u32[]{:S(2)}) async-start(bf16[32,32,128]{2,1,0:T(8,128)(2,1)} %bitcast.6), calls=%async_computation | async-start | bytes 524288 | tf_op jit(solution)/shard_map/all_to_all | solution.py:131
  24.2 7.6 %collective-permute-start = (bf16[128,256]{1,0:T(8,128)(2,1)S(1)}, bf16[128,256]{1,0:T(8,128)(2,1)S(1)}, u32[]{:S(2)}, u32[]{:S(2)}) collective-permute-start(bf16[128,256]{1,0:T(8,128)(2,1)S(1)} %copy-done.5), channel_id=1, source_target_pairs={{0,512},{512,0},{1,513},{513,1},{2,514},{514,2},{3,515},{515,3},{4... | collective-permute-start | bytes 196616 | tf_op jit(solution)/shard_map/ppermute | solution.py:129
  36.9 17.2 %copy-start.1 = (bf16[4,128,256]{2,1,0:T(8,128)(2,1)}, bf16[4,128,256]{2,1,0:T(8,128)(2,1)S(1)}, u32[]{:S(2)}) copy-start(bf16[4,128,256]{2,1,0:T(8,128)(2,1)S(1)} %all_gather.3.refs_4_) | copy-start | bytes 786436
  36.9 22.0 %collective-permute-start.1 = (bf16[4,128,256]{2,1,0:T(8,128)(2,1)S(1)}, bf16[4,128,256]{2,1,0:T(8,128)(2,1)S(1)}, u32[]{:S(2)}, u32[]{:S(2)}) collective-permute-start(bf16[4,128,256]{2,1,0:T(8,128)(2,1)S(1)} %all_gather.3.refs_4_), channel_id=1, source_target_pairs={{0,64},{32,480},{64,128},{96,32},{128,192},{160,96},{192,256},{224... | collective-permute-start | bytes 786440 | tf_op jit(solution)/shard_map/ppermute | solution.py:124
  43.0 37.8 %all-to-all-start.1 = ((bf16[32,64,128]{2,1,0:T(8,128)(2,1)}), bf16[32,64,128]{2,1,0:T(8,128)(2,1)S(1)}, u32[]{:S(2)}, u32[]{:S(2)}) async-start(bf16[32,64,128]{2,1,0:T(8,128)(2,1)} %shard_map.55), calls=%async_computation.1 | async-start | bytes 1048576 | tf_op jit(solution)/shard_map/all_to_all | solution.py:138
  54.1 13.0 %collective-permute-start.2 = (bf16[4,128,256]{2,1,0:T(8,128)(2,1)S(1)}, bf16[4,128,256]{2,1,0:T(8,128)(2,1)S(1)}, u32[]{:S(2)}, u32[]{:S(2)}) collective-permute-start(bf16[4,128,256]{2,1,0:T(8,128)(2,1)S(1)} %all_gather.3.refs_4_), channel_id=1, source_target_pairs={{0,192},{32,352},{64,256},{96,416},{128,320},{160,480},{192,384},{... | collective-permute-start | bytes 786440 | tf_op jit(solution)/shard_map/ppermute | solution.py:124
  58.9 17.2 %collective-permute-start.4 = (bf16[4,128,256]{2,1,0:T(8,128)(2,1)S(1)}, bf16[4,128,256]{2,1,0:T(8,128)(2,1)S(1)}, u32[]{:S(2)}, u32[]{:S(2)}) collective-permute-start(bf16[4,128,256]{2,1,0:T(8,128)(2,1)S(1)} %collective-permute-done.1), channel_id=1, source_target_pairs={{0,64},{32,480},{64,128},{96,32},{128,192},{160,96},{192,256},{224... | collective-permute-start | bytes 786440 | tf_op jit(solution)/shard_map/ppermute | solution.py:124
  67.1 13.8 %copy-start = (bf16[8,128,256]{2,1,0:T(8,128)(2,1)}, bf16[8,128,256]{2,1,0:T(8,128)(2,1)S(1)}, u32[]{:S(2)}) copy-start(bf16[8,128,256]{2,1,0:T(8,128)(2,1)S(1)} %constant_dynamic-update-slice_fusion.refs_5_) | copy-start | bytes 1572868
  67.1 13.7 %collective-permute-start.3 = (bf16[8,128,256]{2,1,0:T(8,128)(2,1)S(1)}, bf16[8,128,256]{2,1,0:T(8,128)(2,1)S(1)}, u32[]{:S(2)}, u32[]{:S(2)}) collective-permute-start(bf16[8,128,256]{2,1,0:T(8,128)(2,1)S(1)} %constant_dynamic-update-slice_fusion.refs_5_), channel_id=1, source_target_pairs={{0,32},{32,0},{1,33},{33,1},{2,34},{34,2},{3,35},{35,3},{4,36},{36... | collective-permute-start | bytes 1572872 | tf_op jit(solution)/shard_map/ppermute | solution.py:143
  71.9 8.9 %collective-permute-start.5 = (bf16[4,128,256]{2,1,0:T(8,128)(2,1)S(1)}, bf16[4,128,256]{2,1,0:T(8,128)(2,1)S(1)}, u32[]{:S(2)}, u32[]{:S(2)}) collective-permute-start(bf16[4,128,256]{2,1,0:T(8,128)(2,1)S(1)} %collective-permute-done.2), channel_id=1, source_target_pairs={{0,64},{32,480},{64,128},{96,32},{128,192},{160,96},{192,256},{224... | collective-permute-start | bytes 786440 | tf_op jit(solution)/shard_map/ppermute | solution.py:124
  76.2 4.7 %copy-start.3 = (bf16[4,128,256]{2,1,0:T(8,128)(2,1)}, bf16[4,128,256]{2,1,0:T(8,128)(2,1)S(1)}, u32[]{:S(2)}) copy-start(bf16[4,128,256]{2,1,0:T(8,128)(2,1)S(1)} %collective-permute-done.4.refs_7_) | copy-start | bytes 786436
  76.2 4.7 %collective-permute-start.6 = (bf16[4,128,256]{2,1,0:T(8,128)(2,1)S(1)}, bf16[4,128,256]{2,1,0:T(8,128)(2,1)S(1)}, u32[]{:S(2)}, u32[]{:S(2)}) collective-permute-start(bf16[4,128,256]{2,1,0:T(8,128)(2,1)S(1)} %collective-permute-done.4.refs_7_), channel_id=1, source_target_pairs={{0,32},{32,0},{1,33},{33,1},{2,34},{34,2},{3,35},{35,3},{4,36},{36... | collective-permute-start | bytes 786440 | tf_op jit(solution)/shard_map/ppermute | solution.py:145
  79.0 0.7 copy-start.6
  80.8 0.7 copy-start.4
  80.9 0.9 %copy-start.2 = (bf16[8,128,256]{2,1,0:T(8,128)(2,1)}, bf16[8,128,256]{2,1,0:T(8,128)(2,1)S(1)}, u32[]{:S(2)}) copy-start(bf16[8,128,256]{2,1,0:T(8,128)(2,1)S(1)} %collective-permute-done.3.refs_6_) | copy-start | bytes 1572868

commit v9 on v8

--- a/solution.py
+++ b/solution.py
@@ -52,8 +52,8 @@
     )(owners, pltpu.with_memory_space_constraint(pieces, pltpu.VMEM))
 
 
-HERE, MINE, THEIRS = (0,), (1, 3), (-1, -3)
-MIDDLE, OPPOSITE, OTHER_MIDDLE = (2,), (4,), (-2,)
+HERE, MINE, THEIRS = (0,), (1, 2), (-1, -2)
+THIRD, OPPOSITE, OTHER_THIRD = (3,), (4,), (-3,)
 
 
 def ladder_kernel(groups, piece_ref, second_ref, here_ref, side_ref, *refs):
@@ -132,20 +132,20 @@
     pair = jnp.stack([amplitudes, partner])
     chip = lax.all_gather(pair, "core", axis=0, tiled=True)
     beside = away(chip, 1)
-    three = away(chip, 3)
+    two = away(chip, 2)
     here = jnp.stack([lax.axis_index("x"), lax.axis_index("zl")])
     copies = pick_and_copy(pieces, panel_owner)
     weights = lax.all_to_all(copies, VIR, 0, 0, tiled=True)
     side = jnp.arange(16, dtype=jnp.int32) + lax.axis_index("core")
-    middle = away(beside, 1)
-    opposite = away(three, 1)
-    mine = jnp.concatenate([beside, three])
+    opposite = away(two, 2)
+    third = away(two, 1)
+    mine = jnp.concatenate([beside, two])
     theirs = lax.ppermute(mine, "core", [(0, 1), (1, 0)])
     second = jnp.arange(24, dtype=jnp.int32) + lax.axis_index("x")
-    other_middle = lax.ppermute(middle, "core", [(0, 1), (1, 0)])
+    other_third = lax.ppermute(third, "core", [(0, 1), (1, 0)])
     first_piece = pair_irrep * (N_VIR // IRREPS)
-    groups = (HERE, MINE, THEIRS, MIDDLE, OPPOSITE, OTHER_MIDDLE)
-    arrays = (chip, mine, theirs, middle, opposite, other_middle)
+    groups = (HERE, MINE, THEIRS, THIRD, OPPOSITE, OTHER_THIRD)
+    arrays = (chip, mine, theirs, third, opposite, other_third)
     return contract(groups, arrays, first_piece, second, here, side, weights)
 
 

time: 86.3 us -> 82.9 us (0.961)
  the two profiles are of different devices: /device:TPU:1 before, /device:TPU:16 now
where the time goes in v9:
time: 82.9 us; the launch traced here: 82.3 us
  starting transfers between devices  57.4 us (69%)
  waiting for transfers between devices  12.3 us (15%)
  Pallas kernels  7.2 us (9%)
  other arithmetic  2.19 us (3%)
  blocking collectives  1.99 us (2%)
  local copies, waits for them, and re-layouts  0.98 us (1%)
    all_to_all x1, starting transfers between devices, per_device(): lax.all_to_all(ordered.reshape(N_VIR, -1, cols), VIR, 0, 0, tiled=True)  22.1 us
    ppermute x4, starting transfers between devices, away(): return lax.ppermute(array, ('x', 'core'), pairs)  14.8 us
    all_to_all x1, starting transfers between devices, per_device(): weights = lax.all_to_all(copies, VIR, 0, 0, tiled=True)  12.2 us
    ppermute x4, waiting for transfers between devices, away(): return lax.ppermute(array, ('x', 'core'), pairs)  7.38 us
    ppermute x1, waiting for transfers between devices, per_device(): partner = lax.ppermute(amplitudes, 'zl', [(0, 1), (1, 0)])  4.92 us
    ppermute x1, starting transfers between devices, per_device(): partner = lax.ppermute(amplitudes, 'zl', [(0, 1), (1, 0)])  4.29 us
    pallas_call x1, Pallas kernels, contract(): pl.pallas_call(lambda *refs: ladder_kernel(groups, *refs), out_shape=jax....  3.94 us
    ppermute x1, starting transfers between devices, per_device(): other_third = lax.ppermute(third, 'core', [(0, 1), (1, 0)])  2.01 us
  transfers between devices with their start and end apart: 9, of which 2 were waited for; matrix products, arithmetic and copies ran while one was open for 3% of the time, Pallas kernels for 2%

profile of v9, /device:TPU:16, one launch (start us, length us, event | category | flops | bytes accessed | tf_op | source)
XLA Modules:
  0.0 82.3 jit_solution(686550360419300500)
XLA Ops:
  0.0 1.7 %irrep_order.1 = bf16[8,128,128]{2,1,0:T(8,128)(2,1)} custom-call(s32[8]{0:T(128)} %bitcast.11, bf16[8,128,128]{2,1,0:T(8,128)(2,1)} %bitcast.8), custom_call_target="tpu_custom_call" | custom-call | tf_op jit(solution)/shard_map/irrep_order/pallas_call | solution.py:22
  1.7 22.1 %all-to-all-start = ((bf16[32,32,128]{2,1,0:T(8,128)(2,1)}), bf16[32,32,128]{2,1,0:T(8,128)(2,1)S(1)}, u32[]{:S(2)}, u32[]{:S(2)}) async-start(bf16[32,32,128]{2,1,0:T(8,128)(2,1)} %bitcast.6), calls=%async_computation | async-start | bytes 524288 | tf_op jit(solution)/shard_map/all_to_all | solution.py:131
  23.8 4.3 %collective-permute-start = (bf16[128,256]{1,0:T(8,128)(2,1)S(1)}, bf16[128,256]{1,0:T(8,128)(2,1)S(1)}, u32[]{:S(2)}, u32[]{:S(2)}) collective-permute-start(bf16[128,256]{1,0:T(8,128)(2,1)S(1)} %copy-done.5), channel_id=1, source_target_pairs={{0,512},{512,0},{1,513},{513,1},{2,514},{514,2},{3,515},{515,3},{4... | collective-permute-start | bytes 196616 | tf_op jit(solution)/shard_map/ppermute | solution.py:129
  28.1 4.9 %collective-permute-done = bf16[128,256]{1,0:T(8,128)(2,1)S(1)} collective-permute-done((bf16[128,256]{1,0:T(8,128)(2,1)S(1)}, bf16[128,256]{1,0:T(8,128)(2,1)S(1)}, u32[]{:S(2)}, u32[]{:S(2)}) %collective-permute-start) | collective-permute-done | bytes 65568 | tf_op jit(solution)/shard_map/ppermute | solution.py:129
  33.0 2.0 %all_gather.3.refs_4_ = bf16[4,128,256]{2,1,0:T(8,128)(2,1)S(1)} all-gather(bf16[2,128,256]{2,1,0:T(8,128)(2,1)S(1)} %pad_maximum_fusion), channel_id=1, replica_groups=mesh['zl'=2,'x'=8,'core'=2,'zh'=4,'y'=8] {'core'}, dimensions={0}, use_global_device_ids=true | all-gather | bytes 393216 | tf_op jit(solution)/shard_map/all_gather | solution.py:133
  35.0 4.3 %collective-permute-start.2 = (bf16[4,128,256]{2,1,0:T(8,128)(2,1)S(1)}, bf16[4,128,256]{2,1,0:T(8,128)(2,1)S(1)}, u32[]{:S(2)}, u32[]{:S(2)}) collective-permute-start(bf16[4,128,256]{2,1,0:T(8,128)(2,1)S(1)} %all_gather.3.refs_4_), channel_id=1, source_target_pairs={{0,128},{32,416},{64,192},{96,480},{128,256},{160,32},{192,320},{2... | collective-permute-start | bytes 786440 | tf_op jit(solution)/shard_map/ppermute | solution.py:124
  39.4 3.4 %collective-permute-start.1 = (bf16[4,128,256]{2,1,0:T(8,128)(2,1)S(1)}, bf16[4,128,256]{2,1,0:T(8,128)(2,1)S(1)}, u32[]{:S(2)}, u32[]{:S(2)}) collective-permute-start(bf16[4,128,256]{2,1,0:T(8,128)(2,1)S(1)} %all_gather.3.refs_4_), channel_id=1, source_target_pairs={{0,64},{32,480},{64,128},{96,32},{128,192},{160,96},{192,256},{224... | collective-permute-start | bytes 786440 | tf_op jit(solution)/shard_map/ppermute | solution.py:124
  42.8 0.0 all-to-all-done.pieces_ref
  42.8 1.6 %shard_map.55 = bf16[32,64,128]{2,1,0:T(8,128)(2,1)} custom-call(s32[2]{0:T(128)} %owner_ref.1, bf16[32,32,128]{2,1,0:T(8,128)(2,1)S(1)} %all-to-all-done.pieces_ref), custom_call_target="tpu_custom_call" | custom-call | tf_op jit(solution)/shard_map/pallas_call | solution.py:44
  44.4 12.2 %all-to-all-start.1 = ((bf16[32,64,128]{2,1,0:T(8,128)(2,1)}), bf16[32,64,128]{2,1,0:T(8,128)(2,1)S(1)}, u32[]{:S(2)}, u32[]{:S(2)}) async-start(bf16[32,64,128]{2,1,0:T(8,128)(2,1)} %shard_map.55), calls=%async_computation.1 | async-start | bytes 1048576 | tf_op jit(solution)/shard_map/all_to_all | solution.py:138
  56.6 0.0 collective-permute-done.2
  56.6 4.6 %collective-permute-start.4 = (bf16[4,128,256]{2,1,0:T(8,128)(2,1)S(1)}, bf16[4,128,256]{2,1,0:T(8,128)(2,1)S(1)}, u32[]{:S(2)}, u32[]{:S(2)}) collective-permute-start(bf16[4,128,256]{2,1,0:T(8,128)(2,1)S(1)} %collective-permute-done.2), channel_id=1, source_target_pairs={{0,64},{32,480},{64,128},{96,32},{128,192},{160,96},{192,256},{224... | collective-permute-start | bytes 786440 | tf_op jit(solution)/shard_map/ppermute | solution.py:124
  61.2 0.0 collective-permute-done.1
  61.3 1.9 %collective-permute-start.3 = (bf16[8,128,256]{2,1,0:T(8,128)(2,1)S(1)}, bf16[8,128,256]{2,1,0:T(8,128)(2,1)S(1)}, u32[]{:S(2)}, u32[]{:S(2)}) collective-permute-start(bf16[8,128,256]{2,1,0:T(8,128)(2,1)S(1)} %constant_dynamic-update-slice_fusion.refs_5_), channel_id=1, source_target_pairs={{0,32},{32,0},{1,33},{33,1},{2,34},{34,2},{3,35},{35,3},{4,36},{36... | collective-permute-start | bytes 1572872 | tf_op jit(solution)/shard_map/ppermute | solution.py:143
  63.2 0.6 iota_add_fusion.refs_3_
  63.8 0.5 iota_add_fusion.1.refs_1_
  64.3 2.5 %collective-permute-start.5 = (bf16[4,128,256]{2,1,0:T(8,128)(2,1)S(1)}, bf16[4,128,256]{2,1,0:T(8,128)(2,1)S(1)}, u32[]{:S(2)}, u32[]{:S(2)}) collective-permute-start(bf16[4,128,256]{2,1,0:T(8,128)(2,1)S(1)} %collective-permute-done.2), channel_id=1, source_target_pairs={{0,128},{32,416},{64,192},{96,480},{128,256},{160,32},{192,320},{2... | collective-permute-start | bytes 786440 | tf_op jit(solution)/shard_map/ppermute | solution.py:124
  66.9 0.0 collective-permute-done.4.refs_7_
  66.9 0.0 copy-start.3
  66.9 2.0 %collective-permute-start.6 = (bf16[4,128,256]{2,1,0:T(8,128)(2,1)S(1)}, bf16[4,128,256]{2,1,0:T(8,128)(2,1)S(1)}, u32[]{:S(2)}, u32[]{:S(2)}) collective-permute-start(bf16[4,128,256]{2,1,0:T(8,128)(2,1)S(1)} %collective-permute-done.4.refs_7_), channel_id=1, source_target_pairs={{0,32},{32,0},{1,33},{33,1},{2,34},{34,2},{3,35},{35,3},{4,36},{36... | collective-permute-start | bytes 786440 | tf_op jit(solution)/shard_map/ppermute | solution.py:145
  68.9 0.0 copy-start.6
  68.9 0.6 pad_add_fusion.refs_2_
  69.5 0.1 copy-done.6
  69.6 0.5 broadcast_multiply_fusion.refs_0_
  70.1 7.4 %collective-permute-done.5.refs_8_ = bf16[4,128,256]{2,1,0:T(8,128)(2,1)S(1)} collective-permute-done((bf16[4,128,256]{2,1,0:T(8,128)(2,1)S(1)}, bf16[4,128,256]{2,1,0:T(8,128)(2,1)S(1)}, u32[]{:S(2)}, u32[]{:S(2)}) %collective-permute-start.5) | collective-permute-done | bytes 262176 | tf_op jit(solution)/shard_map/ppermute | solution.py:124
  77.5 0.0 collective-permute-done.6.refs_9_
  77.5 0.0 collective-permute-done.3.refs_6_
  77.5 0.0 copy-start.2
  77.5 0.0 all-to-all-done.1.refs_10_
  77.5 0.7 copy-done.4
  78.2 0.2 copy-done.2
  78.3 3.9 %ladder.1 = bf16[32,128,128]{2,1,0:T(8,128)(2,1)} custom-call(s32[32]{0:T(128)} %broadcast_multiply_fusion.refs_0_, s32[24]{0:T(128)} %iota_add_fusion.1.refs_1_, s32[2]{0:T(128)} %pad_add_fusion.refs_2_, s32[16]{0:T(128)} %iota_add_fusion.refs_3_, bf16[4,128,256]{2,1,0:T(8,128)(2,1)} %copy-done.1, bf16[8,128,256]{2,1,0:T(8,128)(2,1)} %copy-done, ...), custom_call_target="tpu_custom_call" | custom-call | tf_op jit(solution)/shard_map/ladder/pallas_call | solution.py:103
  (11 shorter events, 0.1 us)
Async XLA Ops:
  1.7 22.1 %copy-start.5 = (bf16[128,256]{1,0:T(8,128)(2,1)S(1)}, bf16[128,256]{1,0:T(8,128)(2,1)}, u32[]{:S(2)}) copy-start(bf16[128,256]{1,0:T(8,128)(2,1)} %param.5) | copy-start | bytes 196612
  1.7 41.1 %all-to-all-start = ((bf16[32,32,128]{2,1,0:T(8,128)(2,1)}), bf16[32,32,128]{2,1,0:T(8,128)(2,1)S(1)}, u32[]{:S(2)}, u32[]{:S(2)}) async-start(bf16[32,32,128]{2,1,0:T(8,128)(2,1)} %bitcast.6), calls=%async_computation | async-start | bytes 524288 | tf_op jit(solution)/shard_map/all_to_all | solution.py:131
  23.8 9.2 %collective-permute-start = (bf16[128,256]{1,0:T(8,128)(2,1)S(1)}, bf16[128,256]{1,0:T(8,128)(2,1)S(1)}, u32[]{:S(2)}, u32[]{:S(2)}) collective-permute-start(bf16[128,256]{1,0:T(8,128)(2,1)S(1)} %copy-done.5), channel_id=1, source_target_pairs={{0,512},{512,0},{1,513},{513,1},{2,514},{514,2},{3,515},{515,3},{4... | collective-permute-start | bytes 196616 | tf_op jit(solution)/shard_map/ppermute | solution.py:129
  35.0 9.3 %copy-start.1 = (bf16[4,128,256]{2,1,0:T(8,128)(2,1)}, bf16[4,128,256]{2,1,0:T(8,128)(2,1)S(1)}, u32[]{:S(2)}) copy-start(bf16[4,128,256]{2,1,0:T(8,128)(2,1)S(1)} %all_gather.3.refs_4_) | copy-start | bytes 786436
  35.0 21.6 %collective-permute-start.2 = (bf16[4,128,256]{2,1,0:T(8,128)(2,1)S(1)}, bf16[4,128,256]{2,1,0:T(8,128)(2,1)S(1)}, u32[]{:S(2)}, u32[]{:S(2)}) collective-permute-start(bf16[4,128,256]{2,1,0:T(8,128)(2,1)S(1)} %all_gather.3.refs_4_), channel_id=1, source_target_pairs={{0,128},{32,416},{64,192},{96,480},{128,256},{160,32},{192,320},{2... | collective-permute-start | bytes 786440 | tf_op jit(solution)/shard_map/ppermute | solution.py:124
  39.4 21.9 %collective-permute-start.1 = (bf16[4,128,256]{2,1,0:T(8,128)(2,1)S(1)}, bf16[4,128,256]{2,1,0:T(8,128)(2,1)S(1)}, u32[]{:S(2)}, u32[]{:S(2)}) collective-permute-start(bf16[4,128,256]{2,1,0:T(8,128)(2,1)S(1)} %all_gather.3.refs_4_), channel_id=1, source_target_pairs={{0,64},{32,480},{64,128},{96,32},{128,192},{160,96},{192,256},{224... | collective-permute-start | bytes 786440 | tf_op jit(solution)/shard_map/ppermute | solution.py:124
  44.4 33.1 %all-to-all-start.1 = ((bf16[32,64,128]{2,1,0:T(8,128)(2,1)}), bf16[32,64,128]{2,1,0:T(8,128)(2,1)S(1)}, u32[]{:S(2)}, u32[]{:S(2)}) async-start(bf16[32,64,128]{2,1,0:T(8,128)(2,1)} %shard_map.55), calls=%async_computation.1 | async-start | bytes 1048576 | tf_op jit(solution)/shard_map/all_to_all | solution.py:138
  56.6 10.2 %collective-permute-start.4 = (bf16[4,128,256]{2,1,0:T(8,128)(2,1)S(1)}, bf16[4,128,256]{2,1,0:T(8,128)(2,1)S(1)}, u32[]{:S(2)}, u32[]{:S(2)}) collective-permute-start(bf16[4,128,256]{2,1,0:T(8,128)(2,1)S(1)} %collective-permute-done.2), channel_id=1, source_target_pairs={{0,64},{32,480},{64,128},{96,32},{128,192},{160,96},{192,256},{224... | collective-permute-start | bytes 786440 | tf_op jit(solution)/shard_map/ppermute | solution.py:124
  61.3 16.2 %copy-start = (bf16[8,128,256]{2,1,0:T(8,128)(2,1)}, bf16[8,128,256]{2,1,0:T(8,128)(2,1)S(1)}, u32[]{:S(2)}) copy-start(bf16[8,128,256]{2,1,0:T(8,128)(2,1)S(1)} %constant_dynamic-update-slice_fusion.refs_5_) | copy-start | bytes 1572868
  61.3 16.1 %collective-permute-start.3 = (bf16[8,128,256]{2,1,0:T(8,128)(2,1)S(1)}, bf16[8,128,256]{2,1,0:T(8,128)(2,1)S(1)}, u32[]{:S(2)}, u32[]{:S(2)}) collective-permute-start(bf16[8,128,256]{2,1,0:T(8,128)(2,1)S(1)} %constant_dynamic-update-slice_fusion.refs_5_), channel_id=1, source_target_pairs={{0,32},{32,0},{1,33},{33,1},{2,34},{34,2},{3,35},{35,3},{4,36},{36... | collective-permute-start | bytes 1572872 | tf_op jit(solution)/shard_map/ppermute | solution.py:143
  64.3 13.1 %collective-permute-start.5 = (bf16[4,128,256]{2,1,0:T(8,128)(2,1)S(1)}, bf16[4,128,256]{2,1,0:T(8,128)(2,1)S(1)}, u32[]{:S(2)}, u32[]{:S(2)}) collective-permute-start(bf16[4,128,256]{2,1,0:T(8,128)(2,1)S(1)} %collective-permute-done.2), channel_id=1, source_target_pairs={{0,128},{32,416},{64,192},{96,480},{128,256},{160,32},{192,320},{2... | collective-permute-start | bytes 786440 | tf_op jit(solution)/shard_map/ppermute | solution.py:124
  66.9 10.6 %copy-start.3 = (bf16[4,128,256]{2,1,0:T(8,128)(2,1)}, bf16[4,128,256]{2,1,0:T(8,128)(2,1)S(1)}, u32[]{:S(2)}) copy-start(bf16[4,128,256]{2,1,0:T(8,128)(2,1)S(1)} %collective-permute-done.4.refs_7_) | copy-start | bytes 786436
  66.9 10.6 %collective-permute-start.6 = (bf16[4,128,256]{2,1,0:T(8,128)(2,1)S(1)}, bf16[4,128,256]{2,1,0:T(8,128)(2,1)S(1)}, u32[]{:S(2)}, u32[]{:S(2)}) collective-permute-start(bf16[4,128,256]{2,1,0:T(8,128)(2,1)S(1)} %collective-permute-done.4.refs_7_), channel_id=1, source_target_pairs={{0,32},{32,0},{1,33},{33,1},{2,34},{34,2},{3,35},{35,3},{4,36},{36... | collective-permute-start | bytes 786440 | tf_op jit(solution)/shard_map/ppermute | solution.py:145
  68.9 0.7 copy-start.6
  77.4 0.7 copy-start.4
  77.5 0.9 %copy-start.2 = (bf16[8,128,256]{2,1,0:T(8,128)(2,1)}, bf16[8,128,256]{2,1,0:T(8,128)(2,1)S(1)}, u32[]{:S(2)}) copy-start(bf16[8,128,256]{2,1,0:T(8,128)(2,1)S(1)} %collective-permute-done.3.refs_6_) | copy-start | bytes 1572868
